TPU v7x, 128 devices: a whole 4x4x4 slice. The times are simulated.
128 devices in a mesh: site: 32 (over z, y, core), branch: 4 (over x).
Axes of the slice: x: 4, y: 4, z: 4, core: 2. Of those that a mesh axis runs over, the one named last changes fastest.
Arguments:
- states: int32 [256, 8192], P(None, 'site'), may hold values from 0 to 63, as said below
- gap_mask: int32 [256, 8192], P(None, 'site'), may hold values 0 or 1
- weights: int32 [8192], P('site'), may hold values from 1 to 9
- leaf_order: int32 [256], replicated, may hold values from 0 to 255, each once
- exchanges: float32 [64, 64], replicated, may hold values from 0.3 to 3
- codon_freq: float32 [64], replicated, may hold values from 0.3 to 3
- omega_ratio: float32 [8], replicated, may hold values from 0.1 to 2
- lengths: float32 [508], P('branch'), may hold values from 0.05 to 1.5
- classes: int32 [508], P('branch'), may hold values from 0 to 7
Outputs:
- grad_exch: float32 [64, 64], replicated
- grad_omega: float32 [8], replicated
- grad_length: float32 [508], P('branch')
- loglik: float32 [], replicated
Inputs may be any that keep to these rules, and one draw needn't show every extreme that they name: `states`: every state is a sense codon: never 10, 11 or 14.
All inputs are finite; a program needn't handle non-finite values. No bound on the sum of `gap_mask` on one device may be relied on, other than what follows from the above.
Results may differ from a plain program's by a relative error of at most 0.0003.
Values sent between devices are 32-bit elements; how exact they have to be, the bound alone decides.
A program may use at most 192 MiB of HBM per device.

v0:
```python
import jax
import jax.numpy as jnp
import numpy as np
from jax import lax
from jax.sharding import PartitionSpec as P
from jax.experimental import pallas as pl
from jax.experimental.pallas import tpu as pltpu
import functools

MESH_ID = pl.DeviceIdType.MESH

LEVELS = 6
LEAF_DEV = 64
EDGES = 127
SLOTS = 128
CLASSES = 8


CODE_TABLE = "FFLLSSSSYYXXCCXWLLLLPPPPHHQQRRRRIIIMTTTTNNKKSSRRVVVVAAAADDEEGGGG"


def codon_tables():
    amino_acid = np.array(list(CODE_TABLE))
    codon_index = np.arange(64)
    digits = np.stack([codon_index // 16, codon_index // 4 % 4, codon_index % 4], 1)
    differ = (digits[:, None, :] != digits[None, :, :]).sum(-1)
    is_sense = amino_acid != "X"
    single = (differ == 1) & is_sense[:, None] & is_sense[None, :]
    nonsyn = single & (amino_acid[:, None] != amino_acid[None, :])
    return (is_sense.astype(np.float32), single.astype(np.float32), nonsyn.astype(np.float32))


def build_rates(exchanges, codon_freq, omega_ratio):
    is_sense, single, nonsyn = codon_tables()
    stationary = codon_freq * is_sense / jnp.sum(codon_freq * is_sense)
    symmetric = 0.5 * (exchanges + exchanges.T)
    factor = 1.0 + nonsyn[None, :, :] * (omega_ratio[:, None, None] - 1.0)
    off_diag = symmetric[None, :, :] * stationary[None, None, :] * factor * single[None, :, :]
    row_total = jnp.sum(off_diag, axis=2)
    mean_rate = jnp.sum(stationary[None, :] * row_total, axis=1)
    identity = jnp.eye(64, dtype=exchanges.dtype)
    rate_matrix = (off_diag - row_total[:, :, None] * identity[None]) / mean_rate[:, None, None]
    return (rate_matrix, stationary)


def product(left, right):
    return jnp.einsum("bij,bjk->bik", left, right, precision=lax.Precision.HIGH)


def expm_taylor(scaled):
    reduced = scaled / 16.0
    identity = jnp.eye(64, dtype=scaled.dtype)
    series = jnp.broadcast_to(identity, scaled.shape)
    for degree in range(8, 0, -1):
        series = identity + product(reduced, series) / degree
    for square_step in range(4):
        series = product(series, series)
    return series


def forward(probs, vectors):
    return jnp.einsum("bij,bjs->bis", probs, vectors, precision=lax.Precision.HIGH)


def carried(probs, vectors):
    return jnp.einsum("bji,bjs->bis", probs, vectors, precision=lax.Precision.HIGH)


def leaf_partials(leaf_states, gap_rows):
    codon_axis = jnp.arange(64, dtype=jnp.int32)
    indicator = (leaf_states[:, None, :] == codon_axis[None, :, None]).astype(jnp.float32)
    return jnp.where(gap_rows[:, None, :] > 0, jnp.float32(1.0), indicator)


def up_pass(probs, leaves):
    levels = [leaves]
    messages = []
    logscale = jnp.zeros(leaves.shape[2:], jnp.float32)
    current = leaves
    for height in range(LEVELS):
        amount = current.shape[0]
        offset = 2 * LEAF_DEV - 2 * amount
        message = forward(probs[offset : offset + amount], current)
        messages.append(message)
        raw_parent = message[0::2] * message[1::2]
        scaling = jnp.sum(raw_parent, axis=1)
        current = raw_parent / scaling[:, None, :]
        logscale = logscale + jnp.sum(jnp.log(scaling), axis=0)
        levels.append(current)
    messages.append(forward(probs[EDGES - 1 : EDGES], current))
    return (levels, messages, logscale)


def root_terms(stationary, top_messages, top_logs):
    members = top_messages.shape[0]
    joint = stationary[:, None] * top_messages[0]
    for member in range(1, members):
        joint = joint * top_messages[member]
    site_ll = jnp.log(jnp.sum(joint, axis=0)) + jnp.sum(top_logs, axis=0)
    above_list = []
    for member in range(members):
        vector = jnp.broadcast_to(stationary[:, None], top_messages.shape[1:])
        for other in range(members):
            if other != member:
                vector = vector * top_messages[other]
        above_list.append(vector)
    return (site_ll, jnp.stack(above_list))


def down_pass(probs, levels, messages, above_top):
    a_list = [above_top]
    current = above_top
    for height in range(LEVELS, 0, -1):
        amount = levels[height].shape[0]
        offset = 2 * LEAF_DEV - 2 * amount
        down_part = carried(probs[offset : offset + amount], current)
        down_part = down_part / jnp.sum(down_part, axis=1, keepdims=True)
        message = messages[height - 1]
        current = jnp.stack([down_part * message[1::2], down_part * message[0::2]], axis=1).reshape(
            message.shape
        )
        a_list.append(current)
    return a_list[::-1]


def weigh(a_list, messages, site_weight, total_sites):
    weighted = []
    for vector, message in zip(a_list, messages):
        likelihood = jnp.sum(vector * message, axis=1)
        weighted.append(vector * (site_weight / (likelihood * total_sites))[:, None, :])
    return weighted


def sum_groups(n_site, n_branch):
    s = lax.axis_index("site")
    k = lax.axis_index("branch")
    core = s % 2
    y = (s // 2) % 4
    z = s // 8
    n_z = n_site // 8
    return [
        (2, core, lambda c: (s - core + c, k)),
        (n_branch, k, lambda c: (s, c)),
        (4, y, lambda c: (s - 2 * y + 2 * c, k)),
        (n_z, z, lambda c: (s - 8 * z + 8 * c, k)),
    ]


def allreduce_kernel(n_site, n_branch, x_ref, o_ref, held, send_sems, recv_sems):
    stages = sum_groups(n_site, n_branch)
    barrier = pltpu.get_barrier_semaphore()
    count = 0
    for size, mine, where in stages:
        for d in range(1, size):
            other = lax.rem(mine + d, size)
            pl.semaphore_signal(barrier, inc=1, device_id=where(other), device_id_type=MESH_ID)
            count += 1
    pl.semaphore_wait(barrier, count)
    total = x_ref[...]
    for st, (size, mine, where) in enumerate(stages):
        held[st, mine] = total
        sends = []
        for d in range(1, size):
            other = lax.rem(mine + d, size)
            copy = pltpu.make_async_remote_copy(
                src_ref=held.at[st, mine],
                dst_ref=held.at[st, mine],
                send_sem=send_sems.at[st, other],
                recv_sem=recv_sems.at[st, mine],
                device_id=where(other),
                device_id_type=MESH_ID,
            )
            copy.start()
            sends.append(copy)
        for d in range(1, size):
            other = lax.rem(mine + d, size)
            incoming = pltpu.make_async_remote_copy(
                src_ref=held.at[st, other],
                dst_ref=held.at[st, other],
                send_sem=send_sems.at[st, other],
                recv_sem=recv_sems.at[st, other],
                device_id=where(other),
                device_id_type=MESH_ID,
            )
            incoming.wait_recv()
        for copy in sends:
            copy.wait_send()
        total = held[st, 0]
        for c in range(1, size):
            total = total + held[st, c]
    o_ref[...] = total


def allreduce_all(x, n_site, n_branch):
    rows = x.shape[0]
    return pl.pallas_call(
        functools.partial(allreduce_kernel, n_site, n_branch),
        out_shape=jax.ShapeDtypeStruct(x.shape, jnp.float32),
        in_specs=[pl.BlockSpec(memory_space=pltpu.VMEM)],
        out_specs=pl.BlockSpec(memory_space=pltpu.VMEM),
        scratch_shapes=[
            pltpu.VMEM((4, 4, rows, 128), jnp.float32),
            pltpu.SemaphoreType.DMA((4, 4)),
            pltpu.SemaphoreType.DMA((4, 4)),
        ],
        compiler_params=pltpu.CompilerParams(collective_id=0, has_side_effects=True),
    )(x)


def exchange_kernel(axis, gather, x_ref, o_ref, held, send_sems, recv_sems):
    n = held.shape[0]
    me = lax.axis_index(axis)
    other_axis = "branch" if axis == "site" else "site"
    fixed = lax.axis_index(other_axis)

    def device(p):
        return (p, fixed) if axis == "site" else (fixed, p)

    barrier = pltpu.get_barrier_semaphore()

    def greet(d, carry):
        pl.semaphore_signal(
            barrier, inc=1, device_id=device(lax.rem(me + d, n)), device_id_type=MESH_ID
        )
        return carry

    lax.fori_loop(1, n, greet, 0)
    pl.semaphore_wait(barrier, n - 1)
    if gather:
        held[me] = x_ref[...]
    else:
        held[me] = x_ref[me]

    def outgoing(d):
        p = lax.rem(me + d, n)
        return pltpu.make_async_remote_copy(
            src_ref=x_ref if gather else x_ref.at[p],
            dst_ref=held.at[me],
            send_sem=send_sems.at[p],
            recv_sem=recv_sems.at[me],
            device_id=device(p),
            device_id_type=MESH_ID,
        )

    def send(d, carry):
        outgoing(d).start()
        return carry

    lax.fori_loop(1, n, send, 0)

    def receive(d, carry):
        p = lax.rem(me + n - d, n)
        pltpu.make_async_remote_copy(
            src_ref=held.at[p],
            dst_ref=held.at[p],
            send_sem=send_sems.at[p],
            recv_sem=recv_sems.at[p],
            device_id=device(p),
            device_id_type=MESH_ID,
        ).wait_recv()
        return carry

    lax.fori_loop(1, n, receive, 0)

    def sent(d, carry):
        outgoing(d).wait_send()
        return carry

    lax.fori_loop(1, n, sent, 0)
    if gather:
        o_ref[...] = held[...]
    else:
        o_ref[...] = lax.fori_loop(1, n, lambda j, acc: acc + held[j], held[0])


def exchange(x, axis, n, gather, collective_id):
    chunk = x.shape if gather else x.shape[1:]
    out_shape = (n,) + chunk if gather else chunk
    return pl.pallas_call(
        functools.partial(exchange_kernel, axis, gather),
        out_shape=jax.ShapeDtypeStruct(out_shape, jnp.float32),
        in_specs=[pl.BlockSpec(memory_space=pltpu.VMEM)],
        out_specs=pl.BlockSpec(memory_space=pltpu.VMEM),
        scratch_shapes=[
            pltpu.VMEM((n,) + chunk, jnp.float32),
            pltpu.SemaphoreType.DMA((n,)),
            pltpu.SemaphoreType.DMA((n,)),
        ],
        compiler_params=pltpu.CompilerParams(collective_id=collective_id, has_side_effects=True),
    )(x)


def pair_scatter_kernel(x_ref, o_ref, pair_buf, pair_sum, held, sems_a, sems_b, sems_c, sems_d):
    n = x_ref.shape[0]
    chips = n // 2
    s = lax.axis_index("site")
    k = lax.axis_index("branch")
    core = s % 2
    chip = s // 2
    partner = s - core + (1 - core)
    barrier = pltpu.get_barrier_semaphore()
    pl.semaphore_signal(barrier, inc=1, device_id=(partner, k), device_id_type=MESH_ID)

    def greet(d, carry):
        peer = 2 * lax.rem(chip + d, chips) + core
        pl.semaphore_signal(barrier, inc=1, device_id=(peer, k), device_id_type=MESH_ID)
        return carry

    lax.fori_loop(1, chips, greet, 0)
    pl.semaphore_wait(barrier, chips)

    def to_partner(m):
        return pltpu.make_async_remote_copy(
            src_ref=x_ref.at[2 * m + 1 - core],
            dst_ref=pair_buf.at[m],
            send_sem=sems_a.at[m],
            recv_sem=sems_b.at[m],
            device_id=(partner, k),
            device_id_type=MESH_ID,
        )

    def first_send(m, carry):
        to_partner(m).start()
        return carry

    lax.fori_loop(0, chips, first_send, 0)

    def first_recv(m, carry):
        to_partner(m).wait_recv()
        return carry

    lax.fori_loop(0, chips, first_recv, 0)

    def first_sent(m, carry):
        to_partner(m).wait_send()
        return carry

    lax.fori_loop(0, chips, first_sent, 0)

    def add_pair(m, carry):
        pair_sum[m] = x_ref[2 * m + core] + pair_buf[m]
        return carry

    lax.fori_loop(0, chips, add_pair, 0)
    held[chip] = pair_sum[chip]

    def to_chip(d):
        c = lax.rem(chip + d, chips)
        return pltpu.make_async_remote_copy(
            src_ref=pair_sum.at[c],
            dst_ref=held.at[chip],
            send_sem=sems_c.at[c],
            recv_sem=sems_d.at[chip],
            device_id=(2 * c + core, k),
            device_id_type=MESH_ID,
        )

    def second_send(d, carry):
        to_chip(d).start()
        return carry

    lax.fori_loop(1, chips, second_send, 0)

    def second_recv(d, carry):
        c = lax.rem(chip + chips - d, chips)
        pltpu.make_async_remote_copy(
            src_ref=held.at[c],
            dst_ref=held.at[c],
            send_sem=sems_c.at[c],
            recv_sem=sems_d.at[c],
            device_id=(2 * c + core, k),
            device_id_type=MESH_ID,
        ).wait_recv()
        return carry

    lax.fori_loop(1, chips, second_recv, 0)

    def second_sent(d, carry):
        to_chip(d).wait_send()
        return carry

    lax.fori_loop(1, chips, second_sent, 0)
    o_ref[...] = lax.fori_loop(1, chips, lambda j, acc: acc + held[j], held[0])


def pair_scatter(x, collective_id):
    n = x.shape[0]
    chunk = x.shape[1:]
    return pl.pallas_call(
        pair_scatter_kernel,
        out_shape=jax.ShapeDtypeStruct(chunk, jnp.float32),
        in_specs=[pl.BlockSpec(memory_space=pltpu.VMEM)],
        out_specs=pl.BlockSpec(memory_space=pltpu.VMEM),
        scratch_shapes=[
            pltpu.VMEM((n // 2,) + chunk, jnp.float32),
            pltpu.VMEM((n // 2,) + chunk, jnp.float32),
            pltpu.VMEM((n // 2,) + chunk, jnp.float32),
            pltpu.SemaphoreType.DMA((n // 2,)),
            pltpu.SemaphoreType.DMA((n // 2,)),
            pltpu.SemaphoreType.DMA((n // 2,)),
            pltpu.SemaphoreType.DMA((n // 2,)),
        ],
        compiler_params=pltpu.CompilerParams(collective_id=collective_id, has_side_effects=True),
    )(x)


def pair_gather_kernel(x_ref, o_ref, held, sems_a, sems_b, sems_c, sems_d):
    n = held.shape[0]
    chips = n // 2
    s = lax.axis_index("site")
    k = lax.axis_index("branch")
    core = s % 2
    chip = s // 2
    partner = s - core + (1 - core)
    barrier = pltpu.get_barrier_semaphore()
    pl.semaphore_signal(barrier, inc=1, device_id=(partner, k), device_id_type=MESH_ID)

    def greet(d, carry):
        peer = 2 * lax.rem(chip + d, chips) + core
        pl.semaphore_signal(barrier, inc=1, device_id=(peer, k), device_id_type=MESH_ID)
        return carry

    lax.fori_loop(1, chips, greet, 0)
    pl.semaphore_wait(barrier, chips)
    held[s] = x_ref[...]

    def to_chip(d):
        c = lax.rem(chip + d, chips)
        return pltpu.make_async_remote_copy(
            src_ref=x_ref,
            dst_ref=held.at[s],
            send_sem=sems_a.at[c],
            recv_sem=sems_b.at[chip],
            device_id=(2 * c + core, k),
            device_id_type=MESH_ID,
        )

    def first_send(d, carry):
        to_chip(d).start()
        return carry

    lax.fori_loop(1, chips, first_send, 0)

    def first_recv(d, carry):
        c = lax.rem(chip + chips - d, chips)
        pltpu.make_async_remote_copy(
            src_ref=held.at[2 * c + core],
            dst_ref=held.at[2 * c + core],
            send_sem=sems_a.at[c],
            recv_sem=sems_b.at[c],
            device_id=(2 * c + core, k),
            device_id_type=MESH_ID,
        ).wait_recv()
        return carry

    lax.fori_loop(1, chips, first_recv, 0)

    def to_partner(d):
        c = lax.rem(chip + d, chips)
        return pltpu.make_async_remote_copy(
            src_ref=held.at[2 * c + core],
            dst_ref=held.at[2 * c + core],
            send_sem=sems_c.at[c],
            recv_sem=sems_d.at[c],
            device_id=(partner, k),
            device_id_type=MESH_ID,
        )

    own = pltpu.make_async_remote_copy(
        src_ref=x_ref,
        dst_ref=held.at[s],
        send_sem=sems_c.at[chip],
        recv_sem=sems_d.at[chip],
        device_id=(partner, k),
        device_id_type=MESH_ID,
    )
    own.start()

    def second_send(d, carry):
        to_partner(d).start()
        return carry

    lax.fori_loop(1, chips, second_send, 0)

    def second_recv(c, carry):
        pltpu.make_async_remote_copy(
            src_ref=held.at[2 * c + 1 - core],
            dst_ref=held.at[2 * c + 1 - core],
            send_sem=sems_c.at[c],
            recv_sem=sems_d.at[c],
            device_id=(partner, k),
            device_id_type=MESH_ID,
        ).wait_recv()
        return carry

    lax.fori_loop(0, chips, second_recv, 0)

    def first_sent(d, carry):
        to_chip(d).wait_send()
        return carry

    lax.fori_loop(1, chips, first_sent, 0)
    own.wait_send()

    def second_sent(d, carry):
        to_partner(d).wait_send()
        return carry

    lax.fori_loop(1, chips, second_sent, 0)
    o_ref[...] = held[...]


def pair_gather(x, n, collective_id):
    return pl.pallas_call(
        pair_gather_kernel,
        out_shape=jax.ShapeDtypeStruct((n,) + x.shape, jnp.float32),
        in_specs=[pl.BlockSpec(memory_space=pltpu.VMEM)],
        out_specs=pl.BlockSpec(memory_space=pltpu.VMEM),
        scratch_shapes=[
            pltpu.VMEM((n,) + x.shape, jnp.float32),
            pltpu.SemaphoreType.DMA((n // 2,)),
            pltpu.SemaphoreType.DMA((n // 2,)),
            pltpu.SemaphoreType.DMA((n // 2,)),
            pltpu.SemaphoreType.DMA((n // 2,)),
        ],
        compiler_params=pltpu.CompilerParams(collective_id=collective_id, has_side_effects=True),
    )(x)


def body(
    states, gap_mask, weights, leaf_order, exchanges, codon_freq, omega_ratio, lengths, classes
):
    site_count = lax.axis_size("site")
    site_pos = lax.axis_index("site")
    subtree = lax.axis_index("branch")
    site_span = states.shape[1]
    total_sites = site_span * site_count
    total_taxa = LEAF_DEV * lax.axis_size("branch")
    rate_matrix, stationary = build_rates(exchanges, codon_freq, omega_ratio)
    slot_len = jnp.concatenate([lengths, jnp.zeros((1,), lengths.dtype)])
    slot_cls = jnp.concatenate([classes, jnp.zeros((1,), jnp.int32)])
    class_pick = (slot_cls[:, None] == jnp.arange(CLASSES, dtype=jnp.int32)[None, :]).astype(
        jnp.float32
    )
    slot_rates = jnp.einsum("bc,cij->bij", class_pick, rate_matrix, precision=lax.Precision.HIGH)
    scaled = slot_rates * slot_len[:, None, None]
    per_dev = SLOTS // site_count
    own_start = site_pos * per_dev
    own_scaled = lax.dynamic_slice_in_dim(scaled, own_start, per_dev, 0)
    own_pull = None
    own_probs, own_pull = jax.vjp(expm_taylor, own_scaled)
    dense = pair_gather(own_probs.reshape(-1, 128), site_count, 1)
    probs = dense.reshape((site_count * per_dev,) + own_probs.shape[1:])
    taxon_rows = lax.dynamic_slice_in_dim(leaf_order, subtree * LEAF_DEV, LEAF_DEV, 0)
    leaves = leaf_partials(
        jnp.take(states, taxon_rows, axis=0), jnp.take(gap_mask, taxon_rows, axis=0)
    )
    levels, messages, logscale = up_pass(probs, leaves)
    top_pack = jnp.concatenate([messages[-1][0], logscale[None, :]], axis=0)
    top_all = lax.all_gather(top_pack, "branch", axis=0, tiled=False)
    top_messages, top_logs = top_all[:, :64, :], top_all[:, 64, :]
    site_ll, above_all = root_terms(stationary, top_messages, top_logs)
    site_weight = weights.astype(jnp.float32)
    loglik_part = jnp.sum(site_weight * site_ll)
    above_top = lax.dynamic_slice_in_dim(above_all, subtree, 1, 0)
    a_list = down_pass(probs, levels, messages, above_top)
    weighted = weigh(a_list, messages, site_weight, total_sites)
    padding = jnp.zeros((1, 64, site_span), jnp.float32)
    weighted_all = jnp.concatenate(weighted + [padding], axis=0)
    partial_all = jnp.concatenate(levels + [padding], axis=0)
    part_above = lax.slice_in_dim(weighted_all, 0, lax.axis_size("site") * per_dev, axis=0)
    part_below = lax.slice_in_dim(partial_all, 0, lax.axis_size("site") * per_dev, axis=0)
    part_counts = jnp.einsum("bis,bjs->bij", part_above, part_below, precision=lax.Precision.HIGH)
    own_counts = pair_scatter(part_counts.reshape(site_count, -1, 128), 2).reshape((per_dev, 64, 64))
    d_scaled = own_pull(own_counts)[0]
    use_rates = lax.dynamic_slice_in_dim(slot_rates, own_start, per_dev, 0)
    use_len = lax.dynamic_slice_in_dim(slot_len, own_start, per_dev, 0)
    use_pick = lax.dynamic_slice_in_dim(class_pick, own_start, per_dev, 0)
    d_length = jnp.sum(d_scaled * use_rates, axis=(1, 2))
    d_rates = jnp.einsum(
        "bc,bij->cij", use_pick, d_scaled * use_len[:, None, None], precision=lax.Precision.HIGH
    )
    unused_rates, pull_rates = jax.vjp(
        lambda table, ratio: build_rates(table, codon_freq, ratio)[0], exchanges, omega_ratio
    )
    d_exch, d_omega = pull_rates(d_rates)
    n_branch = lax.axis_size("branch")
    length_slab = jnp.zeros((n_branch, SLOTS), jnp.float32)
    length_slab = lax.dynamic_update_slice(length_slab, d_length[None, :], (subtree, own_start))
    loglik_keep = jnp.where(subtree == 0, loglik_part, jnp.float32(0.0))
    packed = jnp.concatenate(
        [d_exch.reshape(-1), d_omega, length_slab.reshape(-1), loglik_keep[None]]
    )
    rows = -(-packed.shape[0] // (8 * 128)) * 8
    packed = jnp.pad(packed, (0, rows * 128 - packed.shape[0])).reshape(rows, 128)
    summed = allreduce_all(packed, site_count, n_branch).reshape(-1)
    grad_exch = summed[: 64 * 64].reshape(64, 64)
    grad_omega = summed[64 * 64 : 64 * 64 + CLASSES]
    length_all = summed[64 * 64 + CLASSES : 64 * 64 + CLASSES + n_branch * SLOTS].reshape(n_branch, SLOTS)
    log_total = summed[64 * 64 + CLASSES + n_branch * SLOTS]
    loglik = log_total / total_sites / total_taxa
    length_out = lax.dynamic_index_in_dim(length_all, subtree, 0, keepdims=False)[:EDGES]
    return (grad_exch, grad_omega, length_out, loglik)


def solution(mesh):
    return jax.shard_map(
        body,
        mesh=mesh,
        in_specs=(
            P(None, "site"),
            P(None, "site"),
            P("site"),
            P(),
            P(),
            P(),
            P(),
            P("branch"),
            P("branch"),
        ),
        out_specs=(P(), P(), P("branch"), P()),
        check_vma=False,
    )
```

profile of v0, /device:TPU:1, one launch (start us, length us, event | category | flops | bytes accessed | tf_op | source)
XLA Modules:
  0.0 205.4 jit_solution(1145670123064384596)
XLA Ops:
  4.2 1.2 convert_element_type.44
  5.4 1.3 fusion.78
  8.1 0.8 copy.140
  8.9 0.8 fusion.63
  9.7 1.0 fusion.29
  12.7 1.6 gather_fusion
  14.4 2.2 %fusion.27 = f32[128,64,64]{0,2,1:T(8,128)S(1)} fusion(f32[8]{0:T(128)S(1)} %multiply_reduce_fusion.10, f32[64,64]{1,0:T(8,128)S(1)} %fusion.64, f32[8,64]{0,1:T(8,128)S(1)} %fusion.29, f32[64,64]{1,0:T(8,128)} %constant.112, f32[8]{0:T(128)S(1)} %broadcast_add_fusion, f32[64,64]{1,0:T(8,128)} %constant.111, f32[64,64]{1,0:T(8,128)S(1)} %fusion.63, ...), kind=kOutput, calls=%fused_computation.95 | convolution fusion | flops 25396224 | bytes 2165312 | tf_op jit(solution)/shard_map/bc,cij->bij/dot_general | solution.py:545
  23.7 26.8 %shard_map.174 = f32[32,128,128]{2,1,0:T(8,128)} custom-call(f32[128,128]{1,0:T(8,128)} %reshape.322.x_ref), custom_call_target="tpu_custom_call" | custom-call | tf_op jit(solution)/shard_map/pallas_call | solution.py:514
  50.6 0.9 slice.149
  52.2 0.9 slice.147
  53.2 0.8 slice.148
  54.0 1.0 slice.145
  55.0 0.9 slice.146
  55.9 1.1 slice.143
  57.0 1.2 slice.144
  58.6 3.1 %fusion.7 = f32[64,64,256]{2,1,0:T(8,128)S(1)} fusion(f32[64,64,64]{2,1,0:T(8,128)S(1)} %slice.154, s32[64,256]{1,0:T(8,128)} %broadcast_select_fusion, pred[64,256]{1,0:T(8,128)(4,1)S(1)} %select_compare_fusion), kind=kOutput, calls=%fused_computation.13 | convolution fusion | flops 405798912 | bytes 5324800 | tf_op jit(solution)/shard_map/bij,bjs->bis/dot_general | solution.py:62
  62.2 0.9 log_reduce_fusion
  63.1 1.1 fusion.24
  69.0 4.3 %reshape.323 = f32[128,64,64]{2,1,0:T(8,128)} reshape(f32[32,128,128]{2,1,0:T(8,128)} %shard_map.174) | data formatting | bytes 4194304 | tf_op jit(solution)/shard_map/reshape | solution.py:553
  73.4 1.0 fusion.61
  75.2 0.9 fusion.54
  76.2 10.2 %all-gather.1 = f32[4,65,256]{2,1,0:T(8,128)S(1)} all-gather(f32[1,65,256]{2,1,0:T(8,128)S(1)} %maximum_bitcast_fusion.2), channel_id=2, replica_groups=mesh['site'=32,'branch'=4] {'branch'}, dimensions={0}, use_global_device_ids=true | all-gather | bytes 332800 | tf_op jit(solution)/shard_map/all_gather | solution.py:560
  88.4 1.9 multiply_reduce_fusion.11
  90.9 1.2 fusion.79
  92.0 0.9 fusion.50
  92.9 1.1 fusion.44
  94.4 0.9 multiply_reduce_fusion.9
  96.8 1.2 fusion.84
  101.3 1.0 fusion.12
  104.0 1.1 fusion.87
  105.2 1.9 fusion.11
  107.1 2.7 %fusion.6 = f32[128,64,256]{2,1,0:T(8,128)} fusion(s32[64,256]{1,0:T(8,128)S(1)} %copy-done.38, pred[64,256]{1,0:T(8,128)(4,1)S(1)} %select_compare_fusion), kind=kLoop, calls=%fused_computation.12 | loop fusion | flops 3145727 | bytes 4276224
  109.8 2.4 %multiply_bitcast_fusion.1 = (f32[32,1,64,256]{3,2,0,1:T(8,128)S(1)}, f32[32,1,64,256]{3,2,0,1:T(8,128)S(1)}, f32[128,64,256]{2,1,0:T(8,128)}) fusion(f32[32,64,256]{2,1,0:T(8,128)S(1)} %fusion.11, f32[64,64,256]{2,1,0:T(8,128)S(1)} %copy-done.3, f32[128,64,256]{2,1,0:T(8,128)} %fusion.6, f32[32,256]{1,0:T(8,128)S(1)} %copy-done.44), kind=kLoop, calls=%fused_computation.19 | loop fusion | flops 2097152 | bytes 12615680 | tf_op jit(solution)/shard_map/stack | solution.py:119
  112.8 1.4 fusion.5
  114.2 3.4 %constant_dynamic-update-slice_fusion.1 = f32[128,64,256]{2,1,0:T(8,128)} fusion(f32[64,256]{1,0:T(8,128)S(1)} %multiply_divide_fusion, f32[32,2,64,256]{3,2,1,0:T(8,128)S(1)} %copy.152), kind=kLoop, calls=%fused_computation.166 | loop fusion | flops 1048575 | bytes 8454144
  117.6 1.5 multiply_dynamic-update-slice_fusion
  119.2 1.1 multiply_dynamic-update-slice_fusion.1
  120.2 0.8 multiply_dynamic-update-slice_fusion.2
  123.1 1.2 fusion.25
  124.2 0.9 fusion.30
  127.8 11.7 %fusion.88 = f32[128,64,64]{2,1,0:T(8,128)} fusion(f32[128,64,256]{2,1,0:T(8,128)} %get-tuple-element.43, f32[128,64,256]{2,1,0:T(8,128)} %get-tuple-element.44), kind=kOutput, calls=%fused_computation.232 | convolution fusion | flops 805306368 | bytes 18874368 | tf_op jit(solution)/shard_map/bis,bjs->bij/dot_general | solution.py:573
  139.5 4.7 %reshape.333.x_ref = f32[32,128,128]{2,1,0:T(8,128)} reshape(f32[128,64,64]{2,1,0:T(8,128)} %fusion.88) | data formatting | bytes 4194304 | tf_op jit(solution)/shard_map/reshape | solution.py:574
  144.3 28.0 %shard_map.175 = f32[128,128]{1,0:T(8,128)} custom-call(f32[32,128,128]{2,1,0:T(8,128)} %reshape.333.x_ref), custom_call_target="tpu_custom_call" | custom-call | tf_op jit(solution)/shard_map/pallas_call | solution.py:389
  172.3 1.0 reshape.334
  180.6 1.2 multiply_reduce_fusion.5
  183.3 15.2 %shard_map.176 = f32[40,128]{1,0:T(8,128)} custom-call(f32[40,128]{1,0:T(8,128)} %pad_bitcast_fusion.x_ref), custom_call_target="tpu_custom_call" | custom-call | tf_op jit(solution)/shard_map/pallas_call | solution.py:196
  198.5 1.3 slice.192
  200.4 1.2 slice.190
  (269 shorter events, 45.7 us)
Async XLA Ops:
  0.6 10.7 %copy-start = (s32[256,256]{1,0:T(8,128)S(1)}, s32[256,256]{1,0:T(8,128)}, u32[]{:S(2)}) copy-start(s32[256,256]{1,0:T(8,128)} %param.17) | copy-start | bytes 786436
  1.4 16.6 %copy-start.64 = (f32[8]{0:T(128)}, f32[8]{0:T(128)S(1)}, u32[]{:S(2)}) copy-start(f32[8]{0:T(128)S(1)} %broadcast_add_fusion) | copy-start | bytes 100
  3.4 16.5 %copy-start.51 = (f32[4]{0:T(128)}, f32[4]{0:T(128)S(1)}, u32[]{:S(2)}) copy-start(f32[4]{0:T(128)S(1)} %get-tuple-element.10) | copy-start | bytes 52
  8.1 11.9 %copy-start.8 = (f32[64,64]{1,0:T(8,128)}, f32[64,64]{1,0:T(8,128)S(1)}, u32[]{:S(2)}) copy-start(f32[64,64]{1,0:T(8,128)S(1)} %fusion.64) | copy-start | bytes 49156
  9.7 6.9 %copy-start.40 = (f32[64,64]{1,0:T(8,128)}, f32[64,64]{1,0:T(8,128)S(1)}, u32[]{:S(2)}) copy-start(f32[64,64]{1,0:T(8,128)S(1)} %fusion.63) | copy-start | bytes 49156
  10.7 5.9 %copy-start.45 = (f32[8,64]{0,1:T(8,128)}, f32[8,64]{0,1:T(8,128)S(1)}, u32[]{:S(2)}) copy-start(f32[8,64]{0,1:T(8,128)S(1)} %fusion.29) | copy-start | bytes 6148
  10.8 7.2 %copy-start.66 = (f32[8]{0:T(128)}, f32[8]{0:T(128)S(1)}, u32[]{:S(2)}) copy-start(f32[8]{0:T(128)S(1)} %multiply_reduce_fusion.10) | copy-start | bytes 100
  18.8 36.1 %copy-start.28 = (f32[4,64,64]{2,1,0:T(8,128)}, f32[4,64,64]{2,1,0:T(8,128)S(1)}, u32[]{:S(2)}) copy-start(f32[4,64,64]{2,1,0:T(8,128)S(1)} %fusion.20) | copy-start | bytes 196612
  19.1 35.9 %copy-start.30 = (f32[4,64,64]{2,1,0:T(8,128)}, f32[4,64,64]{2,1,0:T(8,128)S(1)}, u32[]{:S(2)}) copy-start(f32[4,64,64]{2,1,0:T(8,128)S(1)} %fusion.19) | copy-start | bytes 196612
  19.4 35.6 %copy-start.32 = (f32[4,64,64]{2,1,0:T(8,128)}, f32[4,64,64]{2,1,0:T(8,128)S(1)}, u32[]{:S(2)}) copy-start(f32[4,64,64]{2,1,0:T(8,128)S(1)} %fusion.18) | copy-start | bytes 196612
  19.7 35.3 %copy-start.34 = (f32[4,64,64]{2,1,0:T(8,128)}, f32[4,64,64]{2,1,0:T(8,128)S(1)}, u32[]{:S(2)}) copy-start(f32[4,64,64]{2,1,0:T(8,128)S(1)} %fusion.17) | copy-start | bytes 196612
  21.7 36.5 %copy-start.10 = (f32[4,64,64]{2,1,0:T(8,128)}, f32[4,64,64]{2,1,0:T(8,128)S(1)}, u32[]{:S(2)}) copy-start(f32[4,64,64]{2,1,0:T(8,128)S(1)} %fusion.80) | copy-start | bytes 196612
  21.9 36.3 %copy-start.12 = (f32[4,64,64]{2,1,0:T(8,128)}, f32[4,64,64]{2,1,0:T(8,128)S(1)}, u32[]{:S(2)}) copy-start(f32[4,64,64]{2,1,0:T(8,128)S(1)} %fusion.81) | copy-start | bytes 196612
  50.6 7.7 %slice-start = ((f32[32,128,128]{2,1,0:T(8,128)}), f32[16,128,128]{2,1,0:T(8,128)S(1)}, s32[]{:S(2)}) async-start(f32[32,128,128]{2,1,0:T(8,128)} %shard_map.174), calls=%async_computation | async-start | bytes 2097152 | tf_op jit(solution)/shard_map/slice | solution.py:83
  58.6 4.6 %copy-start.6 = (f32[32,64,64]{2,1,0:T(8,128)S(1)}, f32[32,64,64]{2,1,0:T(8,128)}, u32[]{:S(2)}) copy-start(f32[32,64,64]{2,1,0:T(8,128)} %slice.144) | copy-start | bytes 1572868
  90.9 7.4 %copy-start.5 = (f32[8,64,256]{2,1,0:T(8,128)S(1)}, f32[8,64,256]{2,1,0:T(8,128)}, u32[]{:S(2)}) copy-start(f32[8,64,256]{2,1,0:T(8,128)} %copy-done.4) | copy-start | bytes 1572868
  105.2 4.6 %copy-start.3 = (f32[64,64,256]{2,1,0:T(8,128)S(1)}, f32[64,64,256]{2,1,0:T(8,128)}, u32[]{:S(2)}) copy-start(f32[64,64,256]{2,1,0:T(8,128)} %copy-done.2) | copy-start | bytes 12582916
  117.6 4.8 %copy-start.39 = (f32[1,64,256]{2,1,0:T(8,128)S(1)}, f32[1,64,256]{2,1,0:T(8,128)}, u32[]{:S(2)}) copy-start(f32[1,64,256]{2,1,0:T(8,128)} %get-tuple-element.12) | copy-start | bytes 196612
  117.6 4.8 %copy-start.68 = (f32[256]{0:T(256)S(1)}, f32[256]{0:T(256)}, u32[]{:S(2)}) copy-start(f32[256]{0:T(256)} %get-tuple-element.39) | copy-start | bytes 3076
  117.6 5.5 %copy-start.50 = (f32[16,256]{1,0:T(8,128)S(1)}, f32[16,256]{1,0:T(8,128)}, u32[]{:S(2)}) copy-start(f32[16,256]{1,0:T(8,128)} %copy-done.49) | copy-start | bytes 49156
  119.2 5.1 %copy-start.54 = (f32[8,256]{1,0:T(8,128)S(1)}, f32[8,256]{1,0:T(8,128)}, u32[]{:S(2)}) copy-start(f32[8,256]{1,0:T(8,128)} %copy-done.53) | copy-start | bytes 24580
  119.2 6.0 %copy-start.57 = (f32[4,256]{1,0:T(4,128)S(1)}, f32[4,256]{1,0:T(4,128)}, u32[]{:S(2)}) copy-start(f32[4,256]{1,0:T(4,128)} %copy-done.56) | copy-start | bytes 12292
  120.2 5.6 %copy-start.61 = (f32[2,256]{1,0:T(2,128)S(1)}, f32[2,256]{1,0:T(2,128)}, u32[]{:S(2)}) copy-start(f32[2,256]{1,0:T(2,128)} %copy-done.60) | copy-start | bytes 6148
  120.2 6.3 %copy-start.21 = (f32[2,64,256]{2,1,0:T(8,128)S(1)}, f32[2,64,256]{2,1,0:T(8,128)}, u32[]{:S(2)}) copy-start(f32[2,64,256]{2,1,0:T(8,128)} %copy-done.20) | copy-start | bytes 393220
  120.2 6.3 %copy-start.63 = (f32[256]{0:T(256)S(1)}, f32[256]{0:T(256)}, u32[]{:S(2)}) copy-start(f32[256]{0:T(256)} %copy-done.62) | copy-start | bytes 3076
  139.5 33.7 %copy-start.15 = (f32[4,64,64]{2,1,0:T(8,128)S(1)}, f32[4,64,64]{2,1,0:T(8,128)}, u32[]{:S(2)}) copy-start(f32[4,64,64]{2,1,0:T(8,128)} %copy-done.14) | copy-start | bytes 196612
  139.5 34.3 %copy-start.13 = (f32[4,64,64]{2,1,0:T(8,128)S(1)}, f32[4,64,64]{2,1,0:T(8,128)}, u32[]{:S(2)}) copy-start(f32[4,64,64]{2,1,0:T(8,128)} %copy-done.12) | copy-start | bytes 196612
  139.5 34.8 %copy-start.11 = (f32[4,64,64]{2,1,0:T(8,128)S(1)}, f32[4,64,64]{2,1,0:T(8,128)}, u32[]{:S(2)}) copy-start(f32[4,64,64]{2,1,0:T(8,128)} %copy-done.10) | copy-start | bytes 196612
  139.5 35.5 %copy-start.17 = (f32[4,64,64]{2,1,0:T(8,128)S(1)}, f32[4,64,64]{2,1,0:T(8,128)}, u32[]{:S(2)}) copy-start(f32[4,64,64]{2,1,0:T(8,128)} %copy-done.16) | copy-start | bytes 196612
  144.2 31.3 %copy-start.23 = (f32[4,64,64]{2,1,0:T(8,128)S(1)}, f32[4,64,64]{2,1,0:T(8,128)}, u32[]{:S(2)}) copy-start(f32[4,64,64]{2,1,0:T(8,128)} %copy-done.22) | copy-start | bytes 196612
  144.2 31.5 %copy-start.52 = (f32[4]{0:T(128)S(1)}, f32[4]{0:T(128)}, u32[]{:S(2)}) copy-start(f32[4]{0:T(128)} %copy-done.51) | copy-start | bytes 52
  144.2 31.9 %copy-start.35 = (f32[4,64,64]{2,1,0:T(8,128)S(1)}, f32[4,64,64]{2,1,0:T(8,128)}, u32[]{:S(2)}) copy-start(f32[4,64,64]{2,1,0:T(8,128)} %copy-done.34) | copy-start | bytes 196612
  144.2 32.5 %copy-start.33 = (f32[4,64,64]{2,1,0:T(8,128)S(1)}, f32[4,64,64]{2,1,0:T(8,128)}, u32[]{:S(2)}) copy-start(f32[4,64,64]{2,1,0:T(8,128)} %copy-done.32) | copy-start | bytes 196612
  144.2 33.2 %copy-start.31 = (f32[4,64,64]{2,1,0:T(8,128)S(1)}, f32[4,64,64]{2,1,0:T(8,128)}, u32[]{:S(2)}) copy-start(f32[4,64,64]{2,1,0:T(8,128)} %copy-done.30) | copy-start | bytes 196612
  172.2 5.8 %copy-start.29 = (f32[4,64,64]{2,1,0:T(8,128)S(1)}, f32[4,64,64]{2,1,0:T(8,128)}, u32[]{:S(2)}) copy-start(f32[4,64,64]{2,1,0:T(8,128)} %copy-done.28) | copy-start | bytes 196612
  172.3 6.4 %copy-start.27 = (f32[4,64,64]{2,1,0:T(8,128)S(1)}, f32[4,64,64]{2,1,0:T(8,128)}, u32[]{:S(2)}) copy-start(f32[4,64,64]{2,1,0:T(8,128)} %copy-done.26) | copy-start | bytes 196612
  173.8 5.5 %copy-start.25 = (f32[4,64,64]{2,1,0:T(8,128)S(1)}, f32[4,64,64]{2,1,0:T(8,128)}, u32[]{:S(2)}) copy-start(f32[4,64,64]{2,1,0:T(8,128)} %copy-done.24) | copy-start | bytes 196612
  174.3 5.5 %copy-start.9 = (f32[64,64]{1,0:T(8,128)S(1)}, f32[64,64]{1,0:T(8,128)}, u32[]{:S(2)}) copy-start(f32[64,64]{1,0:T(8,128)} %copy-done.8) | copy-start | bytes 49156
  174.4 5.5 %copy-start.69 = (f32[4]{0:T(128)S(1)}, f32[4]{0:T(128)}, u32[]{:S(2)}) copy-start(f32[4]{0:T(128)} %get-tuple-element.9) | copy-start | bytes 52
  174.7 5.9 %copy-start.41 = (f32[64,64]{1,0:T(8,128)S(1)}, f32[64,64]{1,0:T(8,128)}, u32[]{:S(2)}) copy-start(f32[64,64]{1,0:T(8,128)} %copy-done.40) | copy-start | bytes 49156
  174.7 5.9 %copy-start.46 = (f32[8,64]{0,1:T(8,128)S(1)}, f32[8,64]{0,1:T(8,128)}, u32[]{:S(2)}) copy-start(f32[8,64]{0,1:T(8,128)} %copy-done.45) | copy-start | bytes 6148
  174.7 5.9 %copy-start.47 = (f32[64,64]{1,0:T(8,128)S(1)}, f32[64,64]{1,0:T(8,128)}, u32[]{:S(2)}) copy-start(f32[64,64]{1,0:T(8,128)} %constant.112) | copy-start | bytes 49156
  174.7 5.9 %copy-start.48 = (f32[64,64]{1,0:T(8,128)S(1)}, f32[64,64]{1,0:T(8,128)}, u32[]{:S(2)}) copy-start(f32[64,64]{1,0:T(8,128)} %constant.111) | copy-start | bytes 49156
  174.7 5.9 %copy-start.65 = (f32[8]{0:T(128)S(1)}, f32[8]{0:T(128)}, u32[]{:S(2)}) copy-start(f32[8]{0:T(128)} %copy-done.64) | copy-start | bytes 100
  174.7 5.9 %copy-start.67 = (f32[8]{0:T(128)S(1)}, f32[8]{0:T(128)}, u32[]{:S(2)}) copy-start(f32[8]{0:T(128)} %copy-done.66) | copy-start | bytes 100
  174.7 5.9 %copy-start.70 = (f32[8]{0:T(128)S(1)}, f32[8]{0:T(128)}, u32[]{:S(2)}) copy-start(f32[8]{0:T(128)} %multiply_divide_fusion.7) | copy-start | bytes 100
  175.8 6.1 %copy-start.59 = (f32[64]{0:T(128)S(1)}, f32[64]{0:T(128)}, u32[]{:S(2)}) copy-start(f32[64]{0:T(128)} %copy-done.58) | copy-start | bytes 772
  176.2 28.1 %copy-start.1 = (s32[256,256]{1,0:T(8,128)S(1)}, s32[256,256]{1,0:T(8,128)}, u32[]{:S(2)}) copy-start(s32[256,256]{1,0:T(8,128)} %param.17) | copy-start | bytes 786436
  (24 other events, 44.8 us)
where the time goes:
time: 208 us; the launch traced here: 205 us
  Pallas kernels  70 us (34%)
  other arithmetic  48.4 us (23%)
  matrix products  37.7 us (18%)
  local copies, waits for them, and re-layouts  34.5 us (17%)
  blocking collectives  10.2 us (5%)
  between operations  4.57 us (2%)
    pallas_call x1, Pallas kernels, pair_scatter(): pl.pallas_call(pair_scatter_kernel, out_shape=jax.ShapeDtypeStruct(chunk,...  28 us
    pallas_call x1, Pallas kernels, pair_gather(): pl.pallas_call(pair_gather_kernel, out_shape=jax.ShapeDtypeStruct((n,) +...  26.8 us
    unnamed x14, other arithmetic  15.6 us
    pallas_call x1, Pallas kernels, allreduce_all(): pl.pallas_call(functools.partial(allreduce_kernel, n_site, n_branch), out...  15.2 us
    dot_general x1, matrix products, body(): jnp.einsum('bis,bjs->bij', part_above, part_below, precision=lax.Precisio...  11.7 us
    all_gather x1, blocking collectives, body(): top_all = lax.all_gather(top_pack, 'branch', axis=0, tiled=False)  10.2 us
    dot_general x35, matrix products, product(): return jnp.einsum('bij,bjk->bik', left, right, precision=lax.Precision.HIGH)  9.43 us
    slice x8, local copies, waits for them, and re-layouts, down_pass(): down_part = carried(probs[offset:offset + amount], current)  7.58 us

commit v1 on v0

--- a/solution.py
+++ b/solution.py
@@ -325,27 +325,7 @@
 
     lax.fori_loop(0, chips, first_send, 0)
 
-    def first_recv(m, carry):
-        to_partner(m).wait_recv()
-        return carry
-
-    lax.fori_loop(0, chips, first_recv, 0)
-
-    def first_sent(m, carry):
-        to_partner(m).wait_send()
-        return carry
-
-    lax.fori_loop(0, chips, first_sent, 0)
-
-    def add_pair(m, carry):
-        pair_sum[m] = x_ref[2 * m + core] + pair_buf[m]
-        return carry
-
-    lax.fori_loop(0, chips, add_pair, 0)
-    held[chip] = pair_sum[chip]
-
-    def to_chip(d):
-        c = lax.rem(chip + d, chips)
+    def to_chip(c):
         return pltpu.make_async_remote_copy(
             src_ref=pair_sum.at[c],
             dst_ref=held.at[chip],
@@ -355,11 +335,18 @@
             device_id_type=MESH_ID,
         )
 
-    def second_send(d, carry):
-        to_chip(d).start()
-        return carry
-
-    lax.fori_loop(1, chips, second_send, 0)
+    to_partner(chip).wait_recv()
+    pair_sum[chip] = x_ref[2 * chip + core] + pair_buf[chip]
+    held[chip] = pair_sum[chip]
+
+    def add_and_send(d, carry):
+        c = lax.rem(chip + d, chips)
+        to_partner(c).wait_recv()
+        pair_sum[c] = x_ref[2 * c + core] + pair_buf[c]
+        to_chip(c).start()
+        return carry
+
+    lax.fori_loop(1, chips, add_and_send, 0)
 
     def second_recv(d, carry):
         c = lax.rem(chip + chips - d, chips)
@@ -375,8 +362,14 @@
 
     lax.fori_loop(1, chips, second_recv, 0)
 
+    def first_sent(m, carry):
+        to_partner(m).wait_send()
+        return carry
+
+    lax.fori_loop(0, chips, first_sent, 0)
+
     def second_sent(d, carry):
-        to_chip(d).wait_send()
+        to_chip(lax.rem(chip + d, chips)).wait_send()
         return carry
 
     lax.fori_loop(1, chips, second_sent, 0)
@@ -441,22 +434,7 @@
 
     lax.fori_loop(1, chips, first_send, 0)
 
-    def first_recv(d, carry):
-        c = lax.rem(chip + chips - d, chips)
-        pltpu.make_async_remote_copy(
-            src_ref=held.at[2 * c + core],
-            dst_ref=held.at[2 * c + core],
-            send_sem=sems_a.at[c],
-            recv_sem=sems_b.at[c],
-            device_id=(2 * c + core, k),
-            device_id_type=MESH_ID,
-        ).wait_recv()
-        return carry
-
-    lax.fori_loop(1, chips, first_recv, 0)
-
-    def to_partner(d):
-        c = lax.rem(chip + d, chips)
+    def to_partner(c):
         return pltpu.make_async_remote_copy(
             src_ref=held.at[2 * c + core],
             dst_ref=held.at[2 * c + core],
@@ -476,11 +454,20 @@
     )
     own.start()
 
-    def second_send(d, carry):
-        to_partner(d).start()
-        return carry
-
-    lax.fori_loop(1, chips, second_send, 0)
+    def relay(d, carry):
+        c = lax.rem(chip + chips - d, chips)
+        pltpu.make_async_remote_copy(
+            src_ref=held.at[2 * c + core],
+            dst_ref=held.at[2 * c + core],
+            send_sem=sems_a.at[c],
+            recv_sem=sems_b.at[c],
+            device_id=(2 * c + core, k),
+            device_id_type=MESH_ID,
+        ).wait_recv()
+        to_partner(c).start()
+        return carry
+
+    lax.fori_loop(1, chips, relay, 0)
 
     def second_recv(c, carry):
         pltpu.make_async_remote_copy(
@@ -503,7 +490,7 @@
     own.wait_send()
 
     def second_sent(d, carry):
-        to_partner(d).wait_send()
+        to_partner(lax.rem(chip + d, chips)).wait_send()
         return carry
 
     lax.fori_loop(1, chips, second_sent, 0)

time: 208 us -> 205 us (0.986)
  Pallas kernels: 70 us -> 66.5 us
    pallas_call x1, Pallas kernels: 28 us -> 24.6 us  [pair_scatter(): pl.pallas_call(pair_scatter_kernel, out_shape=jax.ShapeDtypeStruct(chunk,...]
where the time goes in v1:
time: 205 us; the launch traced here: 202 us
  Pallas kernels  66.5 us (32%)
  other arithmetic  48.4 us (24%)
  matrix products  37.7 us (18%)
  local copies, waits for them, and re-layouts  34.5 us (17%)
  blocking collectives  10.1 us (5%)
  between operations  4.57 us (2%)
    pallas_call x1, Pallas kernels, pair_gather(): pl.pallas_call(pair_gather_kernel, out_shape=jax.ShapeDtypeStruct((n,) +...  25.9 us
    pallas_call x1, Pallas kernels, pair_scatter(): pl.pallas_call(pair_scatter_kernel, out_shape=jax.ShapeDtypeStruct(chunk,...  24.6 us
    pallas_call x1, Pallas kernels, allreduce_all(): pl.pallas_call(functools.partial(allreduce_kernel, n_site, n_branch), out...  16 us
    unnamed x14, other arithmetic  15.6 us
    dot_general x1, matrix products, body(): jnp.einsum('bis,bjs->bij', part_above, part_below, precision=lax.Precisio...  11.7 us
    all_gather x1, blocking collectives, body(): top_all = lax.all_gather(top_pack, 'branch', axis=0, tiled=False)  10.1 us
    dot_general x35, matrix products, product(): return jnp.einsum('bij,bjk->bik', left, right, precision=lax.Precision.HIGH)  9.43 us
    slice x8, local copies, waits for them, and re-layouts, down_pass(): down_part = carried(probs[offset:offset + amount], current)  7.58 us

profile of v1, /device:TPU:1, one launch (start us, length us, event | category | flops | bytes accessed | tf_op | source)
XLA Modules:
  0.0 201.9 jit_solution(13312023046301621644)
XLA Ops:
  4.2 1.2 convert_element_type.44
  5.4 1.3 fusion.78
  8.1 0.8 copy.140
  8.9 0.8 fusion.63
  9.7 1.0 fusion.29
  12.7 1.6 gather_fusion
  14.4 2.2 %fusion.27 = f32[128,64,64]{0,2,1:T(8,128)S(1)} fusion(f32[8]{0:T(128)S(1)} %multiply_reduce_fusion.10, f32[64,64]{1,0:T(8,128)S(1)} %fusion.64, f32[8,64]{0,1:T(8,128)S(1)} %fusion.29, f32[64,64]{1,0:T(8,128)} %constant.112, f32[8]{0:T(128)S(1)} %broadcast_add_fusion, f32[64,64]{1,0:T(8,128)} %constant.111, f32[64,64]{1,0:T(8,128)S(1)} %fusion.63, ...), kind=kOutput, calls=%fused_computation.95 | convolution fusion | flops 25396224 | bytes 2165312 | tf_op jit(solution)/shard_map/bc,cij->bij/dot_general | solution.py:532
  23.7 25.9 %shard_map.174 = f32[32,128,128]{2,1,0:T(8,128)} custom-call(f32[128,128]{1,0:T(8,128)} %reshape.322.x_ref), custom_call_target="tpu_custom_call" | custom-call | tf_op jit(solution)/shard_map/pallas_call | solution.py:501
  49.6 0.9 slice.149
  51.3 0.9 slice.147
  52.2 0.8 slice.148
  53.0 1.0 slice.145
  54.0 0.9 slice.146
  55.0 1.1 slice.143
  56.0 1.2 slice.144
  57.6 3.1 %fusion.7 = f32[64,64,256]{2,1,0:T(8,128)S(1)} fusion(f32[64,64,64]{2,1,0:T(8,128)S(1)} %slice.154, s32[64,256]{1,0:T(8,128)} %broadcast_select_fusion, pred[64,256]{1,0:T(8,128)(4,1)S(1)} %select_compare_fusion), kind=kOutput, calls=%fused_computation.13 | convolution fusion | flops 405798912 | bytes 5324800 | tf_op jit(solution)/shard_map/bij,bjs->bis/dot_general | solution.py:62
  61.2 0.9 log_reduce_fusion
  62.2 1.1 fusion.24
  68.1 4.3 %reshape.323 = f32[128,64,64]{2,1,0:T(8,128)} reshape(f32[32,128,128]{2,1,0:T(8,128)} %shard_map.174) | data formatting | bytes 4194304 | tf_op jit(solution)/shard_map/reshape | solution.py:540
  72.4 1.0 fusion.61
  74.2 0.9 fusion.54
  75.2 10.1 %all-gather.1 = f32[4,65,256]{2,1,0:T(8,128)S(1)} all-gather(f32[1,65,256]{2,1,0:T(8,128)S(1)} %maximum_bitcast_fusion.2), channel_id=2, replica_groups=mesh['site'=32,'branch'=4] {'branch'}, dimensions={0}, use_global_device_ids=true | all-gather | bytes 332800 | tf_op jit(solution)/shard_map/all_gather | solution.py:547
  87.4 1.9 multiply_reduce_fusion.11
  89.9 1.2 fusion.79
  91.1 0.9 fusion.50
  92.0 1.1 fusion.44
  93.4 0.9 multiply_reduce_fusion.9
  95.9 1.2 fusion.84
  100.4 1.0 fusion.12
  103.1 1.1 fusion.87
  104.2 1.9 fusion.11
  106.1 2.7 %fusion.6 = f32[128,64,256]{2,1,0:T(8,128)} fusion(s32[64,256]{1,0:T(8,128)S(1)} %copy-done.38, pred[64,256]{1,0:T(8,128)(4,1)S(1)} %select_compare_fusion), kind=kLoop, calls=%fused_computation.12 | loop fusion | flops 3145727 | bytes 4276224
  108.8 2.4 %multiply_bitcast_fusion.1 = (f32[32,1,64,256]{3,2,0,1:T(8,128)S(1)}, f32[32,1,64,256]{3,2,0,1:T(8,128)S(1)}, f32[128,64,256]{2,1,0:T(8,128)}) fusion(f32[32,64,256]{2,1,0:T(8,128)S(1)} %fusion.11, f32[64,64,256]{2,1,0:T(8,128)S(1)} %copy-done.3, f32[128,64,256]{2,1,0:T(8,128)} %fusion.6, f32[32,256]{1,0:T(8,128)S(1)} %copy-done.44), kind=kLoop, calls=%fused_computation.19 | loop fusion | flops 2097152 | bytes 12615680 | tf_op jit(solution)/shard_map/stack | solution.py:119
  111.8 1.4 fusion.5
  113.2 3.4 %constant_dynamic-update-slice_fusion.1 = f32[128,64,256]{2,1,0:T(8,128)} fusion(f32[64,256]{1,0:T(8,128)S(1)} %multiply_divide_fusion, f32[32,2,64,256]{3,2,1,0:T(8,128)S(1)} %copy.152), kind=kLoop, calls=%fused_computation.166 | loop fusion | flops 1048575 | bytes 8454144
  116.7 1.5 multiply_dynamic-update-slice_fusion
  118.2 1.1 multiply_dynamic-update-slice_fusion.1
  119.3 0.8 multiply_dynamic-update-slice_fusion.2
  122.1 1.2 fusion.25
  123.3 0.9 fusion.30
  126.9 11.7 %fusion.88 = f32[128,64,64]{2,1,0:T(8,128)} fusion(f32[128,64,256]{2,1,0:T(8,128)} %get-tuple-element.43, f32[128,64,256]{2,1,0:T(8,128)} %get-tuple-element.44), kind=kOutput, calls=%fused_computation.232 | convolution fusion | flops 805306368 | bytes 18874368 | tf_op jit(solution)/shard_map/bis,bjs->bij/dot_general | solution.py:560
  138.6 4.7 %reshape.333.x_ref = f32[32,128,128]{2,1,0:T(8,128)} reshape(f32[128,64,64]{2,1,0:T(8,128)} %fusion.88) | data formatting | bytes 4194304 | tf_op jit(solution)/shard_map/reshape | solution.py:561
  143.3 24.6 %shard_map.175 = f32[128,128]{1,0:T(8,128)} custom-call(f32[32,128,128]{2,1,0:T(8,128)} %reshape.333.x_ref), custom_call_target="tpu_custom_call" | custom-call | tf_op jit(solution)/shard_map/pallas_call | solution.py:382
  167.9 1.0 reshape.334
  176.3 1.2 multiply_reduce_fusion.5
  178.9 16.0 %shard_map.176 = f32[40,128]{1,0:T(8,128)} custom-call(f32[40,128]{1,0:T(8,128)} %pad_bitcast_fusion.x_ref), custom_call_target="tpu_custom_call" | custom-call | tf_op jit(solution)/shard_map/pallas_call | solution.py:196
  195.0 1.3 slice.192
  196.9 1.2 slice.190
  (269 shorter events, 45.7 us)
Async XLA Ops:
  0.6 10.7 %copy-start = (s32[256,256]{1,0:T(8,128)S(1)}, s32[256,256]{1,0:T(8,128)}, u32[]{:S(2)}) copy-start(s32[256,256]{1,0:T(8,128)} %param.17) | copy-start | bytes 786436
  1.4 16.6 %copy-start.64 = (f32[8]{0:T(128)}, f32[8]{0:T(128)S(1)}, u32[]{:S(2)}) copy-start(f32[8]{0:T(128)S(1)} %broadcast_add_fusion) | copy-start | bytes 100
  3.4 16.5 %copy-start.51 = (f32[4]{0:T(128)}, f32[4]{0:T(128)S(1)}, u32[]{:S(2)}) copy-start(f32[4]{0:T(128)S(1)} %get-tuple-element.10) | copy-start | bytes 52
  8.1 11.9 %copy-start.8 = (f32[64,64]{1,0:T(8,128)}, f32[64,64]{1,0:T(8,128)S(1)}, u32[]{:S(2)}) copy-start(f32[64,64]{1,0:T(8,128)S(1)} %fusion.64) | copy-start | bytes 49156
  9.7 6.9 %copy-start.40 = (f32[64,64]{1,0:T(8,128)}, f32[64,64]{1,0:T(8,128)S(1)}, u32[]{:S(2)}) copy-start(f32[64,64]{1,0:T(8,128)S(1)} %fusion.63) | copy-start | bytes 49156
  10.7 5.9 %copy-start.45 = (f32[8,64]{0,1:T(8,128)}, f32[8,64]{0,1:T(8,128)S(1)}, u32[]{:S(2)}) copy-start(f32[8,64]{0,1:T(8,128)S(1)} %fusion.29) | copy-start | bytes 6148
  10.8 7.2 %copy-start.66 = (f32[8]{0:T(128)}, f32[8]{0:T(128)S(1)}, u32[]{:S(2)}) copy-start(f32[8]{0:T(128)S(1)} %multiply_reduce_fusion.10) | copy-start | bytes 100
  18.8 35.2 %copy-start.28 = (f32[4,64,64]{2,1,0:T(8,128)}, f32[4,64,64]{2,1,0:T(8,128)S(1)}, u32[]{:S(2)}) copy-start(f32[4,64,64]{2,1,0:T(8,128)S(1)} %fusion.20) | copy-start | bytes 196612
  19.1 34.9 %copy-start.30 = (f32[4,64,64]{2,1,0:T(8,128)}, f32[4,64,64]{2,1,0:T(8,128)S(1)}, u32[]{:S(2)}) copy-start(f32[4,64,64]{2,1,0:T(8,128)S(1)} %fusion.19) | copy-start | bytes 196612
  19.4 34.6 %copy-start.32 = (f32[4,64,64]{2,1,0:T(8,128)}, f32[4,64,64]{2,1,0:T(8,128)S(1)}, u32[]{:S(2)}) copy-start(f32[4,64,64]{2,1,0:T(8,128)S(1)} %fusion.18) | copy-start | bytes 196612
  19.7 34.4 %copy-start.34 = (f32[4,64,64]{2,1,0:T(8,128)}, f32[4,64,64]{2,1,0:T(8,128)S(1)}, u32[]{:S(2)}) copy-start(f32[4,64,64]{2,1,0:T(8,128)S(1)} %fusion.17) | copy-start | bytes 196612
  21.7 35.5 %copy-start.10 = (f32[4,64,64]{2,1,0:T(8,128)}, f32[4,64,64]{2,1,0:T(8,128)S(1)}, u32[]{:S(2)}) copy-start(f32[4,64,64]{2,1,0:T(8,128)S(1)} %fusion.80) | copy-start | bytes 196612
  21.9 35.3 %copy-start.12 = (f32[4,64,64]{2,1,0:T(8,128)}, f32[4,64,64]{2,1,0:T(8,128)S(1)}, u32[]{:S(2)}) copy-start(f32[4,64,64]{2,1,0:T(8,128)S(1)} %fusion.81) | copy-start | bytes 196612
  49.6 7.7 %slice-start = ((f32[32,128,128]{2,1,0:T(8,128)}), f32[16,128,128]{2,1,0:T(8,128)S(1)}, s32[]{:S(2)}) async-start(f32[32,128,128]{2,1,0:T(8,128)} %shard_map.174), calls=%async_computation | async-start | bytes 2097152 | tf_op jit(solution)/shard_map/slice | solution.py:83
  57.6 4.6 %copy-start.6 = (f32[32,64,64]{2,1,0:T(8,128)S(1)}, f32[32,64,64]{2,1,0:T(8,128)}, u32[]{:S(2)}) copy-start(f32[32,64,64]{2,1,0:T(8,128)} %slice.144) | copy-start | bytes 1572868
  89.9 7.4 %copy-start.5 = (f32[8,64,256]{2,1,0:T(8,128)S(1)}, f32[8,64,256]{2,1,0:T(8,128)}, u32[]{:S(2)}) copy-start(f32[8,64,256]{2,1,0:T(8,128)} %copy-done.4) | copy-start | bytes 1572868
  104.2 4.6 %copy-start.3 = (f32[64,64,256]{2,1,0:T(8,128)S(1)}, f32[64,64,256]{2,1,0:T(8,128)}, u32[]{:S(2)}) copy-start(f32[64,64,256]{2,1,0:T(8,128)} %copy-done.2) | copy-start | bytes 12582916
  116.7 4.8 %copy-start.39 = (f32[1,64,256]{2,1,0:T(8,128)S(1)}, f32[1,64,256]{2,1,0:T(8,128)}, u32[]{:S(2)}) copy-start(f32[1,64,256]{2,1,0:T(8,128)} %get-tuple-element.12) | copy-start | bytes 196612
  116.7 4.8 %copy-start.68 = (f32[256]{0:T(256)S(1)}, f32[256]{0:T(256)}, u32[]{:S(2)}) copy-start(f32[256]{0:T(256)} %get-tuple-element.39) | copy-start | bytes 3076
  116.7 5.5 %copy-start.50 = (f32[16,256]{1,0:T(8,128)S(1)}, f32[16,256]{1,0:T(8,128)}, u32[]{:S(2)}) copy-start(f32[16,256]{1,0:T(8,128)} %copy-done.49) | copy-start | bytes 49156
  118.2 5.1 %copy-start.54 = (f32[8,256]{1,0:T(8,128)S(1)}, f32[8,256]{1,0:T(8,128)}, u32[]{:S(2)}) copy-start(f32[8,256]{1,0:T(8,128)} %copy-done.53) | copy-start | bytes 24580
  118.2 6.0 %copy-start.57 = (f32[4,256]{1,0:T(4,128)S(1)}, f32[4,256]{1,0:T(4,128)}, u32[]{:S(2)}) copy-start(f32[4,256]{1,0:T(4,128)} %copy-done.56) | copy-start | bytes 12292
  119.3 5.6 %copy-start.61 = (f32[2,256]{1,0:T(2,128)S(1)}, f32[2,256]{1,0:T(2,128)}, u32[]{:S(2)}) copy-start(f32[2,256]{1,0:T(2,128)} %copy-done.60) | copy-start | bytes 6148
  119.3 6.3 %copy-start.21 = (f32[2,64,256]{2,1,0:T(8,128)S(1)}, f32[2,64,256]{2,1,0:T(8,128)}, u32[]{:S(2)}) copy-start(f32[2,64,256]{2,1,0:T(8,128)} %copy-done.20) | copy-start | bytes 393220
  119.3 6.3 %copy-start.63 = (f32[256]{0:T(256)S(1)}, f32[256]{0:T(256)}, u32[]{:S(2)}) copy-start(f32[256]{0:T(256)} %copy-done.62) | copy-start | bytes 3076
  138.5 30.4 %copy-start.15 = (f32[4,64,64]{2,1,0:T(8,128)S(1)}, f32[4,64,64]{2,1,0:T(8,128)}, u32[]{:S(2)}) copy-start(f32[4,64,64]{2,1,0:T(8,128)} %copy-done.14) | copy-start | bytes 196612
  138.5 30.9 %copy-start.13 = (f32[4,64,64]{2,1,0:T(8,128)S(1)}, f32[4,64,64]{2,1,0:T(8,128)}, u32[]{:S(2)}) copy-start(f32[4,64,64]{2,1,0:T(8,128)} %copy-done.12) | copy-start | bytes 196612
  138.5 31.5 %copy-start.11 = (f32[4,64,64]{2,1,0:T(8,128)S(1)}, f32[4,64,64]{2,1,0:T(8,128)}, u32[]{:S(2)}) copy-start(f32[4,64,64]{2,1,0:T(8,128)} %copy-done.10) | copy-start | bytes 196612
  138.5 32.1 %copy-start.17 = (f32[4,64,64]{2,1,0:T(8,128)S(1)}, f32[4,64,64]{2,1,0:T(8,128)}, u32[]{:S(2)}) copy-start(f32[4,64,64]{2,1,0:T(8,128)} %copy-done.16) | copy-start | bytes 196612
  143.3 27.9 %copy-start.23 = (f32[4,64,64]{2,1,0:T(8,128)S(1)}, f32[4,64,64]{2,1,0:T(8,128)}, u32[]{:S(2)}) copy-start(f32[4,64,64]{2,1,0:T(8,128)} %copy-done.22) | copy-start | bytes 196612
  143.3 28.2 %copy-start.52 = (f32[4]{0:T(128)S(1)}, f32[4]{0:T(128)}, u32[]{:S(2)}) copy-start(f32[4]{0:T(128)} %copy-done.51) | copy-start | bytes 52
  143.3 28.5 %copy-start.35 = (f32[4,64,64]{2,1,0:T(8,128)S(1)}, f32[4,64,64]{2,1,0:T(8,128)}, u32[]{:S(2)}) copy-start(f32[4,64,64]{2,1,0:T(8,128)} %copy-done.34) | copy-start | bytes 196612
  143.3 29.2 %copy-start.33 = (f32[4,64,64]{2,1,0:T(8,128)S(1)}, f32[4,64,64]{2,1,0:T(8,128)}, u32[]{:S(2)}) copy-start(f32[4,64,64]{2,1,0:T(8,128)} %copy-done.32) | copy-start | bytes 196612
  143.3 29.8 %copy-start.31 = (f32[4,64,64]{2,1,0:T(8,128)S(1)}, f32[4,64,64]{2,1,0:T(8,128)}, u32[]{:S(2)}) copy-start(f32[4,64,64]{2,1,0:T(8,128)} %copy-done.30) | copy-start | bytes 196612
  167.9 5.8 %copy-start.29 = (f32[4,64,64]{2,1,0:T(8,128)S(1)}, f32[4,64,64]{2,1,0:T(8,128)}, u32[]{:S(2)}) copy-start(f32[4,64,64]{2,1,0:T(8,128)} %copy-done.28) | copy-start | bytes 196612
  167.9 6.4 %copy-start.27 = (f32[4,64,64]{2,1,0:T(8,128)S(1)}, f32[4,64,64]{2,1,0:T(8,128)}, u32[]{:S(2)}) copy-start(f32[4,64,64]{2,1,0:T(8,128)} %copy-done.26) | copy-start | bytes 196612
  169.5 5.5 %copy-start.25 = (f32[4,64,64]{2,1,0:T(8,128)S(1)}, f32[4,64,64]{2,1,0:T(8,128)}, u32[]{:S(2)}) copy-start(f32[4,64,64]{2,1,0:T(8,128)} %copy-done.24) | copy-start | bytes 196612
  170.0 5.5 %copy-start.9 = (f32[64,64]{1,0:T(8,128)S(1)}, f32[64,64]{1,0:T(8,128)}, u32[]{:S(2)}) copy-start(f32[64,64]{1,0:T(8,128)} %copy-done.8) | copy-start | bytes 49156
  170.0 5.5 %copy-start.69 = (f32[4]{0:T(128)S(1)}, f32[4]{0:T(128)}, u32[]{:S(2)}) copy-start(f32[4]{0:T(128)} %get-tuple-element.9) | copy-start | bytes 52
  170.3 5.9 %copy-start.41 = (f32[64,64]{1,0:T(8,128)S(1)}, f32[64,64]{1,0:T(8,128)}, u32[]{:S(2)}) copy-start(f32[64,64]{1,0:T(8,128)} %copy-done.40) | copy-start | bytes 49156
  170.3 5.9 %copy-start.46 = (f32[8,64]{0,1:T(8,128)S(1)}, f32[8,64]{0,1:T(8,128)}, u32[]{:S(2)}) copy-start(f32[8,64]{0,1:T(8,128)} %copy-done.45) | copy-start | bytes 6148
  170.3 5.9 %copy-start.47 = (f32[64,64]{1,0:T(8,128)S(1)}, f32[64,64]{1,0:T(8,128)}, u32[]{:S(2)}) copy-start(f32[64,64]{1,0:T(8,128)} %constant.112) | copy-start | bytes 49156
  170.4 5.9 %copy-start.48 = (f32[64,64]{1,0:T(8,128)S(1)}, f32[64,64]{1,0:T(8,128)}, u32[]{:S(2)}) copy-start(f32[64,64]{1,0:T(8,128)} %constant.111) | copy-start | bytes 49156
  170.4 5.9 %copy-start.65 = (f32[8]{0:T(128)S(1)}, f32[8]{0:T(128)}, u32[]{:S(2)}) copy-start(f32[8]{0:T(128)} %copy-done.64) | copy-start | bytes 100
  170.4 5.9 %copy-start.67 = (f32[8]{0:T(128)S(1)}, f32[8]{0:T(128)}, u32[]{:S(2)}) copy-start(f32[8]{0:T(128)} %copy-done.66) | copy-start | bytes 100
  170.4 5.9 %copy-start.70 = (f32[8]{0:T(128)S(1)}, f32[8]{0:T(128)}, u32[]{:S(2)}) copy-start(f32[8]{0:T(128)} %multiply_divide_fusion.7) | copy-start | bytes 100
  171.4 6.1 %copy-start.59 = (f32[64]{0:T(128)S(1)}, f32[64]{0:T(128)}, u32[]{:S(2)}) copy-start(f32[64]{0:T(128)} %copy-done.58) | copy-start | bytes 772
  171.8 28.9 %copy-start.1 = (s32[256,256]{1,0:T(8,128)S(1)}, s32[256,256]{1,0:T(8,128)}, u32[]{:S(2)}) copy-start(s32[256,256]{1,0:T(8,128)} %param.17) | copy-start | bytes 786436
  (24 other events, 44.8 us)

commit v2 on v1

--- a/solution.py
+++ b/solution.py
@@ -544,7 +544,7 @@
     )
     levels, messages, logscale = up_pass(probs, leaves)
     top_pack = jnp.concatenate([messages[-1][0], logscale[None, :]], axis=0)
-    top_all = lax.all_gather(top_pack, "branch", axis=0, tiled=False)
+    top_all = exchange(top_pack, "branch", lax.axis_size("branch"), True, 3)
     top_messages, top_logs = top_all[:, :64, :], top_all[:, 64, :]
     site_ll, above_all = root_terms(stationary, top_messages, top_logs)
     site_weight = weights.astype(jnp.float32)

time: 205 us -> 207 us (level)
  blocking collectives: 10.1 us -> 0 us
  Pallas kernels: 66.5 us -> 76.1 us
  other arithmetic: 48.4 us -> 51.1 us
    all_gather x1 -> x0, blocking collectives: 10.1 us -> none  [body(): top_all = lax.all_gather(top_pack, 'branch', axis=0, tiled=False)]
    pallas_call x0 -> x1, Pallas kernels: none -> 9.42 us  [exchange(): pl.pallas_call(functools.partial(exchange_kernel, axis, gather), out_shap...]
    unnamed x144 -> x146, local copies, waits for them, and re-layouts: 5.47 us -> 6.09 us
    unnamed x14 -> x13, other arithmetic: 15.6 us -> 15.3 us
where the time goes in v2:
time: 207 us; the launch traced here: 205 us
  Pallas kernels  76.1 us (37%)
  other arithmetic  51.1 us (25%)
  matrix products  37.7 us (18%)
  local copies, waits for them, and re-layouts  35.1 us (17%)
  between operations  4.57 us (2%)
    pallas_call x1, Pallas kernels, pair_gather(): pl.pallas_call(pair_gather_kernel, out_shape=jax.ShapeDtypeStruct((n,) +...  25.9 us
    pallas_call x1, Pallas kernels, pair_scatter(): pl.pallas_call(pair_scatter_kernel, out_shape=jax.ShapeDtypeStruct(chunk,...  24.9 us
    pallas_call x1, Pallas kernels, allreduce_all(): pl.pallas_call(functools.partial(allreduce_kernel, n_site, n_branch), out...  15.9 us
    unnamed x13, other arithmetic  15.3 us
    dot_general x1, matrix products, body(): jnp.einsum('bis,bjs->bij', part_above, part_below, precision=lax.Precisio...  11.7 us
    dot_general x35, matrix products, product(): return jnp.einsum('bij,bjk->bik', left, right, precision=lax.Precision.HIGH)  9.43 us
    pallas_call x1, Pallas kernels, exchange(): pl.pallas_call(functools.partial(exchange_kernel, axis, gather), out_shap...  9.42 us
    slice x8, local copies, waits for them, and re-layouts, down_pass(): down_part = carried(probs[offset:offset + amount], current)  7.58 us

profile of v2, /device:TPU:1, one launch (start us, length us, event | category | flops | bytes accessed | tf_op | source)
XLA Modules:
  0.0 204.6 jit_solution(18116565453916913167)
XLA Ops:
  4.2 1.2 convert_element_type.44
  5.4 1.3 fusion.77
  8.1 0.8 copy.99
  9.7 1.0 fusion.29
  12.7 1.6 gather_fusion
  14.4 2.2 %fusion.27 = f32[128,64,64]{0,2,1:T(8,128)S(1)} fusion(f32[8]{0:T(128)S(1)} %multiply_reduce_fusion.10, f32[64,64]{1,0:T(8,128)S(1)} %fusion.63, f32[8,64]{0,1:T(8,128)S(1)} %fusion.29, f32[64,64]{1,0:T(8,128)} %constant.112, f32[8]{0:T(128)S(1)} %broadcast_add_fusion, f32[64,64]{1,0:T(8,128)} %constant.111, f32[64,64]{1,0:T(8,128)S(1)} %fusion.62, ...), kind=kOutput, calls=%fused_computation.95 | convolution fusion | flops 25396224 | bytes 2165312 | tf_op jit(solution)/shard_map/bc,cij->bij/dot_general | solution.py:532
  23.7 25.9 %shard_map.174 = f32[32,128,128]{2,1,0:T(8,128)} custom-call(f32[128,128]{1,0:T(8,128)} %reshape.322.x_ref), custom_call_target="tpu_custom_call" | custom-call | tf_op jit(solution)/shard_map/pallas_call | solution.py:501
  49.6 0.9 slice.149
  51.3 0.9 slice.147
  53.0 1.0 slice.145
  54.0 0.9 slice.146
  55.0 1.1 slice.143
  56.0 1.2 slice.144
  57.6 3.1 %fusion.7 = f32[64,64,256]{2,1,0:T(8,128)S(1)} fusion(f32[64,64,64]{2,1,0:T(8,128)S(1)} %slice.154, s32[64,256]{1,0:T(8,128)} %broadcast_select_fusion, pred[64,256]{1,0:T(8,128)(4,1)S(1)} %select_compare_fusion), kind=kOutput, calls=%fused_computation.13 | convolution fusion | flops 405798912 | bytes 5324800 | tf_op jit(solution)/shard_map/bij,bjs->bis/dot_general | solution.py:62
  61.2 0.9 log_reduce_fusion
  62.2 1.1 fusion.24
  68.1 4.3 %reshape.323 = f32[128,64,64]{2,1,0:T(8,128)} reshape(f32[32,128,128]{2,1,0:T(8,128)} %shard_map.174) | data formatting | bytes 4194304 | tf_op jit(solution)/shard_map/reshape | solution.py:540
  72.4 1.0 fusion.60
  74.2 0.9 fusion.54
  76.5 9.4 %shard_map.175 = f32[4,65,256]{2,1,0:T(8,128)} custom-call(f32[65,256]{1,0:T(8,128)} %pad_maximum_fusion.5.x_ref), custom_call_target="tpu_custom_call" | custom-call | tf_op jit(solution)/shard_map/pallas_call | solution.py:279
  86.7 1.0 fusion.48
  87.7 1.0 multiply_multiply_fusion.3
  88.7 1.5 fusion.49
  90.2 1.9 multiply_reduce_fusion.11
  92.7 1.2 fusion.78
  93.9 0.9 fusion.50
  94.8 1.1 fusion.44
  96.0 0.9 multiply_reduce_fusion.9
  98.5 1.2 fusion.83
  103.0 1.2 fusion.12
  105.9 1.1 fusion.86
  107.0 1.9 fusion.11
  108.9 2.7 %fusion.6 = f32[128,64,256]{2,1,0:T(8,128)} fusion(s32[64,256]{1,0:T(8,128)S(1)} %copy-done.38, pred[64,256]{1,0:T(8,128)(4,1)S(1)} %select_compare_fusion), kind=kLoop, calls=%fused_computation.12 | loop fusion | flops 3145727 | bytes 4276224
  111.6 2.4 %multiply_bitcast_fusion.1 = (f32[32,1,64,256]{3,2,0,1:T(8,128)S(1)}, f32[32,1,64,256]{3,2,0,1:T(8,128)S(1)}, f32[128,64,256]{2,1,0:T(8,128)}) fusion(f32[32,64,256]{2,1,0:T(8,128)S(1)} %fusion.11, f32[64,64,256]{2,1,0:T(8,128)S(1)} %copy-done.3, f32[128,64,256]{2,1,0:T(8,128)} %fusion.6, f32[32,256]{1,0:T(8,128)S(1)} %copy-done.44), kind=kLoop, calls=%fused_computation.19 | loop fusion | flops 2097152 | bytes 12615680 | tf_op jit(solution)/shard_map/stack | solution.py:119
  114.6 1.4 fusion.5
  116.0 3.2 %constant_dynamic-update-slice_fusion.1 = f32[128,64,256]{2,1,0:T(8,128)} fusion(f32[64,256]{1,0:T(8,128)S(1)} %multiply_divide_fusion, f32[32,2,64,256]{3,2,1,0:T(8,128)S(1)} %copy.111), kind=kLoop, calls=%fused_computation.165 | loop fusion | flops 1048575 | bytes 8454144
  119.2 1.5 multiply_dynamic-update-slice_fusion
  120.8 1.1 multiply_dynamic-update-slice_fusion.1
  124.7 1.2 fusion.25
  125.8 0.9 fusion.30
  129.4 11.7 %fusion.87 = f32[128,64,64]{2,1,0:T(8,128)} fusion(f32[128,64,256]{2,1,0:T(8,128)} %get-tuple-element.43, f32[128,64,256]{2,1,0:T(8,128)} %get-tuple-element.44), kind=kOutput, calls=%fused_computation.231 | convolution fusion | flops 805306368 | bytes 18874368 | tf_op jit(solution)/shard_map/bis,bjs->bij/dot_general | solution.py:560
  141.1 4.7 %reshape.333.x_ref = f32[32,128,128]{2,1,0:T(8,128)} reshape(f32[128,64,64]{2,1,0:T(8,128)} %fusion.87) | data formatting | bytes 4194304 | tf_op jit(solution)/shard_map/reshape | solution.py:561
  145.9 24.9 %shard_map.176 = f32[128,128]{1,0:T(8,128)} custom-call(f32[32,128,128]{2,1,0:T(8,128)} %reshape.333.x_ref), custom_call_target="tpu_custom_call" | custom-call | tf_op jit(solution)/shard_map/pallas_call | solution.py:382
  170.8 1.0 reshape.334
  179.2 1.2 multiply_reduce_fusion.5
  181.8 15.9 %shard_map.177 = f32[40,128]{1,0:T(8,128)} custom-call(f32[40,128]{1,0:T(8,128)} %pad_bitcast_fusion.x_ref), custom_call_target="tpu_custom_call" | custom-call | tf_op jit(solution)/shard_map/pallas_call | solution.py:196
  197.7 1.3 slice.187
  199.6 1.2 slice.185
  (271 shorter events, 47.9 us)
Async XLA Ops:
  0.6 10.7 %copy-start = (s32[256,256]{1,0:T(8,128)S(1)}, s32[256,256]{1,0:T(8,128)}, u32[]{:S(2)}) copy-start(s32[256,256]{1,0:T(8,128)} %param.17) | copy-start | bytes 786436
  1.4 16.6 %copy-start.65 = (f32[8]{0:T(128)}, f32[8]{0:T(128)S(1)}, u32[]{:S(2)}) copy-start(f32[8]{0:T(128)S(1)} %broadcast_add_fusion) | copy-start | bytes 100
  3.4 16.5 %copy-start.52 = (f32[4]{0:T(128)}, f32[4]{0:T(128)S(1)}, u32[]{:S(2)}) copy-start(f32[4]{0:T(128)S(1)} %get-tuple-element.10) | copy-start | bytes 52
  8.1 11.9 %copy-start.8 = (f32[64,64]{1,0:T(8,128)}, f32[64,64]{1,0:T(8,128)S(1)}, u32[]{:S(2)}) copy-start(f32[64,64]{1,0:T(8,128)S(1)} %fusion.63) | copy-start | bytes 49156
  9.7 6.9 %copy-start.40 = (f32[64,64]{1,0:T(8,128)}, f32[64,64]{1,0:T(8,128)S(1)}, u32[]{:S(2)}) copy-start(f32[64,64]{1,0:T(8,128)S(1)} %fusion.62) | copy-start | bytes 49156
  10.7 5.9 %copy-start.45 = (f32[8,64]{0,1:T(8,128)}, f32[8,64]{0,1:T(8,128)S(1)}, u32[]{:S(2)}) copy-start(f32[8,64]{0,1:T(8,128)S(1)} %fusion.29) | copy-start | bytes 6148
  10.8 7.2 %copy-start.67 = (f32[8]{0:T(128)}, f32[8]{0:T(128)S(1)}, u32[]{:S(2)}) copy-start(f32[8]{0:T(128)S(1)} %multiply_reduce_fusion.10) | copy-start | bytes 100
  18.8 35.2 %copy-start.28 = (f32[4,64,64]{2,1,0:T(8,128)}, f32[4,64,64]{2,1,0:T(8,128)S(1)}, u32[]{:S(2)}) copy-start(f32[4,64,64]{2,1,0:T(8,128)S(1)} %fusion.20) | copy-start | bytes 196612
  19.1 34.9 %copy-start.30 = (f32[4,64,64]{2,1,0:T(8,128)}, f32[4,64,64]{2,1,0:T(8,128)S(1)}, u32[]{:S(2)}) copy-start(f32[4,64,64]{2,1,0:T(8,128)S(1)} %fusion.19) | copy-start | bytes 196612
  19.4 34.6 %copy-start.32 = (f32[4,64,64]{2,1,0:T(8,128)}, f32[4,64,64]{2,1,0:T(8,128)S(1)}, u32[]{:S(2)}) copy-start(f32[4,64,64]{2,1,0:T(8,128)S(1)} %fusion.18) | copy-start | bytes 196612
  19.7 34.4 %copy-start.34 = (f32[4,64,64]{2,1,0:T(8,128)}, f32[4,64,64]{2,1,0:T(8,128)S(1)}, u32[]{:S(2)}) copy-start(f32[4,64,64]{2,1,0:T(8,128)S(1)} %fusion.17) | copy-start | bytes 196612
  21.7 35.5 %copy-start.10 = (f32[4,64,64]{2,1,0:T(8,128)}, f32[4,64,64]{2,1,0:T(8,128)S(1)}, u32[]{:S(2)}) copy-start(f32[4,64,64]{2,1,0:T(8,128)S(1)} %fusion.79) | copy-start | bytes 196612
  21.9 35.3 %copy-start.12 = (f32[4,64,64]{2,1,0:T(8,128)}, f32[4,64,64]{2,1,0:T(8,128)S(1)}, u32[]{:S(2)}) copy-start(f32[4,64,64]{2,1,0:T(8,128)S(1)} %fusion.80) | copy-start | bytes 196612
  49.6 7.7 %slice-start = ((f32[32,128,128]{2,1,0:T(8,128)}), f32[16,128,128]{2,1,0:T(8,128)S(1)}, s32[]{:S(2)}) async-start(f32[32,128,128]{2,1,0:T(8,128)} %shard_map.174), calls=%async_computation | async-start | bytes 2097152 | tf_op jit(solution)/shard_map/slice | solution.py:83
  57.6 4.6 %copy-start.6 = (f32[32,64,64]{2,1,0:T(8,128)S(1)}, f32[32,64,64]{2,1,0:T(8,128)}, u32[]{:S(2)}) copy-start(f32[32,64,64]{2,1,0:T(8,128)} %slice.144) | copy-start | bytes 1572868
  92.7 7.2 %copy-start.5 = (f32[8,64,256]{2,1,0:T(8,128)S(1)}, f32[8,64,256]{2,1,0:T(8,128)}, u32[]{:S(2)}) copy-start(f32[8,64,256]{2,1,0:T(8,128)} %copy-done.4) | copy-start | bytes 1572868
  107.0 4.6 %copy-start.3 = (f32[64,64,256]{2,1,0:T(8,128)S(1)}, f32[64,64,256]{2,1,0:T(8,128)}, u32[]{:S(2)}) copy-start(f32[64,64,256]{2,1,0:T(8,128)} %copy-done.2) | copy-start | bytes 12582916
  119.2 4.8 %copy-start.39 = (f32[1,64,256]{2,1,0:T(8,128)S(1)}, f32[1,64,256]{2,1,0:T(8,128)}, u32[]{:S(2)}) copy-start(f32[1,64,256]{2,1,0:T(8,128)} %get-tuple-element.12) | copy-start | bytes 196612
  119.2 4.8 %copy-start.69 = (f32[256]{0:T(256)S(1)}, f32[256]{0:T(256)}, u32[]{:S(2)}) copy-start(f32[256]{0:T(256)} %get-tuple-element.39) | copy-start | bytes 3076
  119.2 5.5 %copy-start.51 = (f32[16,256]{1,0:T(8,128)S(1)}, f32[16,256]{1,0:T(8,128)}, u32[]{:S(2)}) copy-start(f32[16,256]{1,0:T(8,128)} %copy-done.50) | copy-start | bytes 49156
  120.8 5.1 %copy-start.55 = (f32[8,256]{1,0:T(8,128)S(1)}, f32[8,256]{1,0:T(8,128)}, u32[]{:S(2)}) copy-start(f32[8,256]{1,0:T(8,128)} %copy-done.54) | copy-start | bytes 24580
  120.8 6.0 %copy-start.58 = (f32[4,256]{1,0:T(4,128)S(1)}, f32[4,256]{1,0:T(4,128)}, u32[]{:S(2)}) copy-start(f32[4,256]{1,0:T(4,128)} %copy-done.57) | copy-start | bytes 12292
  121.8 5.6 %copy-start.62 = (f32[2,256]{1,0:T(2,128)S(1)}, f32[2,256]{1,0:T(2,128)}, u32[]{:S(2)}) copy-start(f32[2,256]{1,0:T(2,128)} %copy-done.61) | copy-start | bytes 6148
  121.8 6.3 %copy-start.21 = (f32[2,64,256]{2,1,0:T(8,128)S(1)}, f32[2,64,256]{2,1,0:T(8,128)}, u32[]{:S(2)}) copy-start(f32[2,64,256]{2,1,0:T(8,128)} %copy-done.20) | copy-start | bytes 393220
  121.8 6.3 %copy-start.64 = (f32[256]{0:T(256)S(1)}, f32[256]{0:T(256)}, u32[]{:S(2)}) copy-start(f32[256]{0:T(256)} %copy-done.63) | copy-start | bytes 3076
  141.1 30.7 %copy-start.15 = (f32[4,64,64]{2,1,0:T(8,128)S(1)}, f32[4,64,64]{2,1,0:T(8,128)}, u32[]{:S(2)}) copy-start(f32[4,64,64]{2,1,0:T(8,128)} %copy-done.14) | copy-start | bytes 196612
  141.1 31.2 %copy-start.13 = (f32[4,64,64]{2,1,0:T(8,128)S(1)}, f32[4,64,64]{2,1,0:T(8,128)}, u32[]{:S(2)}) copy-start(f32[4,64,64]{2,1,0:T(8,128)} %copy-done.12) | copy-start | bytes 196612
  141.1 31.8 %copy-start.11 = (f32[4,64,64]{2,1,0:T(8,128)S(1)}, f32[4,64,64]{2,1,0:T(8,128)}, u32[]{:S(2)}) copy-start(f32[4,64,64]{2,1,0:T(8,128)} %copy-done.10) | copy-start | bytes 196612
  141.1 32.4 %copy-start.17 = (f32[4,64,64]{2,1,0:T(8,128)S(1)}, f32[4,64,64]{2,1,0:T(8,128)}, u32[]{:S(2)}) copy-start(f32[4,64,64]{2,1,0:T(8,128)} %copy-done.16) | copy-start | bytes 196612
  145.8 28.2 %copy-start.23 = (f32[4,64,64]{2,1,0:T(8,128)S(1)}, f32[4,64,64]{2,1,0:T(8,128)}, u32[]{:S(2)}) copy-start(f32[4,64,64]{2,1,0:T(8,128)} %copy-done.22) | copy-start | bytes 196612
  145.8 28.5 %copy-start.53 = (f32[4]{0:T(128)S(1)}, f32[4]{0:T(128)}, u32[]{:S(2)}) copy-start(f32[4]{0:T(128)} %copy-done.52) | copy-start | bytes 52
  145.8 28.9 %copy-start.35 = (f32[4,64,64]{2,1,0:T(8,128)S(1)}, f32[4,64,64]{2,1,0:T(8,128)}, u32[]{:S(2)}) copy-start(f32[4,64,64]{2,1,0:T(8,128)} %copy-done.34) | copy-start | bytes 196612
  145.8 29.5 %copy-start.33 = (f32[4,64,64]{2,1,0:T(8,128)S(1)}, f32[4,64,64]{2,1,0:T(8,128)}, u32[]{:S(2)}) copy-start(f32[4,64,64]{2,1,0:T(8,128)} %copy-done.32) | copy-start | bytes 196612
  145.8 30.1 %copy-start.31 = (f32[4,64,64]{2,1,0:T(8,128)S(1)}, f32[4,64,64]{2,1,0:T(8,128)}, u32[]{:S(2)}) copy-start(f32[4,64,64]{2,1,0:T(8,128)} %copy-done.30) | copy-start | bytes 196612
  170.8 5.8 %copy-start.29 = (f32[4,64,64]{2,1,0:T(8,128)S(1)}, f32[4,64,64]{2,1,0:T(8,128)}, u32[]{:S(2)}) copy-start(f32[4,64,64]{2,1,0:T(8,128)} %copy-done.28) | copy-start | bytes 196612
  170.8 6.4 %copy-start.27 = (f32[4,64,64]{2,1,0:T(8,128)S(1)}, f32[4,64,64]{2,1,0:T(8,128)}, u32[]{:S(2)}) copy-start(f32[4,64,64]{2,1,0:T(8,128)} %copy-done.26) | copy-start | bytes 196612
  172.3 5.5 %copy-start.25 = (f32[4,64,64]{2,1,0:T(8,128)S(1)}, f32[4,64,64]{2,1,0:T(8,128)}, u32[]{:S(2)}) copy-start(f32[4,64,64]{2,1,0:T(8,128)} %copy-done.24) | copy-start | bytes 196612
  172.9 5.6 %copy-start.9 = (f32[64,64]{1,0:T(8,128)S(1)}, f32[64,64]{1,0:T(8,128)}, u32[]{:S(2)}) copy-start(f32[64,64]{1,0:T(8,128)} %copy-done.8) | copy-start | bytes 49156
  172.9 5.5 %copy-start.70 = (f32[4]{0:T(128)S(1)}, f32[4]{0:T(128)}, u32[]{:S(2)}) copy-start(f32[4]{0:T(128)} %get-tuple-element.9) | copy-start | bytes 52
  173.2 5.9 %copy-start.41 = (f32[64,64]{1,0:T(8,128)S(1)}, f32[64,64]{1,0:T(8,128)}, u32[]{:S(2)}) copy-start(f32[64,64]{1,0:T(8,128)} %copy-done.40) | copy-start | bytes 49156
  173.2 5.9 %copy-start.46 = (f32[8,64]{0,1:T(8,128)S(1)}, f32[8,64]{0,1:T(8,128)}, u32[]{:S(2)}) copy-start(f32[8,64]{0,1:T(8,128)} %copy-done.45) | copy-start | bytes 6148
  173.2 5.9 %copy-start.47 = (f32[64,64]{1,0:T(8,128)S(1)}, f32[64,64]{1,0:T(8,128)}, u32[]{:S(2)}) copy-start(f32[64,64]{1,0:T(8,128)} %constant.112) | copy-start | bytes 49156
  173.2 5.9 %copy-start.48 = (f32[64,64]{1,0:T(8,128)S(1)}, f32[64,64]{1,0:T(8,128)}, u32[]{:S(2)}) copy-start(f32[64,64]{1,0:T(8,128)} %constant.111) | copy-start | bytes 49156
  173.2 5.9 %copy-start.66 = (f32[8]{0:T(128)S(1)}, f32[8]{0:T(128)}, u32[]{:S(2)}) copy-start(f32[8]{0:T(128)} %copy-done.65) | copy-start | bytes 100
  173.3 5.9 %copy-start.68 = (f32[8]{0:T(128)S(1)}, f32[8]{0:T(128)}, u32[]{:S(2)}) copy-start(f32[8]{0:T(128)} %copy-done.67) | copy-start | bytes 100
  173.3 5.9 %copy-start.71 = (f32[8]{0:T(128)S(1)}, f32[8]{0:T(128)}, u32[]{:S(2)}) copy-start(f32[8]{0:T(128)} %multiply_divide_fusion.7) | copy-start | bytes 100
  174.3 6.1 %copy-start.60 = (f32[64]{0:T(128)S(1)}, f32[64]{0:T(128)}, u32[]{:S(2)}) copy-start(f32[64]{0:T(128)} %copy-done.59) | copy-start | bytes 772
  174.7 28.8 %copy-start.1 = (s32[256,256]{1,0:T(8,128)S(1)}, s32[256,256]{1,0:T(8,128)}, u32[]{:S(2)}) copy-start(s32[256,256]{1,0:T(8,128)} %param.17) | copy-start | bytes 786436
  (25 other events, 44.5 us)

commit v3 on v1

--- a/solution.py
+++ b/solution.py
@@ -135,14 +135,11 @@
     s = lax.axis_index("site")
     k = lax.axis_index("branch")
     core = s % 2
-    y = (s // 2) % 4
-    z = s // 8
-    n_z = n_site // 8
+    plane = s // 2
     return [
         (2, core, lambda c: (s - core + c, k)),
         (n_branch, k, lambda c: (s, c)),
-        (4, y, lambda c: (s - 2 * y + 2 * c, k)),
-        (n_z, z, lambda c: (s - 8 * z + 8 * c, k)),
+        (n_site // 2, plane, lambda c: (2 * c + core, k)),
     ]
 
 
@@ -199,9 +196,9 @@
         in_specs=[pl.BlockSpec(memory_space=pltpu.VMEM)],
         out_specs=pl.BlockSpec(memory_space=pltpu.VMEM),
         scratch_shapes=[
-            pltpu.VMEM((4, 4, rows, 128), jnp.float32),
-            pltpu.SemaphoreType.DMA((4, 4)),
-            pltpu.SemaphoreType.DMA((4, 4)),
+            pltpu.VMEM((3, n_site // 2, rows, 128), jnp.float32),
+            pltpu.SemaphoreType.DMA((3, n_site // 2)),
+            pltpu.SemaphoreType.DMA((3, n_site // 2)),
         ],
         compiler_params=pltpu.CompilerParams(collective_id=0, has_side_effects=True),
     )(x)

time: 205 us -> 205 us (level)
  no operation moved by 1% of the time
where the time goes in v3:
time: 205 us; the launch traced here: 203 us
  Pallas kernels  67.7 us (33%)
  other arithmetic  48.4 us (24%)
  matrix products  37.7 us (18%)
  local copies, waits for them, and re-layouts  34.5 us (17%)
  blocking collectives  10.1 us (5%)
  between operations  4.57 us (2%)
    pallas_call x1, Pallas kernels, pair_gather(): pl.pallas_call(pair_gather_kernel, out_shape=jax.ShapeDtypeStruct((n,) +...  25.9 us
    pallas_call x1, Pallas kernels, pair_scatter(): pl.pallas_call(pair_scatter_kernel, out_shape=jax.ShapeDtypeStruct(chunk,...  24.6 us
    pallas_call x1, Pallas kernels, allreduce_all(): pl.pallas_call(functools.partial(allreduce_kernel, n_site, n_branch), out...  17.2 us
    unnamed x14, other arithmetic  15.6 us
    dot_general x1, matrix products, body(): jnp.einsum('bis,bjs->bij', part_above, part_below, precision=lax.Precisio...  11.7 us
    all_gather x1, blocking collectives, body(): top_all = lax.all_gather(top_pack, 'branch', axis=0, tiled=False)  10.1 us
    dot_general x35, matrix products, product(): return jnp.einsum('bij,bjk->bik', left, right, precision=lax.Precision.HIGH)  9.43 us
    slice x8, local copies, waits for them, and re-layouts, down_pass(): down_part = carried(probs[offset:offset + amount], current)  7.58 us

profile of v3, /device:TPU:1, one launch (start us, length us, event | category | flops | bytes accessed | tf_op | source)
XLA Modules:
  0.0 203.0 jit_solution(17464176784464610974)
XLA Ops:
  4.2 1.2 convert_element_type.44
  5.4 1.3 fusion.78
  8.1 0.8 copy.140
  8.9 0.8 fusion.63
  9.7 1.0 fusion.29
  12.7 1.6 gather_fusion
  14.4 2.2 %fusion.27 = f32[128,64,64]{0,2,1:T(8,128)S(1)} fusion(f32[8]{0:T(128)S(1)} %multiply_reduce_fusion.10, f32[64,64]{1,0:T(8,128)S(1)} %fusion.64, f32[8,64]{0,1:T(8,128)S(1)} %fusion.29, f32[64,64]{1,0:T(8,128)} %constant.112, f32[8]{0:T(128)S(1)} %broadcast_add_fusion, f32[64,64]{1,0:T(8,128)} %constant.111, f32[64,64]{1,0:T(8,128)S(1)} %fusion.63, ...), kind=kOutput, calls=%fused_computation.95 | convolution fusion | flops 25396224 | bytes 2165312 | tf_op jit(solution)/shard_map/bc,cij->bij/dot_general | solution.py:529
  23.7 25.9 %shard_map.174 = f32[32,128,128]{2,1,0:T(8,128)} custom-call(f32[128,128]{1,0:T(8,128)} %reshape.322.x_ref), custom_call_target="tpu_custom_call" | custom-call | tf_op jit(solution)/shard_map/pallas_call | solution.py:498
  49.6 0.9 slice.149
  51.3 0.9 slice.147
  52.2 0.8 slice.148
  53.0 1.0 slice.145
  54.0 0.9 slice.146
  55.0 1.1 slice.143
  56.0 1.2 slice.144
  57.6 3.1 %fusion.7 = f32[64,64,256]{2,1,0:T(8,128)S(1)} fusion(f32[64,64,64]{2,1,0:T(8,128)S(1)} %slice.154, s32[64,256]{1,0:T(8,128)} %broadcast_select_fusion, pred[64,256]{1,0:T(8,128)(4,1)S(1)} %select_compare_fusion), kind=kOutput, calls=%fused_computation.13 | convolution fusion | flops 405798912 | bytes 5324800 | tf_op jit(solution)/shard_map/bij,bjs->bis/dot_general | solution.py:62
  61.2 0.9 log_reduce_fusion
  62.2 1.1 fusion.24
  68.1 4.3 %reshape.323 = f32[128,64,64]{2,1,0:T(8,128)} reshape(f32[32,128,128]{2,1,0:T(8,128)} %shard_map.174) | data formatting | bytes 4194304 | tf_op jit(solution)/shard_map/reshape | solution.py:537
  72.4 1.0 fusion.61
  74.2 0.9 fusion.54
  75.2 10.1 %all-gather.1 = f32[4,65,256]{2,1,0:T(8,128)S(1)} all-gather(f32[1,65,256]{2,1,0:T(8,128)S(1)} %maximum_bitcast_fusion.2), channel_id=2, replica_groups=mesh['site'=32,'branch'=4] {'branch'}, dimensions={0}, use_global_device_ids=true | all-gather | bytes 332800 | tf_op jit(solution)/shard_map/all_gather | solution.py:544
  87.4 1.9 multiply_reduce_fusion.11
  89.9 1.2 fusion.79
  91.1 0.9 fusion.50
  92.0 1.1 fusion.44
  93.4 0.9 multiply_reduce_fusion.9
  95.9 1.2 fusion.84
  100.4 1.0 fusion.12
  103.1 1.1 fusion.87
  104.2 1.9 fusion.11
  106.1 2.7 %fusion.6 = f32[128,64,256]{2,1,0:T(8,128)} fusion(s32[64,256]{1,0:T(8,128)S(1)} %copy-done.38, pred[64,256]{1,0:T(8,128)(4,1)S(1)} %select_compare_fusion), kind=kLoop, calls=%fused_computation.12 | loop fusion | flops 3145727 | bytes 4276224
  108.8 2.4 %multiply_bitcast_fusion.1 = (f32[32,1,64,256]{3,2,0,1:T(8,128)S(1)}, f32[32,1,64,256]{3,2,0,1:T(8,128)S(1)}, f32[128,64,256]{2,1,0:T(8,128)}) fusion(f32[32,64,256]{2,1,0:T(8,128)S(1)} %fusion.11, f32[64,64,256]{2,1,0:T(8,128)S(1)} %copy-done.3, f32[128,64,256]{2,1,0:T(8,128)} %fusion.6, f32[32,256]{1,0:T(8,128)S(1)} %copy-done.44), kind=kLoop, calls=%fused_computation.19 | loop fusion | flops 2097152 | bytes 12615680 | tf_op jit(solution)/shard_map/stack | solution.py:119
  111.8 1.4 fusion.5
  113.2 3.4 %constant_dynamic-update-slice_fusion.1 = f32[128,64,256]{2,1,0:T(8,128)} fusion(f32[64,256]{1,0:T(8,128)S(1)} %multiply_divide_fusion, f32[32,2,64,256]{3,2,1,0:T(8,128)S(1)} %copy.152), kind=kLoop, calls=%fused_computation.166 | loop fusion | flops 1048575 | bytes 8454144
  116.7 1.5 multiply_dynamic-update-slice_fusion
  118.2 1.1 multiply_dynamic-update-slice_fusion.1
  119.3 0.8 multiply_dynamic-update-slice_fusion.2
  122.1 1.2 fusion.25
  123.3 0.9 fusion.30
  126.9 11.7 %fusion.88 = f32[128,64,64]{2,1,0:T(8,128)} fusion(f32[128,64,256]{2,1,0:T(8,128)} %get-tuple-element.43, f32[128,64,256]{2,1,0:T(8,128)} %get-tuple-element.44), kind=kOutput, calls=%fused_computation.232 | convolution fusion | flops 805306368 | bytes 18874368 | tf_op jit(solution)/shard_map/bis,bjs->bij/dot_general | solution.py:557
  138.6 4.7 %reshape.333.x_ref = f32[32,128,128]{2,1,0:T(8,128)} reshape(f32[128,64,64]{2,1,0:T(8,128)} %fusion.88) | data formatting | bytes 4194304 | tf_op jit(solution)/shard_map/reshape | solution.py:558
  143.3 24.6 %shard_map.175 = f32[128,128]{1,0:T(8,128)} custom-call(f32[32,128,128]{2,1,0:T(8,128)} %reshape.333.x_ref), custom_call_target="tpu_custom_call" | custom-call | tf_op jit(solution)/shard_map/pallas_call | solution.py:379
  167.9 1.0 reshape.334
  176.3 1.2 multiply_reduce_fusion.5
  178.9 17.2 %shard_map.176 = f32[40,128]{1,0:T(8,128)} custom-call(f32[40,128]{1,0:T(8,128)} %pad_bitcast_fusion.x_ref), custom_call_target="tpu_custom_call" | custom-call | tf_op jit(solution)/shard_map/pallas_call | solution.py:193
  196.1 1.3 slice.192
  198.0 1.2 slice.190
  (269 shorter events, 45.7 us)
Async XLA Ops:
  0.6 10.7 %copy-start = (s32[256,256]{1,0:T(8,128)S(1)}, s32[256,256]{1,0:T(8,128)}, u32[]{:S(2)}) copy-start(s32[256,256]{1,0:T(8,128)} %param.17) | copy-start | bytes 786436
  1.4 16.6 %copy-start.64 = (f32[8]{0:T(128)}, f32[8]{0:T(128)S(1)}, u32[]{:S(2)}) copy-start(f32[8]{0:T(128)S(1)} %broadcast_add_fusion) | copy-start | bytes 100
  3.4 16.5 %copy-start.51 = (f32[4]{0:T(128)}, f32[4]{0:T(128)S(1)}, u32[]{:S(2)}) copy-start(f32[4]{0:T(128)S(1)} %get-tuple-element.10) | copy-start | bytes 52
  8.1 11.9 %copy-start.8 = (f32[64,64]{1,0:T(8,128)}, f32[64,64]{1,0:T(8,128)S(1)}, u32[]{:S(2)}) copy-start(f32[64,64]{1,0:T(8,128)S(1)} %fusion.64) | copy-start | bytes 49156
  9.7 6.9 %copy-start.40 = (f32[64,64]{1,0:T(8,128)}, f32[64,64]{1,0:T(8,128)S(1)}, u32[]{:S(2)}) copy-start(f32[64,64]{1,0:T(8,128)S(1)} %fusion.63) | copy-start | bytes 49156
  10.7 5.9 %copy-start.45 = (f32[8,64]{0,1:T(8,128)}, f32[8,64]{0,1:T(8,128)S(1)}, u32[]{:S(2)}) copy-start(f32[8,64]{0,1:T(8,128)S(1)} %fusion.29) | copy-start | bytes 6148
  10.8 7.2 %copy-start.66 = (f32[8]{0:T(128)}, f32[8]{0:T(128)S(1)}, u32[]{:S(2)}) copy-start(f32[8]{0:T(128)S(1)} %multiply_reduce_fusion.10) | copy-start | bytes 100
  18.8 35.2 %copy-start.28 = (f32[4,64,64]{2,1,0:T(8,128)}, f32[4,64,64]{2,1,0:T(8,128)S(1)}, u32[]{:S(2)}) copy-start(f32[4,64,64]{2,1,0:T(8,128)S(1)} %fusion.20) | copy-start | bytes 196612
  19.1 34.9 %copy-start.30 = (f32[4,64,64]{2,1,0:T(8,128)}, f32[4,64,64]{2,1,0:T(8,128)S(1)}, u32[]{:S(2)}) copy-start(f32[4,64,64]{2,1,0:T(8,128)S(1)} %fusion.19) | copy-start | bytes 196612
  19.4 34.6 %copy-start.32 = (f32[4,64,64]{2,1,0:T(8,128)}, f32[4,64,64]{2,1,0:T(8,128)S(1)}, u32[]{:S(2)}) copy-start(f32[4,64,64]{2,1,0:T(8,128)S(1)} %fusion.18) | copy-start | bytes 196612
  19.7 34.4 %copy-start.34 = (f32[4,64,64]{2,1,0:T(8,128)}, f32[4,64,64]{2,1,0:T(8,128)S(1)}, u32[]{:S(2)}) copy-start(f32[4,64,64]{2,1,0:T(8,128)S(1)} %fusion.17) | copy-start | bytes 196612
  21.7 35.5 %copy-start.10 = (f32[4,64,64]{2,1,0:T(8,128)}, f32[4,64,64]{2,1,0:T(8,128)S(1)}, u32[]{:S(2)}) copy-start(f32[4,64,64]{2,1,0:T(8,128)S(1)} %fusion.80) | copy-start | bytes 196612
  21.9 35.3 %copy-start.12 = (f32[4,64,64]{2,1,0:T(8,128)}, f32[4,64,64]{2,1,0:T(8,128)S(1)}, u32[]{:S(2)}) copy-start(f32[4,64,64]{2,1,0:T(8,128)S(1)} %fusion.81) | copy-start | bytes 196612
  49.6 7.7 %slice-start = ((f32[32,128,128]{2,1,0:T(8,128)}), f32[16,128,128]{2,1,0:T(8,128)S(1)}, s32[]{:S(2)}) async-start(f32[32,128,128]{2,1,0:T(8,128)} %shard_map.174), calls=%async_computation | async-start | bytes 2097152 | tf_op jit(solution)/shard_map/slice | solution.py:83
  57.6 4.6 %copy-start.6 = (f32[32,64,64]{2,1,0:T(8,128)S(1)}, f32[32,64,64]{2,1,0:T(8,128)}, u32[]{:S(2)}) copy-start(f32[32,64,64]{2,1,0:T(8,128)} %slice.144) | copy-start | bytes 1572868
  89.9 7.4 %copy-start.5 = (f32[8,64,256]{2,1,0:T(8,128)S(1)}, f32[8,64,256]{2,1,0:T(8,128)}, u32[]{:S(2)}) copy-start(f32[8,64,256]{2,1,0:T(8,128)} %copy-done.4) | copy-start | bytes 1572868
  104.2 4.6 %copy-start.3 = (f32[64,64,256]{2,1,0:T(8,128)S(1)}, f32[64,64,256]{2,1,0:T(8,128)}, u32[]{:S(2)}) copy-start(f32[64,64,256]{2,1,0:T(8,128)} %copy-done.2) | copy-start | bytes 12582916
  116.7 4.8 %copy-start.39 = (f32[1,64,256]{2,1,0:T(8,128)S(1)}, f32[1,64,256]{2,1,0:T(8,128)}, u32[]{:S(2)}) copy-start(f32[1,64,256]{2,1,0:T(8,128)} %get-tuple-element.12) | copy-start | bytes 196612
  116.7 4.8 %copy-start.68 = (f32[256]{0:T(256)S(1)}, f32[256]{0:T(256)}, u32[]{:S(2)}) copy-start(f32[256]{0:T(256)} %get-tuple-element.39) | copy-start | bytes 3076
  116.7 5.5 %copy-start.50 = (f32[16,256]{1,0:T(8,128)S(1)}, f32[16,256]{1,0:T(8,128)}, u32[]{:S(2)}) copy-start(f32[16,256]{1,0:T(8,128)} %copy-done.49) | copy-start | bytes 49156
  118.2 5.1 %copy-start.54 = (f32[8,256]{1,0:T(8,128)S(1)}, f32[8,256]{1,0:T(8,128)}, u32[]{:S(2)}) copy-start(f32[8,256]{1,0:T(8,128)} %copy-done.53) | copy-start | bytes 24580
  118.2 6.0 %copy-start.57 = (f32[4,256]{1,0:T(4,128)S(1)}, f32[4,256]{1,0:T(4,128)}, u32[]{:S(2)}) copy-start(f32[4,256]{1,0:T(4,128)} %copy-done.56) | copy-start | bytes 12292
  119.3 5.6 %copy-start.61 = (f32[2,256]{1,0:T(2,128)S(1)}, f32[2,256]{1,0:T(2,128)}, u32[]{:S(2)}) copy-start(f32[2,256]{1,0:T(2,128)} %copy-done.60) | copy-start | bytes 6148
  119.3 6.3 %copy-start.21 = (f32[2,64,256]{2,1,0:T(8,128)S(1)}, f32[2,64,256]{2,1,0:T(8,128)}, u32[]{:S(2)}) copy-start(f32[2,64,256]{2,1,0:T(8,128)} %copy-done.20) | copy-start | bytes 393220
  119.3 6.3 %copy-start.63 = (f32[256]{0:T(256)S(1)}, f32[256]{0:T(256)}, u32[]{:S(2)}) copy-start(f32[256]{0:T(256)} %copy-done.62) | copy-start | bytes 3076
  138.5 30.4 %copy-start.15 = (f32[4,64,64]{2,1,0:T(8,128)S(1)}, f32[4,64,64]{2,1,0:T(8,128)}, u32[]{:S(2)}) copy-start(f32[4,64,64]{2,1,0:T(8,128)} %copy-done.14) | copy-start | bytes 196612
  138.5 30.9 %copy-start.13 = (f32[4,64,64]{2,1,0:T(8,128)S(1)}, f32[4,64,64]{2,1,0:T(8,128)}, u32[]{:S(2)}) copy-start(f32[4,64,64]{2,1,0:T(8,128)} %copy-done.12) | copy-start | bytes 196612
  138.5 31.5 %copy-start.11 = (f32[4,64,64]{2,1,0:T(8,128)S(1)}, f32[4,64,64]{2,1,0:T(8,128)}, u32[]{:S(2)}) copy-start(f32[4,64,64]{2,1,0:T(8,128)} %copy-done.10) | copy-start | bytes 196612
  138.5 32.1 %copy-start.17 = (f32[4,64,64]{2,1,0:T(8,128)S(1)}, f32[4,64,64]{2,1,0:T(8,128)}, u32[]{:S(2)}) copy-start(f32[4,64,64]{2,1,0:T(8,128)} %copy-done.16) | copy-start | bytes 196612
  143.3 27.9 %copy-start.23 = (f32[4,64,64]{2,1,0:T(8,128)S(1)}, f32[4,64,64]{2,1,0:T(8,128)}, u32[]{:S(2)}) copy-start(f32[4,64,64]{2,1,0:T(8,128)} %copy-done.22) | copy-start | bytes 196612
  143.3 28.2 %copy-start.52 = (f32[4]{0:T(128)S(1)}, f32[4]{0:T(128)}, u32[]{:S(2)}) copy-start(f32[4]{0:T(128)} %copy-done.51) | copy-start | bytes 52
  143.3 28.5 %copy-start.35 = (f32[4,64,64]{2,1,0:T(8,128)S(1)}, f32[4,64,64]{2,1,0:T(8,128)}, u32[]{:S(2)}) copy-start(f32[4,64,64]{2,1,0:T(8,128)} %copy-done.34) | copy-start | bytes 196612
  143.3 29.2 %copy-start.33 = (f32[4,64,64]{2,1,0:T(8,128)S(1)}, f32[4,64,64]{2,1,0:T(8,128)}, u32[]{:S(2)}) copy-start(f32[4,64,64]{2,1,0:T(8,128)} %copy-done.32) | copy-start | bytes 196612
  143.3 29.8 %copy-start.31 = (f32[4,64,64]{2,1,0:T(8,128)S(1)}, f32[4,64,64]{2,1,0:T(8,128)}, u32[]{:S(2)}) copy-start(f32[4,64,64]{2,1,0:T(8,128)} %copy-done.30) | copy-start | bytes 196612
  167.9 5.8 %copy-start.29 = (f32[4,64,64]{2,1,0:T(8,128)S(1)}, f32[4,64,64]{2,1,0:T(8,128)}, u32[]{:S(2)}) copy-start(f32[4,64,64]{2,1,0:T(8,128)} %copy-done.28) | copy-start | bytes 196612
  167.9 6.4 %copy-start.27 = (f32[4,64,64]{2,1,0:T(8,128)S(1)}, f32[4,64,64]{2,1,0:T(8,128)}, u32[]{:S(2)}) copy-start(f32[4,64,64]{2,1,0:T(8,128)} %copy-done.26) | copy-start | bytes 196612
  169.5 5.5 %copy-start.25 = (f32[4,64,64]{2,1,0:T(8,128)S(1)}, f32[4,64,64]{2,1,0:T(8,128)}, u32[]{:S(2)}) copy-start(f32[4,64,64]{2,1,0:T(8,128)} %copy-done.24) | copy-start | bytes 196612
  170.0 5.5 %copy-start.9 = (f32[64,64]{1,0:T(8,128)S(1)}, f32[64,64]{1,0:T(8,128)}, u32[]{:S(2)}) copy-start(f32[64,64]{1,0:T(8,128)} %copy-done.8) | copy-start | bytes 49156
  170.0 5.5 %copy-start.69 = (f32[4]{0:T(128)S(1)}, f32[4]{0:T(128)}, u32[]{:S(2)}) copy-start(f32[4]{0:T(128)} %get-tuple-element.9) | copy-start | bytes 52
  170.3 5.9 %copy-start.41 = (f32[64,64]{1,0:T(8,128)S(1)}, f32[64,64]{1,0:T(8,128)}, u32[]{:S(2)}) copy-start(f32[64,64]{1,0:T(8,128)} %copy-done.40) | copy-start | bytes 49156
  170.3 5.9 %copy-start.46 = (f32[8,64]{0,1:T(8,128)S(1)}, f32[8,64]{0,1:T(8,128)}, u32[]{:S(2)}) copy-start(f32[8,64]{0,1:T(8,128)} %copy-done.45) | copy-start | bytes 6148
  170.3 5.9 %copy-start.47 = (f32[64,64]{1,0:T(8,128)S(1)}, f32[64,64]{1,0:T(8,128)}, u32[]{:S(2)}) copy-start(f32[64,64]{1,0:T(8,128)} %constant.112) | copy-start | bytes 49156
  170.4 5.9 %copy-start.48 = (f32[64,64]{1,0:T(8,128)S(1)}, f32[64,64]{1,0:T(8,128)}, u32[]{:S(2)}) copy-start(f32[64,64]{1,0:T(8,128)} %constant.111) | copy-start | bytes 49156
  170.4 5.9 %copy-start.65 = (f32[8]{0:T(128)S(1)}, f32[8]{0:T(128)}, u32[]{:S(2)}) copy-start(f32[8]{0:T(128)} %copy-done.64) | copy-start | bytes 100
  170.4 5.9 %copy-start.67 = (f32[8]{0:T(128)S(1)}, f32[8]{0:T(128)}, u32[]{:S(2)}) copy-start(f32[8]{0:T(128)} %copy-done.66) | copy-start | bytes 100
  170.4 5.9 %copy-start.70 = (f32[8]{0:T(128)S(1)}, f32[8]{0:T(128)}, u32[]{:S(2)}) copy-start(f32[8]{0:T(128)} %multiply_divide_fusion.7) | copy-start | bytes 100
  171.4 6.1 %copy-start.59 = (f32[64]{0:T(128)S(1)}, f32[64]{0:T(128)}, u32[]{:S(2)}) copy-start(f32[64]{0:T(128)} %copy-done.58) | copy-start | bytes 772
  171.8 30.1 %copy-start.1 = (s32[256,256]{1,0:T(8,128)S(1)}, s32[256,256]{1,0:T(8,128)}, u32[]{:S(2)}) copy-start(s32[256,256]{1,0:T(8,128)} %param.17) | copy-start | bytes 786436
  (24 other events, 44.8 us)

commit v4 on v3

--- a/solution.py
+++ b/solution.py
@@ -316,8 +316,8 @@
             device_id_type=MESH_ID,
         )
 
-    def first_send(m, carry):
-        to_partner(m).start()
+    def first_send(d, carry):
+        to_partner(lax.rem(chip + d, chips)).start()
         return carry
 
     lax.fori_loop(0, chips, first_send, 0)

time: 205 us -> 205 us (level)
  no operation moved by 1% of the time
where the time goes in v4:
time: 205 us; the launch traced here: 203 us
  Pallas kernels  67.7 us (33%)
  other arithmetic  48.4 us (24%)
  matrix products  37.7 us (18%)
  local copies, waits for them, and re-layouts  34.5 us (17%)
  blocking collectives  10.1 us (5%)
  between operations  4.57 us (2%)
    pallas_call x1, Pallas kernels, pair_gather(): pl.pallas_call(pair_gather_kernel, out_shape=jax.ShapeDtypeStruct((n,) +...  25.9 us
    pallas_call x1, Pallas kernels, pair_scatter(): pl.pallas_call(pair_scatter_kernel, out_shape=jax.ShapeDtypeStruct(chunk,...  24.6 us
    pallas_call x1, Pallas kernels, allreduce_all(): pl.pallas_call(functools.partial(allreduce_kernel, n_site, n_branch), out...  17.1 us
    unnamed x14, other arithmetic  15.6 us
    dot_general x1, matrix products, body(): jnp.einsum('bis,bjs->bij', part_above, part_below, precision=lax.Precisio...  11.7 us
    all_gather x1, blocking collectives, body(): top_all = lax.all_gather(top_pack, 'branch', axis=0, tiled=False)  10.1 us
    dot_general x35, matrix products, product(): return jnp.einsum('bij,bjk->bik', left, right, precision=lax.Precision.HIGH)  9.43 us
    slice x8, local copies, waits for them, and re-layouts, down_pass(): down_part = carried(probs[offset:offset + amount], current)  7.58 us

profile of v4, /device:TPU:1, one launch (start us, length us, event | category | flops | bytes accessed | tf_op | source)
XLA Modules:
  0.0 203.0 jit_solution(14221667853441341229)
XLA Ops:
  4.2 1.2 convert_element_type.44
  5.4 1.3 fusion.78
  8.1 0.8 copy.140
  8.9 0.8 fusion.63
  9.7 1.0 fusion.29
  12.7 1.6 gather_fusion
  14.4 2.2 %fusion.27 = f32[128,64,64]{0,2,1:T(8,128)S(1)} fusion(f32[8]{0:T(128)S(1)} %multiply_reduce_fusion.10, f32[64,64]{1,0:T(8,128)S(1)} %fusion.64, f32[8,64]{0,1:T(8,128)S(1)} %fusion.29, f32[64,64]{1,0:T(8,128)} %constant.112, f32[8]{0:T(128)S(1)} %broadcast_add_fusion, f32[64,64]{1,0:T(8,128)} %constant.111, f32[64,64]{1,0:T(8,128)S(1)} %fusion.63, ...), kind=kOutput, calls=%fused_computation.95 | convolution fusion | flops 25396224 | bytes 2165312 | tf_op jit(solution)/shard_map/bc,cij->bij/dot_general | solution.py:529
  23.7 25.9 %shard_map.174 = f32[32,128,128]{2,1,0:T(8,128)} custom-call(f32[128,128]{1,0:T(8,128)} %reshape.322.x_ref), custom_call_target="tpu_custom_call" | custom-call | tf_op jit(solution)/shard_map/pallas_call | solution.py:498
  49.6 0.9 slice.149
  51.3 0.9 slice.147
  52.2 0.8 slice.148
  53.0 1.0 slice.145
  54.0 0.9 slice.146
  55.0 1.1 slice.143
  56.0 1.2 slice.144
  57.6 3.1 %fusion.7 = f32[64,64,256]{2,1,0:T(8,128)S(1)} fusion(f32[64,64,64]{2,1,0:T(8,128)S(1)} %slice.154, s32[64,256]{1,0:T(8,128)} %broadcast_select_fusion, pred[64,256]{1,0:T(8,128)(4,1)S(1)} %select_compare_fusion), kind=kOutput, calls=%fused_computation.13 | convolution fusion | flops 405798912 | bytes 5324800 | tf_op jit(solution)/shard_map/bij,bjs->bis/dot_general | solution.py:62
  61.2 0.9 log_reduce_fusion
  62.2 1.1 fusion.24
  68.1 4.3 %reshape.323 = f32[128,64,64]{2,1,0:T(8,128)} reshape(f32[32,128,128]{2,1,0:T(8,128)} %shard_map.174) | data formatting | bytes 4194304 | tf_op jit(solution)/shard_map/reshape | solution.py:537
  72.4 1.0 fusion.61
  74.2 0.9 fusion.54
  75.2 10.1 %all-gather.1 = f32[4,65,256]{2,1,0:T(8,128)S(1)} all-gather(f32[1,65,256]{2,1,0:T(8,128)S(1)} %maximum_bitcast_fusion.2), channel_id=2, replica_groups=mesh['site'=32,'branch'=4] {'branch'}, dimensions={0}, use_global_device_ids=true | all-gather | bytes 332800 | tf_op jit(solution)/shard_map/all_gather | solution.py:544
  87.4 1.9 multiply_reduce_fusion.11
  89.9 1.2 fusion.79
  91.1 0.9 fusion.50
  92.0 1.1 fusion.44
  93.4 0.9 multiply_reduce_fusion.9
  95.9 1.2 fusion.84
  100.4 1.0 fusion.12
  103.1 1.1 fusion.87
  104.2 1.9 fusion.11
  106.1 2.7 %fusion.6 = f32[128,64,256]{2,1,0:T(8,128)} fusion(s32[64,256]{1,0:T(8,128)S(1)} %copy-done.38, pred[64,256]{1,0:T(8,128)(4,1)S(1)} %select_compare_fusion), kind=kLoop, calls=%fused_computation.12 | loop fusion | flops 3145727 | bytes 4276224
  108.8 2.4 %multiply_bitcast_fusion.1 = (f32[32,1,64,256]{3,2,0,1:T(8,128)S(1)}, f32[32,1,64,256]{3,2,0,1:T(8,128)S(1)}, f32[128,64,256]{2,1,0:T(8,128)}) fusion(f32[32,64,256]{2,1,0:T(8,128)S(1)} %fusion.11, f32[64,64,256]{2,1,0:T(8,128)S(1)} %copy-done.3, f32[128,64,256]{2,1,0:T(8,128)} %fusion.6, f32[32,256]{1,0:T(8,128)S(1)} %copy-done.44), kind=kLoop, calls=%fused_computation.19 | loop fusion | flops 2097152 | bytes 12615680 | tf_op jit(solution)/shard_map/stack | solution.py:119
  111.8 1.4 fusion.5
  113.2 3.4 %constant_dynamic-update-slice_fusion.1 = f32[128,64,256]{2,1,0:T(8,128)} fusion(f32[64,256]{1,0:T(8,128)S(1)} %multiply_divide_fusion, f32[32,2,64,256]{3,2,1,0:T(8,128)S(1)} %copy.152), kind=kLoop, calls=%fused_computation.166 | loop fusion | flops 1048575 | bytes 8454144
  116.7 1.5 multiply_dynamic-update-slice_fusion
  118.2 1.1 multiply_dynamic-update-slice_fusion.1
  119.3 0.8 multiply_dynamic-update-slice_fusion.2
  122.1 1.2 fusion.25
  123.3 0.9 fusion.30
  126.9 11.7 %fusion.88 = f32[128,64,64]{2,1,0:T(8,128)} fusion(f32[128,64,256]{2,1,0:T(8,128)} %get-tuple-element.43, f32[128,64,256]{2,1,0:T(8,128)} %get-tuple-element.44), kind=kOutput, calls=%fused_computation.232 | convolution fusion | flops 805306368 | bytes 18874368 | tf_op jit(solution)/shard_map/bis,bjs->bij/dot_general | solution.py:557
  138.6 4.7 %reshape.333.x_ref = f32[32,128,128]{2,1,0:T(8,128)} reshape(f32[128,64,64]{2,1,0:T(8,128)} %fusion.88) | data formatting | bytes 4194304 | tf_op jit(solution)/shard_map/reshape | solution.py:558
  143.3 24.6 %shard_map.175 = f32[128,128]{1,0:T(8,128)} custom-call(f32[32,128,128]{2,1,0:T(8,128)} %reshape.333.x_ref), custom_call_target="tpu_custom_call" | custom-call | tf_op jit(solution)/shard_map/pallas_call | solution.py:379
  167.9 1.0 reshape.334
  176.3 1.2 multiply_reduce_fusion.5
  179.0 17.1 %shard_map.176 = f32[40,128]{1,0:T(8,128)} custom-call(f32[40,128]{1,0:T(8,128)} %pad_bitcast_fusion.x_ref), custom_call_target="tpu_custom_call" | custom-call | tf_op jit(solution)/shard_map/pallas_call | solution.py:193
  196.1 1.3 slice.192
  198.0 1.2 slice.190
  (269 shorter events, 45.7 us)
Async XLA Ops:
  0.6 10.7 %copy-start = (s32[256,256]{1,0:T(8,128)S(1)}, s32[256,256]{1,0:T(8,128)}, u32[]{:S(2)}) copy-start(s32[256,256]{1,0:T(8,128)} %param.17) | copy-start | bytes 786436
  1.4 16.6 %copy-start.64 = (f32[8]{0:T(128)}, f32[8]{0:T(128)S(1)}, u32[]{:S(2)}) copy-start(f32[8]{0:T(128)S(1)} %broadcast_add_fusion) | copy-start | bytes 100
  3.4 16.5 %copy-start.51 = (f32[4]{0:T(128)}, f32[4]{0:T(128)S(1)}, u32[]{:S(2)}) copy-start(f32[4]{0:T(128)S(1)} %get-tuple-element.10) | copy-start | bytes 52
  8.1 11.9 %copy-start.8 = (f32[64,64]{1,0:T(8,128)}, f32[64,64]{1,0:T(8,128)S(1)}, u32[]{:S(2)}) copy-start(f32[64,64]{1,0:T(8,128)S(1)} %fusion.64) | copy-start | bytes 49156
  9.7 6.9 %copy-start.40 = (f32[64,64]{1,0:T(8,128)}, f32[64,64]{1,0:T(8,128)S(1)}, u32[]{:S(2)}) copy-start(f32[64,64]{1,0:T(8,128)S(1)} %fusion.63) | copy-start | bytes 49156
  10.7 5.9 %copy-start.45 = (f32[8,64]{0,1:T(8,128)}, f32[8,64]{0,1:T(8,128)S(1)}, u32[]{:S(2)}) copy-start(f32[8,64]{0,1:T(8,128)S(1)} %fusion.29) | copy-start | bytes 6148
  10.8 7.2 %copy-start.66 = (f32[8]{0:T(128)}, f32[8]{0:T(128)S(1)}, u32[]{:S(2)}) copy-start(f32[8]{0:T(128)S(1)} %multiply_reduce_fusion.10) | copy-start | bytes 100
  18.8 35.2 %copy-start.28 = (f32[4,64,64]{2,1,0:T(8,128)}, f32[4,64,64]{2,1,0:T(8,128)S(1)}, u32[]{:S(2)}) copy-start(f32[4,64,64]{2,1,0:T(8,128)S(1)} %fusion.20) | copy-start | bytes 196612
  19.1 34.9 %copy-start.30 = (f32[4,64,64]{2,1,0:T(8,128)}, f32[4,64,64]{2,1,0:T(8,128)S(1)}, u32[]{:S(2)}) copy-start(f32[4,64,64]{2,1,0:T(8,128)S(1)} %fusion.19) | copy-start | bytes 196612
  19.4 34.6 %copy-start.32 = (f32[4,64,64]{2,1,0:T(8,128)}, f32[4,64,64]{2,1,0:T(8,128)S(1)}, u32[]{:S(2)}) copy-start(f32[4,64,64]{2,1,0:T(8,128)S(1)} %fusion.18) | copy-start | bytes 196612
  19.7 34.4 %copy-start.34 = (f32[4,64,64]{2,1,0:T(8,128)}, f32[4,64,64]{2,1,0:T(8,128)S(1)}, u32[]{:S(2)}) copy-start(f32[4,64,64]{2,1,0:T(8,128)S(1)} %fusion.17) | copy-start | bytes 196612
  21.7 35.5 %copy-start.10 = (f32[4,64,64]{2,1,0:T(8,128)}, f32[4,64,64]{2,1,0:T(8,128)S(1)}, u32[]{:S(2)}) copy-start(f32[4,64,64]{2,1,0:T(8,128)S(1)} %fusion.80) | copy-start | bytes 196612
  21.9 35.3 %copy-start.12 = (f32[4,64,64]{2,1,0:T(8,128)}, f32[4,64,64]{2,1,0:T(8,128)S(1)}, u32[]{:S(2)}) copy-start(f32[4,64,64]{2,1,0:T(8,128)S(1)} %fusion.81) | copy-start | bytes 196612
  49.6 7.7 %slice-start = ((f32[32,128,128]{2,1,0:T(8,128)}), f32[16,128,128]{2,1,0:T(8,128)S(1)}, s32[]{:S(2)}) async-start(f32[32,128,128]{2,1,0:T(8,128)} %shard_map.174), calls=%async_computation | async-start | bytes 2097152 | tf_op jit(solution)/shard_map/slice | solution.py:83
  57.6 4.6 %copy-start.6 = (f32[32,64,64]{2,1,0:T(8,128)S(1)}, f32[32,64,64]{2,1,0:T(8,128)}, u32[]{:S(2)}) copy-start(f32[32,64,64]{2,1,0:T(8,128)} %slice.144) | copy-start | bytes 1572868
  89.9 7.4 %copy-start.5 = (f32[8,64,256]{2,1,0:T(8,128)S(1)}, f32[8,64,256]{2,1,0:T(8,128)}, u32[]{:S(2)}) copy-start(f32[8,64,256]{2,1,0:T(8,128)} %copy-done.4) | copy-start | bytes 1572868
  104.2 4.6 %copy-start.3 = (f32[64,64,256]{2,1,0:T(8,128)S(1)}, f32[64,64,256]{2,1,0:T(8,128)}, u32[]{:S(2)}) copy-start(f32[64,64,256]{2,1,0:T(8,128)} %copy-done.2) | copy-start | bytes 12582916
  116.7 4.8 %copy-start.39 = (f32[1,64,256]{2,1,0:T(8,128)S(1)}, f32[1,64,256]{2,1,0:T(8,128)}, u32[]{:S(2)}) copy-start(f32[1,64,256]{2,1,0:T(8,128)} %get-tuple-element.12) | copy-start | bytes 196612
  116.7 4.8 %copy-start.68 = (f32[256]{0:T(256)S(1)}, f32[256]{0:T(256)}, u32[]{:S(2)}) copy-start(f32[256]{0:T(256)} %get-tuple-element.39) | copy-start | bytes 3076
  116.7 5.5 %copy-start.50 = (f32[16,256]{1,0:T(8,128)S(1)}, f32[16,256]{1,0:T(8,128)}, u32[]{:S(2)}) copy-start(f32[16,256]{1,0:T(8,128)} %copy-done.49) | copy-start | bytes 49156
  118.2 5.1 %copy-start.54 = (f32[8,256]{1,0:T(8,128)S(1)}, f32[8,256]{1,0:T(8,128)}, u32[]{:S(2)}) copy-start(f32[8,256]{1,0:T(8,128)} %copy-done.53) | copy-start | bytes 24580
  118.2 6.0 %copy-start.57 = (f32[4,256]{1,0:T(4,128)S(1)}, f32[4,256]{1,0:T(4,128)}, u32[]{:S(2)}) copy-start(f32[4,256]{1,0:T(4,128)} %copy-done.56) | copy-start | bytes 12292
  119.3 5.6 %copy-start.61 = (f32[2,256]{1,0:T(2,128)S(1)}, f32[2,256]{1,0:T(2,128)}, u32[]{:S(2)}) copy-start(f32[2,256]{1,0:T(2,128)} %copy-done.60) | copy-start | bytes 6148
  119.3 6.3 %copy-start.21 = (f32[2,64,256]{2,1,0:T(8,128)S(1)}, f32[2,64,256]{2,1,0:T(8,128)}, u32[]{:S(2)}) copy-start(f32[2,64,256]{2,1,0:T(8,128)} %copy-done.20) | copy-start | bytes 393220
  119.3 6.3 %copy-start.63 = (f32[256]{0:T(256)S(1)}, f32[256]{0:T(256)}, u32[]{:S(2)}) copy-start(f32[256]{0:T(256)} %copy-done.62) | copy-start | bytes 3076
  138.5 30.4 %copy-start.15 = (f32[4,64,64]{2,1,0:T(8,128)S(1)}, f32[4,64,64]{2,1,0:T(8,128)}, u32[]{:S(2)}) copy-start(f32[4,64,64]{2,1,0:T(8,128)} %copy-done.14) | copy-start | bytes 196612
  138.5 30.9 %copy-start.13 = (f32[4,64,64]{2,1,0:T(8,128)S(1)}, f32[4,64,64]{2,1,0:T(8,128)}, u32[]{:S(2)}) copy-start(f32[4,64,64]{2,1,0:T(8,128)} %copy-done.12) | copy-start | bytes 196612
  138.5 31.5 %copy-start.11 = (f32[4,64,64]{2,1,0:T(8,128)S(1)}, f32[4,64,64]{2,1,0:T(8,128)}, u32[]{:S(2)}) copy-start(f32[4,64,64]{2,1,0:T(8,128)} %copy-done.10) | copy-start | bytes 196612
  138.5 32.1 %copy-start.17 = (f32[4,64,64]{2,1,0:T(8,128)S(1)}, f32[4,64,64]{2,1,0:T(8,128)}, u32[]{:S(2)}) copy-start(f32[4,64,64]{2,1,0:T(8,128)} %copy-done.16) | copy-start | bytes 196612
  143.3 27.9 %copy-start.23 = (f32[4,64,64]{2,1,0:T(8,128)S(1)}, f32[4,64,64]{2,1,0:T(8,128)}, u32[]{:S(2)}) copy-start(f32[4,64,64]{2,1,0:T(8,128)} %copy-done.22) | copy-start | bytes 196612
  143.3 28.2 %copy-start.52 = (f32[4]{0:T(128)S(1)}, f32[4]{0:T(128)}, u32[]{:S(2)}) copy-start(f32[4]{0:T(128)} %copy-done.51) | copy-start | bytes 52
  143.3 28.6 %copy-start.35 = (f32[4,64,64]{2,1,0:T(8,128)S(1)}, f32[4,64,64]{2,1,0:T(8,128)}, u32[]{:S(2)}) copy-start(f32[4,64,64]{2,1,0:T(8,128)} %copy-done.34) | copy-start | bytes 196612
  143.3 29.2 %copy-start.33 = (f32[4,64,64]{2,1,0:T(8,128)S(1)}, f32[4,64,64]{2,1,0:T(8,128)}, u32[]{:S(2)}) copy-start(f32[4,64,64]{2,1,0:T(8,128)} %copy-done.32) | copy-start | bytes 196612
  143.3 29.8 %copy-start.31 = (f32[4,64,64]{2,1,0:T(8,128)S(1)}, f32[4,64,64]{2,1,0:T(8,128)}, u32[]{:S(2)}) copy-start(f32[4,64,64]{2,1,0:T(8,128)} %copy-done.30) | copy-start | bytes 196612
  167.9 5.8 %copy-start.29 = (f32[4,64,64]{2,1,0:T(8,128)S(1)}, f32[4,64,64]{2,1,0:T(8,128)}, u32[]{:S(2)}) copy-start(f32[4,64,64]{2,1,0:T(8,128)} %copy-done.28) | copy-start | bytes 196612
  167.9 6.4 %copy-start.27 = (f32[4,64,64]{2,1,0:T(8,128)S(1)}, f32[4,64,64]{2,1,0:T(8,128)}, u32[]{:S(2)}) copy-start(f32[4,64,64]{2,1,0:T(8,128)} %copy-done.26) | copy-start | bytes 196612
  169.5 5.5 %copy-start.25 = (f32[4,64,64]{2,1,0:T(8,128)S(1)}, f32[4,64,64]{2,1,0:T(8,128)}, u32[]{:S(2)}) copy-start(f32[4,64,64]{2,1,0:T(8,128)} %copy-done.24) | copy-start | bytes 196612
  170.0 5.5 %copy-start.9 = (f32[64,64]{1,0:T(8,128)S(1)}, f32[64,64]{1,0:T(8,128)}, u32[]{:S(2)}) copy-start(f32[64,64]{1,0:T(8,128)} %copy-done.8) | copy-start | bytes 49156
  170.0 5.5 %copy-start.69 = (f32[4]{0:T(128)S(1)}, f32[4]{0:T(128)}, u32[]{:S(2)}) copy-start(f32[4]{0:T(128)} %get-tuple-element.9) | copy-start | bytes 52
  170.3 5.9 %copy-start.41 = (f32[64,64]{1,0:T(8,128)S(1)}, f32[64,64]{1,0:T(8,128)}, u32[]{:S(2)}) copy-start(f32[64,64]{1,0:T(8,128)} %copy-done.40) | copy-start | bytes 49156
  170.3 5.9 %copy-start.46 = (f32[8,64]{0,1:T(8,128)S(1)}, f32[8,64]{0,1:T(8,128)}, u32[]{:S(2)}) copy-start(f32[8,64]{0,1:T(8,128)} %copy-done.45) | copy-start | bytes 6148
  170.4 5.9 %copy-start.47 = (f32[64,64]{1,0:T(8,128)S(1)}, f32[64,64]{1,0:T(8,128)}, u32[]{:S(2)}) copy-start(f32[64,64]{1,0:T(8,128)} %constant.112) | copy-start | bytes 49156
  170.4 5.9 %copy-start.48 = (f32[64,64]{1,0:T(8,128)S(1)}, f32[64,64]{1,0:T(8,128)}, u32[]{:S(2)}) copy-start(f32[64,64]{1,0:T(8,128)} %constant.111) | copy-start | bytes 49156
  170.4 5.9 %copy-start.65 = (f32[8]{0:T(128)S(1)}, f32[8]{0:T(128)}, u32[]{:S(2)}) copy-start(f32[8]{0:T(128)} %copy-done.64) | copy-start | bytes 100
  170.4 5.9 %copy-start.67 = (f32[8]{0:T(128)S(1)}, f32[8]{0:T(128)}, u32[]{:S(2)}) copy-start(f32[8]{0:T(128)} %copy-done.66) | copy-start | bytes 100
  170.4 5.9 %copy-start.70 = (f32[8]{0:T(128)S(1)}, f32[8]{0:T(128)}, u32[]{:S(2)}) copy-start(f32[8]{0:T(128)} %multiply_divide_fusion.7) | copy-start | bytes 100
  171.5 6.1 %copy-start.59 = (f32[64]{0:T(128)S(1)}, f32[64]{0:T(128)}, u32[]{:S(2)}) copy-start(f32[64]{0:T(128)} %copy-done.58) | copy-start | bytes 772
  171.8 30.0 %copy-start.1 = (s32[256,256]{1,0:T(8,128)S(1)}, s32[256,256]{1,0:T(8,128)}, u32[]{:S(2)}) copy-start(s32[256,256]{1,0:T(8,128)} %param.17) | copy-start | bytes 786436
  (24 other events, 44.8 us)

commit v5 on v3

--- a/solution.py
+++ b/solution.py
@@ -137,8 +137,7 @@
     core = s % 2
     plane = s // 2
     return [
-        (2, core, lambda c: (s - core + c, k)),
-        (n_branch, k, lambda c: (s, c)),
+        (2 * n_branch, 2 * k + core, lambda c: (s - core + c % 2, c // 2)),
         (n_site // 2, plane, lambda c: (2 * c + core, k)),
     ]
 
@@ -196,9 +195,9 @@
         in_specs=[pl.BlockSpec(memory_space=pltpu.VMEM)],
         out_specs=pl.BlockSpec(memory_space=pltpu.VMEM),
         scratch_shapes=[
-            pltpu.VMEM((3, n_site // 2, rows, 128), jnp.float32),
-            pltpu.SemaphoreType.DMA((3, n_site // 2)),
-            pltpu.SemaphoreType.DMA((3, n_site // 2)),
+            pltpu.VMEM((2, n_site // 2, rows, 128), jnp.float32),
+            pltpu.SemaphoreType.DMA((2, n_site // 2)),
+            pltpu.SemaphoreType.DMA((2, n_site // 2)),
         ],
         compiler_params=pltpu.CompilerParams(collective_id=0, has_side_effects=True),
     )(x)

time: 205 us -> 205 us (level)
  no operation moved by 1% of the time
where the time goes in v5:
time: 205 us; the launch traced here: 204 us
  Pallas kernels  68.2 us (33%)
  other arithmetic  48.4 us (24%)
  matrix products  37.7 us (18%)
  local copies, waits for them, and re-layouts  34.5 us (17%)
  blocking collectives  10.1 us (5%)
  between operations  4.57 us (2%)
    pallas_call x1, Pallas kernels, pair_gather(): pl.pallas_call(pair_gather_kernel, out_shape=jax.ShapeDtypeStruct((n,) +...  25.9 us
    pallas_call x1, Pallas kernels, pair_scatter(): pl.pallas_call(pair_scatter_kernel, out_shape=jax.ShapeDtypeStruct(chunk,...  24.6 us
    pallas_call x1, Pallas kernels, allreduce_all(): pl.pallas_call(functools.partial(allreduce_kernel, n_site, n_branch), out...  17.7 us
    unnamed x14, other arithmetic  15.6 us
    dot_general x1, matrix products, body(): jnp.einsum('bis,bjs->bij', part_above, part_below, precision=lax.Precisio...  11.7 us
    all_gather x1, blocking collectives, body(): top_all = lax.all_gather(top_pack, 'branch', axis=0, tiled=False)  10.1 us
    dot_general x35, matrix products, product(): return jnp.einsum('bij,bjk->bik', left, right, precision=lax.Precision.HIGH)  9.43 us
    slice x8, local copies, waits for them, and re-layouts, down_pass(): down_part = carried(probs[offset:offset + amount], current)  7.58 us

profile of v5, /device:TPU:1, one launch (start us, length us, event | category | flops | bytes accessed | tf_op | source)
XLA Modules:
  0.0 203.6 jit_solution(17632997574757855398)
XLA Ops:
  4.2 1.2 convert_element_type.44
  5.4 1.3 fusion.78
  8.1 0.8 copy.140
  8.9 0.8 fusion.63
  9.7 1.0 fusion.29
  12.7 1.6 gather_fusion
  14.4 2.2 %fusion.27 = f32[128,64,64]{0,2,1:T(8,128)S(1)} fusion(f32[8]{0:T(128)S(1)} %multiply_reduce_fusion.10, f32[64,64]{1,0:T(8,128)S(1)} %fusion.64, f32[8,64]{0,1:T(8,128)S(1)} %fusion.29, f32[64,64]{1,0:T(8,128)} %constant.112, f32[8]{0:T(128)S(1)} %broadcast_add_fusion, f32[64,64]{1,0:T(8,128)} %constant.111, f32[64,64]{1,0:T(8,128)S(1)} %fusion.63, ...), kind=kOutput, calls=%fused_computation.95 | convolution fusion | flops 25396224 | bytes 2165312 | tf_op jit(solution)/shard_map/bc,cij->bij/dot_general | solution.py:528
  23.7 25.9 %shard_map.174 = f32[32,128,128]{2,1,0:T(8,128)} custom-call(f32[128,128]{1,0:T(8,128)} %reshape.322.x_ref), custom_call_target="tpu_custom_call" | custom-call | tf_op jit(solution)/shard_map/pallas_call | solution.py:497
  49.6 0.9 slice.149
  51.3 0.9 slice.147
  52.2 0.8 slice.148
  53.0 1.0 slice.145
  54.0 0.9 slice.146
  55.0 1.1 slice.143
  56.0 1.2 slice.144
  57.6 3.1 %fusion.7 = f32[64,64,256]{2,1,0:T(8,128)S(1)} fusion(f32[64,64,64]{2,1,0:T(8,128)S(1)} %slice.154, s32[64,256]{1,0:T(8,128)} %broadcast_select_fusion, pred[64,256]{1,0:T(8,128)(4,1)S(1)} %select_compare_fusion), kind=kOutput, calls=%fused_computation.13 | convolution fusion | flops 405798912 | bytes 5324800 | tf_op jit(solution)/shard_map/bij,bjs->bis/dot_general | solution.py:62
  61.2 0.9 log_reduce_fusion
  62.2 1.1 fusion.24
  68.1 4.3 %reshape.323 = f32[128,64,64]{2,1,0:T(8,128)} reshape(f32[32,128,128]{2,1,0:T(8,128)} %shard_map.174) | data formatting | bytes 4194304 | tf_op jit(solution)/shard_map/reshape | solution.py:536
  72.4 1.0 fusion.61
  74.2 0.9 fusion.54
  75.2 10.1 %all-gather.1 = f32[4,65,256]{2,1,0:T(8,128)S(1)} all-gather(f32[1,65,256]{2,1,0:T(8,128)S(1)} %maximum_bitcast_fusion.2), channel_id=2, replica_groups=mesh['site'=32,'branch'=4] {'branch'}, dimensions={0}, use_global_device_ids=true | all-gather | bytes 332800 | tf_op jit(solution)/shard_map/all_gather | solution.py:543
  87.4 1.9 multiply_reduce_fusion.11
  89.9 1.2 fusion.79
  91.1 0.9 fusion.50
  92.0 1.1 fusion.44
  93.4 0.9 multiply_reduce_fusion.9
  95.9 1.2 fusion.84
  100.4 1.0 fusion.12
  103.1 1.1 fusion.87
  104.2 1.9 fusion.11
  106.1 2.7 %fusion.6 = f32[128,64,256]{2,1,0:T(8,128)} fusion(s32[64,256]{1,0:T(8,128)S(1)} %copy-done.38, pred[64,256]{1,0:T(8,128)(4,1)S(1)} %select_compare_fusion), kind=kLoop, calls=%fused_computation.12 | loop fusion | flops 3145727 | bytes 4276224
  108.8 2.4 %multiply_bitcast_fusion.1 = (f32[32,1,64,256]{3,2,0,1:T(8,128)S(1)}, f32[32,1,64,256]{3,2,0,1:T(8,128)S(1)}, f32[128,64,256]{2,1,0:T(8,128)}) fusion(f32[32,64,256]{2,1,0:T(8,128)S(1)} %fusion.11, f32[64,64,256]{2,1,0:T(8,128)S(1)} %copy-done.3, f32[128,64,256]{2,1,0:T(8,128)} %fusion.6, f32[32,256]{1,0:T(8,128)S(1)} %copy-done.44), kind=kLoop, calls=%fused_computation.19 | loop fusion | flops 2097152 | bytes 12615680 | tf_op jit(solution)/shard_map/stack | solution.py:119
  111.8 1.4 fusion.5
  113.2 3.4 %constant_dynamic-update-slice_fusion.1 = f32[128,64,256]{2,1,0:T(8,128)} fusion(f32[64,256]{1,0:T(8,128)S(1)} %multiply_divide_fusion, f32[32,2,64,256]{3,2,1,0:T(8,128)S(1)} %copy.152), kind=kLoop, calls=%fused_computation.166 | loop fusion | flops 1048575 | bytes 8454144
  116.7 1.5 multiply_dynamic-update-slice_fusion
  118.2 1.1 multiply_dynamic-update-slice_fusion.1
  119.3 0.8 multiply_dynamic-update-slice_fusion.2
  122.1 1.2 fusion.25
  123.3 0.9 fusion.30
  126.9 11.7 %fusion.88 = f32[128,64,64]{2,1,0:T(8,128)} fusion(f32[128,64,256]{2,1,0:T(8,128)} %get-tuple-element.43, f32[128,64,256]{2,1,0:T(8,128)} %get-tuple-element.44), kind=kOutput, calls=%fused_computation.232 | convolution fusion | flops 805306368 | bytes 18874368 | tf_op jit(solution)/shard_map/bis,bjs->bij/dot_general | solution.py:556
  138.6 4.7 %reshape.333.x_ref = f32[32,128,128]{2,1,0:T(8,128)} reshape(f32[128,64,64]{2,1,0:T(8,128)} %fusion.88) | data formatting | bytes 4194304 | tf_op jit(solution)/shard_map/reshape | solution.py:557
  143.3 24.6 %shard_map.175 = f32[128,128]{1,0:T(8,128)} custom-call(f32[32,128,128]{2,1,0:T(8,128)} %reshape.333.x_ref), custom_call_target="tpu_custom_call" | custom-call | tf_op jit(solution)/shard_map/pallas_call | solution.py:378
  167.9 1.0 reshape.334
  176.3 1.2 multiply_reduce_fusion.5
  178.9 17.7 %shard_map.176 = f32[40,128]{1,0:T(8,128)} custom-call(f32[40,128]{1,0:T(8,128)} %pad_bitcast_fusion.x_ref), custom_call_target="tpu_custom_call" | custom-call | tf_op jit(solution)/shard_map/pallas_call | solution.py:192
  196.7 1.3 slice.192
  198.6 1.2 slice.190
  (269 shorter events, 45.7 us)
Async XLA Ops:
  0.6 10.7 %copy-start = (s32[256,256]{1,0:T(8,128)S(1)}, s32[256,256]{1,0:T(8,128)}, u32[]{:S(2)}) copy-start(s32[256,256]{1,0:T(8,128)} %param.17) | copy-start | bytes 786436
  1.4 16.6 %copy-start.64 = (f32[8]{0:T(128)}, f32[8]{0:T(128)S(1)}, u32[]{:S(2)}) copy-start(f32[8]{0:T(128)S(1)} %broadcast_add_fusion) | copy-start | bytes 100
  3.4 16.5 %copy-start.51 = (f32[4]{0:T(128)}, f32[4]{0:T(128)S(1)}, u32[]{:S(2)}) copy-start(f32[4]{0:T(128)S(1)} %get-tuple-element.10) | copy-start | bytes 52
  8.1 11.9 %copy-start.8 = (f32[64,64]{1,0:T(8,128)}, f32[64,64]{1,0:T(8,128)S(1)}, u32[]{:S(2)}) copy-start(f32[64,64]{1,0:T(8,128)S(1)} %fusion.64) | copy-start | bytes 49156
  9.7 6.9 %copy-start.40 = (f32[64,64]{1,0:T(8,128)}, f32[64,64]{1,0:T(8,128)S(1)}, u32[]{:S(2)}) copy-start(f32[64,64]{1,0:T(8,128)S(1)} %fusion.63) | copy-start | bytes 49156
  10.7 5.9 %copy-start.45 = (f32[8,64]{0,1:T(8,128)}, f32[8,64]{0,1:T(8,128)S(1)}, u32[]{:S(2)}) copy-start(f32[8,64]{0,1:T(8,128)S(1)} %fusion.29) | copy-start | bytes 6148
  10.8 7.2 %copy-start.66 = (f32[8]{0:T(128)}, f32[8]{0:T(128)S(1)}, u32[]{:S(2)}) copy-start(f32[8]{0:T(128)S(1)} %multiply_reduce_fusion.10) | copy-start | bytes 100
  18.8 35.2 %copy-start.28 = (f32[4,64,64]{2,1,0:T(8,128)}, f32[4,64,64]{2,1,0:T(8,128)S(1)}, u32[]{:S(2)}) copy-start(f32[4,64,64]{2,1,0:T(8,128)S(1)} %fusion.20) | copy-start | bytes 196612
  19.1 34.9 %copy-start.30 = (f32[4,64,64]{2,1,0:T(8,128)}, f32[4,64,64]{2,1,0:T(8,128)S(1)}, u32[]{:S(2)}) copy-start(f32[4,64,64]{2,1,0:T(8,128)S(1)} %fusion.19) | copy-start | bytes 196612
  19.4 34.6 %copy-start.32 = (f32[4,64,64]{2,1,0:T(8,128)}, f32[4,64,64]{2,1,0:T(8,128)S(1)}, u32[]{:S(2)}) copy-start(f32[4,64,64]{2,1,0:T(8,128)S(1)} %fusion.18) | copy-start | bytes 196612
  19.7 34.4 %copy-start.34 = (f32[4,64,64]{2,1,0:T(8,128)}, f32[4,64,64]{2,1,0:T(8,128)S(1)}, u32[]{:S(2)}) copy-start(f32[4,64,64]{2,1,0:T(8,128)S(1)} %fusion.17) | copy-start | bytes 196612
  21.7 35.5 %copy-start.10 = (f32[4,64,64]{2,1,0:T(8,128)}, f32[4,64,64]{2,1,0:T(8,128)S(1)}, u32[]{:S(2)}) copy-start(f32[4,64,64]{2,1,0:T(8,128)S(1)} %fusion.80) | copy-start | bytes 196612
  21.9 35.3 %copy-start.12 = (f32[4,64,64]{2,1,0:T(8,128)}, f32[4,64,64]{2,1,0:T(8,128)S(1)}, u32[]{:S(2)}) copy-start(f32[4,64,64]{2,1,0:T(8,128)S(1)} %fusion.81) | copy-start | bytes 196612
  49.6 7.7 %slice-start = ((f32[32,128,128]{2,1,0:T(8,128)}), f32[16,128,128]{2,1,0:T(8,128)S(1)}, s32[]{:S(2)}) async-start(f32[32,128,128]{2,1,0:T(8,128)} %shard_map.174), calls=%async_computation | async-start | bytes 2097152 | tf_op jit(solution)/shard_map/slice | solution.py:83
  57.6 4.6 %copy-start.6 = (f32[32,64,64]{2,1,0:T(8,128)S(1)}, f32[32,64,64]{2,1,0:T(8,128)}, u32[]{:S(2)}) copy-start(f32[32,64,64]{2,1,0:T(8,128)} %slice.144) | copy-start | bytes 1572868
  89.9 7.4 %copy-start.5 = (f32[8,64,256]{2,1,0:T(8,128)S(1)}, f32[8,64,256]{2,1,0:T(8,128)}, u32[]{:S(2)}) copy-start(f32[8,64,256]{2,1,0:T(8,128)} %copy-done.4) | copy-start | bytes 1572868
  104.2 4.6 %copy-start.3 = (f32[64,64,256]{2,1,0:T(8,128)S(1)}, f32[64,64,256]{2,1,0:T(8,128)}, u32[]{:S(2)}) copy-start(f32[64,64,256]{2,1,0:T(8,128)} %copy-done.2) | copy-start | bytes 12582916
  116.7 4.8 %copy-start.39 = (f32[1,64,256]{2,1,0:T(8,128)S(1)}, f32[1,64,256]{2,1,0:T(8,128)}, u32[]{:S(2)}) copy-start(f32[1,64,256]{2,1,0:T(8,128)} %get-tuple-element.12) | copy-start | bytes 196612
  116.7 4.8 %copy-start.68 = (f32[256]{0:T(256)S(1)}, f32[256]{0:T(256)}, u32[]{:S(2)}) copy-start(f32[256]{0:T(256)} %get-tuple-element.39) | copy-start | bytes 3076
  116.7 5.5 %copy-start.50 = (f32[16,256]{1,0:T(8,128)S(1)}, f32[16,256]{1,0:T(8,128)}, u32[]{:S(2)}) copy-start(f32[16,256]{1,0:T(8,128)} %copy-done.49) | copy-start | bytes 49156
  118.2 5.1 %copy-start.54 = (f32[8,256]{1,0:T(8,128)S(1)}, f32[8,256]{1,0:T(8,128)}, u32[]{:S(2)}) copy-start(f32[8,256]{1,0:T(8,128)} %copy-done.53) | copy-start | bytes 24580
  118.2 6.0 %copy-start.57 = (f32[4,256]{1,0:T(4,128)S(1)}, f32[4,256]{1,0:T(4,128)}, u32[]{:S(2)}) copy-start(f32[4,256]{1,0:T(4,128)} %copy-done.56) | copy-start | bytes 12292
  119.3 5.6 %copy-start.61 = (f32[2,256]{1,0:T(2,128)S(1)}, f32[2,256]{1,0:T(2,128)}, u32[]{:S(2)}) copy-start(f32[2,256]{1,0:T(2,128)} %copy-done.60) | copy-start | bytes 6148
  119.3 6.3 %copy-start.21 = (f32[2,64,256]{2,1,0:T(8,128)S(1)}, f32[2,64,256]{2,1,0:T(8,128)}, u32[]{:S(2)}) copy-start(f32[2,64,256]{2,1,0:T(8,128)} %copy-done.20) | copy-start | bytes 393220
  119.3 6.3 %copy-start.63 = (f32[256]{0:T(256)S(1)}, f32[256]{0:T(256)}, u32[]{:S(2)}) copy-start(f32[256]{0:T(256)} %copy-done.62) | copy-start | bytes 3076
  138.5 30.4 %copy-start.15 = (f32[4,64,64]{2,1,0:T(8,128)S(1)}, f32[4,64,64]{2,1,0:T(8,128)}, u32[]{:S(2)}) copy-start(f32[4,64,64]{2,1,0:T(8,128)} %copy-done.14) | copy-start | bytes 196612
  138.5 30.9 %copy-start.13 = (f32[4,64,64]{2,1,0:T(8,128)S(1)}, f32[4,64,64]{2,1,0:T(8,128)}, u32[]{:S(2)}) copy-start(f32[4,64,64]{2,1,0:T(8,128)} %copy-done.12) | copy-start | bytes 196612
  138.5 31.5 %copy-start.11 = (f32[4,64,64]{2,1,0:T(8,128)S(1)}, f32[4,64,64]{2,1,0:T(8,128)}, u32[]{:S(2)}) copy-start(f32[4,64,64]{2,1,0:T(8,128)} %copy-done.10) | copy-start | bytes 196612
  138.5 32.1 %copy-start.17 = (f32[4,64,64]{2,1,0:T(8,128)S(1)}, f32[4,64,64]{2,1,0:T(8,128)}, u32[]{:S(2)}) copy-start(f32[4,64,64]{2,1,0:T(8,128)} %copy-done.16) | copy-start | bytes 196612
  143.3 27.9 %copy-start.23 = (f32[4,64,64]{2,1,0:T(8,128)S(1)}, f32[4,64,64]{2,1,0:T(8,128)}, u32[]{:S(2)}) copy-start(f32[4,64,64]{2,1,0:T(8,128)} %copy-done.22) | copy-start | bytes 196612
  143.3 28.2 %copy-start.52 = (f32[4]{0:T(128)S(1)}, f32[4]{0:T(128)}, u32[]{:S(2)}) copy-start(f32[4]{0:T(128)} %copy-done.51) | copy-start | bytes 52
  143.3 28.5 %copy-start.35 = (f32[4,64,64]{2,1,0:T(8,128)S(1)}, f32[4,64,64]{2,1,0:T(8,128)}, u32[]{:S(2)}) copy-start(f32[4,64,64]{2,1,0:T(8,128)} %copy-done.34) | copy-start | bytes 196612
  143.3 29.2 %copy-start.33 = (f32[4,64,64]{2,1,0:T(8,128)S(1)}, f32[4,64,64]{2,1,0:T(8,128)}, u32[]{:S(2)}) copy-start(f32[4,64,64]{2,1,0:T(8,128)} %copy-done.32) | copy-start | bytes 196612
  143.3 29.8 %copy-start.31 = (f32[4,64,64]{2,1,0:T(8,128)S(1)}, f32[4,64,64]{2,1,0:T(8,128)}, u32[]{:S(2)}) copy-start(f32[4,64,64]{2,1,0:T(8,128)} %copy-done.30) | copy-start | bytes 196612
  167.9 5.8 %copy-start.29 = (f32[4,64,64]{2,1,0:T(8,128)S(1)}, f32[4,64,64]{2,1,0:T(8,128)}, u32[]{:S(2)}) copy-start(f32[4,64,64]{2,1,0:T(8,128)} %copy-done.28) | copy-start | bytes 196612
  167.9 6.4 %copy-start.27 = (f32[4,64,64]{2,1,0:T(8,128)S(1)}, f32[4,64,64]{2,1,0:T(8,128)}, u32[]{:S(2)}) copy-start(f32[4,64,64]{2,1,0:T(8,128)} %copy-done.26) | copy-start | bytes 196612
  169.5 5.5 %copy-start.25 = (f32[4,64,64]{2,1,0:T(8,128)S(1)}, f32[4,64,64]{2,1,0:T(8,128)}, u32[]{:S(2)}) copy-start(f32[4,64,64]{2,1,0:T(8,128)} %copy-done.24) | copy-start | bytes 196612
  170.0 5.5 %copy-start.9 = (f32[64,64]{1,0:T(8,128)S(1)}, f32[64,64]{1,0:T(8,128)}, u32[]{:S(2)}) copy-start(f32[64,64]{1,0:T(8,128)} %copy-done.8) | copy-start | bytes 49156
  170.0 5.5 %copy-start.69 = (f32[4]{0:T(128)S(1)}, f32[4]{0:T(128)}, u32[]{:S(2)}) copy-start(f32[4]{0:T(128)} %get-tuple-element.9) | copy-start | bytes 52
  170.3 5.9 %copy-start.41 = (f32[64,64]{1,0:T(8,128)S(1)}, f32[64,64]{1,0:T(8,128)}, u32[]{:S(2)}) copy-start(f32[64,64]{1,0:T(8,128)} %copy-done.40) | copy-start | bytes 49156
  170.3 5.9 %copy-start.46 = (f32[8,64]{0,1:T(8,128)S(1)}, f32[8,64]{0,1:T(8,128)}, u32[]{:S(2)}) copy-start(f32[8,64]{0,1:T(8,128)} %copy-done.45) | copy-start | bytes 6148
  170.3 5.9 %copy-start.47 = (f32[64,64]{1,0:T(8,128)S(1)}, f32[64,64]{1,0:T(8,128)}, u32[]{:S(2)}) copy-start(f32[64,64]{1,0:T(8,128)} %constant.112) | copy-start | bytes 49156
  170.4 5.9 %copy-start.48 = (f32[64,64]{1,0:T(8,128)S(1)}, f32[64,64]{1,0:T(8,128)}, u32[]{:S(2)}) copy-start(f32[64,64]{1,0:T(8,128)} %constant.111) | copy-start | bytes 49156
  170.4 5.9 %copy-start.65 = (f32[8]{0:T(128)S(1)}, f32[8]{0:T(128)}, u32[]{:S(2)}) copy-start(f32[8]{0:T(128)} %copy-done.64) | copy-start | bytes 100
  170.4 5.9 %copy-start.67 = (f32[8]{0:T(128)S(1)}, f32[8]{0:T(128)}, u32[]{:S(2)}) copy-start(f32[8]{0:T(128)} %copy-done.66) | copy-start | bytes 100
  170.4 5.9 %copy-start.70 = (f32[8]{0:T(128)S(1)}, f32[8]{0:T(128)}, u32[]{:S(2)}) copy-start(f32[8]{0:T(128)} %multiply_divide_fusion.7) | copy-start | bytes 100
  171.4 6.1 %copy-start.59 = (f32[64]{0:T(128)S(1)}, f32[64]{0:T(128)}, u32[]{:S(2)}) copy-start(f32[64]{0:T(128)} %copy-done.58) | copy-start | bytes 772
  171.8 30.6 %copy-start.1 = (s32[256,256]{1,0:T(8,128)S(1)}, s32[256,256]{1,0:T(8,128)}, u32[]{:S(2)}) copy-start(s32[256,256]{1,0:T(8,128)} %param.17) | copy-start | bytes 786436
  (24 other events, 44.8 us)

commit v6 on v3

--- a/solution.py
+++ b/solution.py
@@ -491,13 +491,22 @@
         return carry
 
     lax.fori_loop(1, chips, second_sent, 0)
-    o_ref[...] = held[...]
+    per = o_ref.shape[0] // n
+    width = o_ref.shape[2]
+
+    def unpack(p, carry):
+        for q in range(per):
+            o_ref[per * p + q] = held[p, :, q * width : (q + 1) * width]
+        return carry
+
+    lax.fori_loop(0, n, unpack, 0)
 
 
 def pair_gather(x, n, collective_id):
+    per = x.shape[1] // x.shape[0]
     return pl.pallas_call(
         pair_gather_kernel,
-        out_shape=jax.ShapeDtypeStruct((n,) + x.shape, jnp.float32),
+        out_shape=jax.ShapeDtypeStruct((n * per, x.shape[0], x.shape[0]), jnp.float32),
         in_specs=[pl.BlockSpec(memory_space=pltpu.VMEM)],
         out_specs=pl.BlockSpec(memory_space=pltpu.VMEM),
         scratch_shapes=[
@@ -533,8 +542,8 @@
     own_scaled = lax.dynamic_slice_in_dim(scaled, own_start, per_dev, 0)
     own_pull = None
     own_probs, own_pull = jax.vjp(expm_taylor, own_scaled)
-    dense = pair_gather(own_probs.reshape(-1, 128), site_count, 1)
-    probs = dense.reshape((site_count * per_dev,) + own_probs.shape[1:])
+    packed_probs = own_probs.transpose(1, 0, 2).reshape(own_probs.shape[1], -1)
+    probs = pair_gather(packed_probs, site_count, 1)
     taxon_rows = lax.dynamic_slice_in_dim(leaf_order, subtree * LEAF_DEV, LEAF_DEV, 0)
     leaves = leaf_partials(
         jnp.take(states, taxon_rows, axis=0), jnp.take(gap_mask, taxon_rows, axis=0)

time: 205 us -> 189 us (0.922)
  local copies, waits for them, and re-layouts: 34.5 us -> 23.1 us
  other arithmetic: 48.4 us -> 43.9 us
  Pallas kernels: 67.7 us -> 70.9 us
  matrix products: 37.7 us -> 35 us
    slice x11 -> x0, local copies, waits for them, and re-layouts: 7.92 us -> none  [the longest x8 7.58 us: down_pass(): down_part = carried(probs[offset:offset + amount], current)]
    reshape x2 -> x1, local copies, waits for them, and re-layouts: 5.03 us -> 0.77 us  [body(): packed_probs = own_probs.transpose(1, 0, 2).reshape(own_probs.shape[1], -1)]
    reduce_sum x5, other arithmetic: 3.42 us -> 0.12 us  [up_pass(): logscale = logscale + jnp.sum(jnp.log(scaling), axis=0)]
    pallas_call x1, Pallas kernels: 25.9 us -> 29.1 us  [pair_gather(): pl.pallas_call(pair_gather_kernel, out_shape=jax.ShapeDtypeStruct((n * pe...]
    dot_general x7, matrix products: 7.44 us -> 4.67 us  [forward(): jnp.einsum('bij,bjs->bis', probs, vectors, precision=lax.Precision.HIGH)]
where the time goes in v6:
time: 189 us; the launch traced here: 188 us
  Pallas kernels  70.9 us (38%)
  other arithmetic  43.9 us (23%)
  matrix products  35 us (19%)
  local copies, waits for them, and re-layouts  23.1 us (12%)
  blocking collectives  10.3 us (5%)
  between operations  4.54 us (2%)
    pallas_call x1, Pallas kernels, pair_gather(): pl.pallas_call(pair_gather_kernel, out_shape=jax.ShapeDtypeStruct((n * pe...  29.1 us
    pallas_call x1, Pallas kernels, pair_scatter(): pl.pallas_call(pair_scatter_kernel, out_shape=jax.ShapeDtypeStruct(chunk,...  24.6 us
    pallas_call x1, Pallas kernels, allreduce_all(): pl.pallas_call(functools.partial(allreduce_kernel, n_site, n_branch), out...  17.2 us
    unnamed x14, other arithmetic  15.6 us
    dot_general x1, matrix products, body(): jnp.einsum('bis,bjs->bij', part_above, part_below, precision=lax.Precisio...  11.7 us
    all_gather x1, blocking collectives, body(): top_all = lax.all_gather(top_pack, 'branch', axis=0, tiled=False)  10.3 us
    dot_general x35, matrix products, product(): return jnp.einsum('bij,bjk->bik', left, right, precision=lax.Precision.HIGH)  9.43 us
    unnamed x144, local copies, waits for them, and re-layouts  6.24 us

profile of v6, /device:TPU:1, one launch (start us, length us, event | category | flops | bytes accessed | tf_op | source)
XLA Modules:
  0.0 187.7 jit_solution(5515370708715516782)
XLA Ops:
  1.4 0.7 pad_add_fusion
  2.1 0.7 pad_maximum_fusion.5
  3.4 0.8 compare_and_fusion
  4.2 1.2 convert_element_type.44
  5.4 1.3 fusion.82
  8.1 0.8 copy.143
  8.9 0.8 fusion.65
  9.7 1.0 fusion.29
  12.1 1.6 gather_fusion
  13.8 2.2 %fusion.27 = f32[128,64,64]{0,2,1:T(8,128)S(1)} fusion(f32[8]{0:T(128)S(1)} %multiply_reduce_fusion.10, f32[64,64]{1,0:T(8,128)S(1)} %fusion.66, f32[8,64]{0,1:T(8,128)S(1)} %fusion.29, f32[64,64]{1,0:T(8,128)} %constant.112, f32[8]{0:T(128)S(1)} %broadcast_add_fusion, f32[64,64]{1,0:T(8,128)} %constant.111, f32[64,64]{1,0:T(8,128)S(1)} %fusion.65, ...), kind=kOutput, calls=%fused_computation.96 | convolution fusion | flops 25396224 | bytes 2165312 | tf_op jit(solution)/shard_map/bc,cij->bij/dot_general | solution.py:538
  22.6 0.8 reshape.314.x_ref
  23.4 29.1 %shard_map.174 = f32[128,64,64]{2,1,0:T(8,128)} custom-call(f32[64,256]{1,0:T(8,128)} %reshape.314.x_ref), custom_call_target="tpu_custom_call" | custom-call | tf_op jit(solution)/shard_map/pallas_call | solution.py:507
  52.5 0.9 convert_select_fusion.4
  53.5 1.2 copy-done.2
  54.7 2.0 %fusion.7 = f32[64,64,256]{2,1,0:T(8,128)S(1)} fusion(f32[128,64,64]{2,1,0:T(8,128)S(1)} %copy-done.2, f32[64,64,256]{2,1,0:T(8,128)S(1)} %convert_select_fusion.4), kind=kOutput, calls=%fused_computation.13 | convolution fusion | flops 402653184 | bytes 10485760 | tf_op jit(solution)/shard_map/bij,bjs->bis/dot_general | solution.py:62
  57.2 1.1 fusion.24
  61.7 10.3 %all-gather.1 = f32[4,65,256]{2,1,0:T(8,128)S(1)} all-gather(f32[1,65,256]{2,1,0:T(8,128)S(1)} %maximum_bitcast_fusion.2), channel_id=2, replica_groups=mesh['site'=32,'branch'=4] {'branch'}, dimensions={0}, use_global_device_ids=true | all-gather | bytes 332800 | tf_op jit(solution)/shard_map/all_gather | solution.py:553
  72.9 1.2 multiply_reduce_fusion.11
  74.8 1.2 fusion.83
  75.9 0.9 fusion.50
  76.8 0.9 multiply_reduce_fusion.9
  78.4 1.1 fusion.44
  79.8 1.1 multiply_reduce_fusion.7
  80.9 0.8 multiply_divide_fusion.4
  81.7 1.2 fusion.93
  85.6 1.0 fusion.12
  87.3 1.2 fusion.96
  88.5 1.9 fusion.11
  90.8 2.7 %fusion.6 = f32[128,64,256]{2,1,0:T(8,128)} fusion(s32[64,256]{1,0:T(8,128)S(1)} %copy-done.37, pred[64,256]{1,0:T(8,128)(4,1)S(1)} %select_compare_fusion), kind=kLoop, calls=%fused_computation.12 | loop fusion | flops 3145727 | bytes 4276224
  93.5 2.4 %multiply_bitcast_fusion.1 = (f32[32,1,64,256]{3,2,0,1:T(8,128)S(1)}, f32[32,1,64,256]{3,2,0,1:T(8,128)S(1)}, f32[128,64,256]{2,1,0:T(8,128)}) fusion(f32[32,64,256]{2,1,0:T(8,128)S(1)} %fusion.11, f32[64,64,256]{2,1,0:T(8,128)S(1)} %copy-done.5, f32[128,64,256]{2,1,0:T(8,128)} %fusion.6, f32[32,256]{1,0:T(8,128)S(1)} %copy-done.42), kind=kLoop, calls=%fused_computation.19 | loop fusion | flops 2097152 | bytes 12615680 | tf_op jit(solution)/shard_map/stack | solution.py:119
  96.5 1.4 fusion.5
  98.0 3.4 %constant_dynamic-update-slice_fusion.1 = f32[128,64,256]{2,1,0:T(8,128)} fusion(f32[64,256]{1,0:T(8,128)S(1)} %multiply_divide_fusion, f32[32,2,64,256]{3,2,1,0:T(8,128)S(1)} %copy.156), kind=kLoop, calls=%fused_computation.166 | loop fusion | flops 1048575 | bytes 8454144
  101.3 1.5 multiply_dynamic-update-slice_fusion
  102.9 1.1 multiply_dynamic-update-slice_fusion.1
  104.0 0.8 multiply_dynamic-update-slice_fusion.2
  104.8 0.7 multiply_dynamic-update-slice_fusion.3
  106.8 1.2 fusion.25
  108.0 0.9 fusion.30
  108.9 0.7 fusion.42
  111.5 11.7 %fusion.87 = f32[128,64,64]{2,1,0:T(8,128)} fusion(f32[128,64,256]{2,1,0:T(8,128)} %get-tuple-element.43, f32[128,64,256]{2,1,0:T(8,128)} %get-tuple-element.44), kind=kOutput, calls=%fused_computation.231 | convolution fusion | flops 805306368 | bytes 18874368 | tf_op jit(solution)/shard_map/bis,bjs->bij/dot_general | solution.py:566
  123.2 4.7 %reshape.324.x_ref = f32[32,128,128]{2,1,0:T(8,128)} reshape(f32[128,64,64]{2,1,0:T(8,128)} %fusion.87) | data formatting | bytes 4194304 | tf_op jit(solution)/shard_map/reshape | solution.py:567
  128.0 24.6 %shard_map.175 = f32[128,128]{1,0:T(8,128)} custom-call(f32[32,128,128]{2,1,0:T(8,128)} %reshape.324.x_ref), custom_call_target="tpu_custom_call" | custom-call | tf_op jit(solution)/shard_map/pallas_call | solution.py:379
  152.6 1.0 reshape.325
  161.0 1.2 multiply_reduce_fusion.5
  163.6 17.2 %shard_map.176 = f32[40,128]{1,0:T(8,128)} custom-call(f32[40,128]{1,0:T(8,128)} %pad_bitcast_fusion.x_ref), custom_call_target="tpu_custom_call" | custom-call | tf_op jit(solution)/shard_map/pallas_call | solution.py:193
  180.8 1.3 slice.171
  182.7 1.2 slice.169
  183.9 0.7 slice_bitcast_fusion
  (259 shorter events, 33.7 us)
Async XLA Ops:
  0.6 10.7 %copy-start = (s32[256,256]{1,0:T(8,128)S(1)}, s32[256,256]{1,0:T(8,128)}, u32[]{:S(2)}) copy-start(s32[256,256]{1,0:T(8,128)} %param.17) | copy-start | bytes 786436
  1.4 16.0 %copy-start.63 = (f32[8]{0:T(128)}, f32[8]{0:T(128)S(1)}, u32[]{:S(2)}) copy-start(f32[8]{0:T(128)S(1)} %broadcast_add_fusion) | copy-start | bytes 100
  3.4 15.9 %copy-start.49 = (f32[4]{0:T(128)}, f32[4]{0:T(128)S(1)}, u32[]{:S(2)}) copy-start(f32[4]{0:T(128)S(1)} %get-tuple-element.10) | copy-start | bytes 52
  8.1 11.3 %copy-start.10 = (f32[64,64]{1,0:T(8,128)}, f32[64,64]{1,0:T(8,128)S(1)}, u32[]{:S(2)}) copy-start(f32[64,64]{1,0:T(8,128)S(1)} %fusion.66) | copy-start | bytes 49156
  9.7 6.4 %copy-start.39 = (f32[64,64]{1,0:T(8,128)}, f32[64,64]{1,0:T(8,128)S(1)}, u32[]{:S(2)}) copy-start(f32[64,64]{1,0:T(8,128)S(1)} %fusion.65) | copy-start | bytes 49156
  10.7 5.3 %copy-start.43 = (f32[8,64]{0,1:T(8,128)}, f32[8,64]{0,1:T(8,128)S(1)}, u32[]{:S(2)}) copy-start(f32[8,64]{0,1:T(8,128)S(1)} %fusion.29) | copy-start | bytes 6148
  10.8 6.6 %copy-start.65 = (f32[8]{0:T(128)}, f32[8]{0:T(128)S(1)}, u32[]{:S(2)}) copy-start(f32[8]{0:T(128)S(1)} %multiply_reduce_fusion.10) | copy-start | bytes 100
  12.1 40.4 %copy-start.36 = (s32[64,256]{1,0:T(8,128)}, s32[64,256]{1,0:T(8,128)S(1)}, u32[]{:S(2)}) copy-start(s32[64,256]{1,0:T(8,128)S(1)} %broadcast_select_fusion) | copy-start | bytes 196612
  18.5 3.9 %copy-start.30 = (f32[4,64,64]{2,1,0:T(8,128)}, f32[4,64,64]{2,1,0:T(8,128)S(1)}, u32[]{:S(2)}) copy-start(f32[4,64,64]{2,1,0:T(8,128)S(1)} %fusion.19) | copy-start | bytes 196612
  21.2 32.3 %copy-start.12 = (f32[4,64,64]{2,1,0:T(8,128)}, f32[4,64,64]{2,1,0:T(8,128)S(1)}, u32[]{:S(2)}) copy-start(f32[4,64,64]{2,1,0:T(8,128)S(1)} %fusion.84) | copy-start | bytes 196612
  21.4 32.1 %copy-start.14 = (f32[4,64,64]{2,1,0:T(8,128)}, f32[4,64,64]{2,1,0:T(8,128)S(1)}, u32[]{:S(2)}) copy-start(f32[4,64,64]{2,1,0:T(8,128)S(1)} %fusion.85) | copy-start | bytes 196612
  59.5 12.6 %copy-start.57 = (f32[64]{0:T(128)S(1)}, f32[64]{0:T(128)}, u32[]{:S(2)}) copy-start(f32[64]{0:T(128)} %copy-done.56) | copy-start | bytes 772
  59.5 13.4 %copy-start.68 = (s32[256]{0:T(256)S(1)}, s32[256]{0:T(256)}, u32[]{:S(2)}) copy-start(s32[256]{0:T(256)} %param.19) | copy-start | bytes 3076
  60.5 19.2 %copy-start.8 = (f32[4,64,256]{2,1,0:T(8,128)}, f32[4,64,256]{2,1,0:T(8,128)S(1)}, u32[]{:S(2)}) copy-start(f32[4,64,256]{2,1,0:T(8,128)S(1)} %fusion.43) | copy-start | bytes 786436
  74.7 8.4 %copy-start.7 = (f32[8,64,256]{2,1,0:T(8,128)S(1)}, f32[8,64,256]{2,1,0:T(8,128)}, u32[]{:S(2)}) copy-start(f32[8,64,256]{2,1,0:T(8,128)} %copy-done.6) | copy-start | bytes 1572868
  79.7 3.7 %copy-start.3 = (f32[128,64,64]{2,1,0:T(8,128)S(1)}, f32[128,64,64]{2,1,0:T(8,128)}, u32[]{:S(2)}) copy-start(f32[128,64,64]{2,1,0:T(8,128)} %shard_map.174) | copy-start | bytes 6291460
  101.3 4.8 %copy-start.38 = (f32[1,64,256]{2,1,0:T(8,128)S(1)}, f32[1,64,256]{2,1,0:T(8,128)}, u32[]{:S(2)}) copy-start(f32[1,64,256]{2,1,0:T(8,128)} %get-tuple-element.12) | copy-start | bytes 196612
  101.3 4.8 %copy-start.67 = (f32[256]{0:T(256)S(1)}, f32[256]{0:T(256)}, u32[]{:S(2)}) copy-start(f32[256]{0:T(256)} %get-tuple-element.39) | copy-start | bytes 3076
  101.3 5.5 %copy-start.48 = (f32[16,256]{1,0:T(8,128)S(1)}, f32[16,256]{1,0:T(8,128)}, u32[]{:S(2)}) copy-start(f32[16,256]{1,0:T(8,128)} %copy-done.47) | copy-start | bytes 49156
  102.9 5.1 %copy-start.52 = (f32[8,256]{1,0:T(8,128)S(1)}, f32[8,256]{1,0:T(8,128)}, u32[]{:S(2)}) copy-start(f32[8,256]{1,0:T(8,128)} %copy-done.51) | copy-start | bytes 24580
  102.9 6.0 %copy-start.55 = (f32[4,256]{1,0:T(4,128)S(1)}, f32[4,256]{1,0:T(4,128)}, u32[]{:S(2)}) copy-start(f32[4,256]{1,0:T(4,128)} %copy-done.54) | copy-start | bytes 12292
  104.0 5.6 %copy-start.9 = (f32[4,64,256]{2,1,0:T(8,128)S(1)}, f32[4,64,256]{2,1,0:T(8,128)}, u32[]{:S(2)}) copy-start(f32[4,64,256]{2,1,0:T(8,128)} %copy-done.8) | copy-start | bytes 786436
  104.0 5.6 %copy-start.60 = (f32[2,256]{1,0:T(2,128)S(1)}, f32[2,256]{1,0:T(2,128)}, u32[]{:S(2)}) copy-start(f32[2,256]{1,0:T(2,128)} %copy-done.59) | copy-start | bytes 6148
  104.0 6.3 %copy-start.21 = (f32[2,64,256]{2,1,0:T(8,128)S(1)}, f32[2,64,256]{2,1,0:T(8,128)}, u32[]{:S(2)}) copy-start(f32[2,64,256]{2,1,0:T(8,128)} %copy-done.20) | copy-start | bytes 393220
  104.0 6.3 %copy-start.62 = (f32[256]{0:T(256)S(1)}, f32[256]{0:T(256)}, u32[]{:S(2)}) copy-start(f32[256]{0:T(256)} %copy-done.61) | copy-start | bytes 3076
  123.2 30.4 %copy-start.17 = (f32[4,64,64]{2,1,0:T(8,128)S(1)}, f32[4,64,64]{2,1,0:T(8,128)}, u32[]{:S(2)}) copy-start(f32[4,64,64]{2,1,0:T(8,128)} %copy-done.16) | copy-start | bytes 196612
  123.2 30.9 %copy-start.15 = (f32[4,64,64]{2,1,0:T(8,128)S(1)}, f32[4,64,64]{2,1,0:T(8,128)}, u32[]{:S(2)}) copy-start(f32[4,64,64]{2,1,0:T(8,128)} %copy-done.14) | copy-start | bytes 196612
  123.2 31.5 %copy-start.13 = (f32[4,64,64]{2,1,0:T(8,128)S(1)}, f32[4,64,64]{2,1,0:T(8,128)}, u32[]{:S(2)}) copy-start(f32[4,64,64]{2,1,0:T(8,128)} %copy-done.12) | copy-start | bytes 196612
  123.2 32.1 %copy-start.19 = (f32[4,64,64]{2,1,0:T(8,128)S(1)}, f32[4,64,64]{2,1,0:T(8,128)}, u32[]{:S(2)}) copy-start(f32[4,64,64]{2,1,0:T(8,128)} %copy-done.18) | copy-start | bytes 196612
  128.0 27.9 %copy-start.23 = (f32[4,64,64]{2,1,0:T(8,128)S(1)}, f32[4,64,64]{2,1,0:T(8,128)}, u32[]{:S(2)}) copy-start(f32[4,64,64]{2,1,0:T(8,128)} %copy-done.22) | copy-start | bytes 196612
  128.0 28.2 %copy-start.50 = (f32[4]{0:T(128)S(1)}, f32[4]{0:T(128)}, u32[]{:S(2)}) copy-start(f32[4]{0:T(128)} %copy-done.49) | copy-start | bytes 52
  128.0 28.5 %copy-start.35 = (f32[4,64,64]{2,1,0:T(8,128)S(1)}, f32[4,64,64]{2,1,0:T(8,128)}, u32[]{:S(2)}) copy-start(f32[4,64,64]{2,1,0:T(8,128)} %copy-done.34) | copy-start | bytes 196612
  128.0 29.2 %copy-start.33 = (f32[4,64,64]{2,1,0:T(8,128)S(1)}, f32[4,64,64]{2,1,0:T(8,128)}, u32[]{:S(2)}) copy-start(f32[4,64,64]{2,1,0:T(8,128)} %copy-done.32) | copy-start | bytes 196612
  128.0 29.8 %copy-start.31 = (f32[4,64,64]{2,1,0:T(8,128)S(1)}, f32[4,64,64]{2,1,0:T(8,128)}, u32[]{:S(2)}) copy-start(f32[4,64,64]{2,1,0:T(8,128)} %copy-done.30) | copy-start | bytes 196612
  152.6 5.8 %copy-start.29 = (f32[4,64,64]{2,1,0:T(8,128)S(1)}, f32[4,64,64]{2,1,0:T(8,128)}, u32[]{:S(2)}) copy-start(f32[4,64,64]{2,1,0:T(8,128)} %copy-done.28) | copy-start | bytes 196612
  152.6 6.4 %copy-start.27 = (f32[4,64,64]{2,1,0:T(8,128)S(1)}, f32[4,64,64]{2,1,0:T(8,128)}, u32[]{:S(2)}) copy-start(f32[4,64,64]{2,1,0:T(8,128)} %copy-done.26) | copy-start | bytes 196612
  154.1 5.5 %copy-start.25 = (f32[4,64,64]{2,1,0:T(8,128)S(1)}, f32[4,64,64]{2,1,0:T(8,128)}, u32[]{:S(2)}) copy-start(f32[4,64,64]{2,1,0:T(8,128)} %copy-done.24) | copy-start | bytes 196612
  154.7 5.5 %copy-start.11 = (f32[64,64]{1,0:T(8,128)S(1)}, f32[64,64]{1,0:T(8,128)}, u32[]{:S(2)}) copy-start(f32[64,64]{1,0:T(8,128)} %copy-done.10) | copy-start | bytes 49156
  154.7 5.5 %copy-start.69 = (f32[4]{0:T(128)S(1)}, f32[4]{0:T(128)}, u32[]{:S(2)}) copy-start(f32[4]{0:T(128)} %get-tuple-element.9) | copy-start | bytes 52
  155.0 5.9 %copy-start.40 = (f32[64,64]{1,0:T(8,128)S(1)}, f32[64,64]{1,0:T(8,128)}, u32[]{:S(2)}) copy-start(f32[64,64]{1,0:T(8,128)} %copy-done.39) | copy-start | bytes 49156
  155.0 5.9 %copy-start.44 = (f32[8,64]{0,1:T(8,128)S(1)}, f32[8,64]{0,1:T(8,128)}, u32[]{:S(2)}) copy-start(f32[8,64]{0,1:T(8,128)} %copy-done.43) | copy-start | bytes 6148
  155.0 5.9 %copy-start.45 = (f32[64,64]{1,0:T(8,128)S(1)}, f32[64,64]{1,0:T(8,128)}, u32[]{:S(2)}) copy-start(f32[64,64]{1,0:T(8,128)} %constant.112) | copy-start | bytes 49156
  155.0 5.9 %copy-start.46 = (f32[64,64]{1,0:T(8,128)S(1)}, f32[64,64]{1,0:T(8,128)}, u32[]{:S(2)}) copy-start(f32[64,64]{1,0:T(8,128)} %constant.111) | copy-start | bytes 49156
  155.1 5.9 %copy-start.64 = (f32[8]{0:T(128)S(1)}, f32[8]{0:T(128)}, u32[]{:S(2)}) copy-start(f32[8]{0:T(128)} %copy-done.63) | copy-start | bytes 100
  155.1 5.9 %copy-start.66 = (f32[8]{0:T(128)S(1)}, f32[8]{0:T(128)}, u32[]{:S(2)}) copy-start(f32[8]{0:T(128)} %copy-done.65) | copy-start | bytes 100
  155.1 5.9 %copy-start.70 = (f32[8]{0:T(128)S(1)}, f32[8]{0:T(128)}, u32[]{:S(2)}) copy-start(f32[8]{0:T(128)} %multiply_divide_fusion.7) | copy-start | bytes 100
  156.1 6.1 %copy-start.58 = (f32[64]{0:T(128)S(1)}, f32[64]{0:T(128)}, u32[]{:S(2)}) copy-start(f32[64]{0:T(128)} %copy-done.56) | copy-start | bytes 772
  156.5 30.1 %copy-start.1 = (s32[256,256]{1,0:T(8,128)S(1)}, s32[256,256]{1,0:T(8,128)}, u32[]{:S(2)}) copy-start(s32[256,256]{1,0:T(8,128)} %param.17) | copy-start | bytes 786436
  (23 other events, 40.8 us)

commit v7 on v6

--- a/solution.py
+++ b/solution.py
@@ -287,8 +287,17 @@
     )(x)
 
 
-def pair_scatter_kernel(x_ref, o_ref, pair_buf, pair_sum, held, sems_a, sems_b, sems_c, sems_d):
-    n = x_ref.shape[0]
+def pair_scatter_kernel(x_ref, o_ref, packed, pair_buf, pair_sum, held, sems_a, sems_b, sems_c, sems_d):
+    n = packed.shape[0]
+    per = o_ref.shape[0]
+    width = o_ref.shape[2]
+
+    def pack(p, carry):
+        for q in range(per):
+            packed[p, :, q * width : (q + 1) * width] = x_ref[per * p + q]
+        return carry
+
+    lax.fori_loop(0, n, pack, 0)
     chips = n // 2
     s = lax.axis_index("site")
     k = lax.axis_index("branch")
@@ -308,7 +317,7 @@
 
     def to_partner(m):
         return pltpu.make_async_remote_copy(
-            src_ref=x_ref.at[2 * m + 1 - core],
+            src_ref=packed.at[2 * m + 1 - core],
             dst_ref=pair_buf.at[m],
             send_sem=sems_a.at[m],
             recv_sem=sems_b.at[m],
@@ -333,13 +342,13 @@
         )
 
     to_partner(chip).wait_recv()
-    pair_sum[chip] = x_ref[2 * chip + core] + pair_buf[chip]
+    pair_sum[chip] = packed[2 * chip + core] + pair_buf[chip]
     held[chip] = pair_sum[chip]
 
     def add_and_send(d, carry):
         c = lax.rem(chip + d, chips)
         to_partner(c).wait_recv()
-        pair_sum[c] = x_ref[2 * c + core] + pair_buf[c]
+        pair_sum[c] = packed[2 * c + core] + pair_buf[c]
         to_chip(c).start()
         return carry
 
@@ -370,18 +379,21 @@
         return carry
 
     lax.fori_loop(1, chips, second_sent, 0)
-    o_ref[...] = lax.fori_loop(1, chips, lambda j, acc: acc + held[j], held[0])
-
-
-def pair_scatter(x, collective_id):
-    n = x.shape[0]
-    chunk = x.shape[1:]
+    total = lax.fori_loop(1, chips, lambda j, acc: acc + held[j], held[0])
+    for q in range(per):
+        o_ref[q] = total[:, q * width : (q + 1) * width]
+
+
+def pair_scatter(x, n, collective_id):
+    per = x.shape[0] // n
+    chunk = (x.shape[1], per * x.shape[2])
     return pl.pallas_call(
         pair_scatter_kernel,
-        out_shape=jax.ShapeDtypeStruct(chunk, jnp.float32),
+        out_shape=jax.ShapeDtypeStruct((per,) + x.shape[1:], jnp.float32),
         in_specs=[pl.BlockSpec(memory_space=pltpu.VMEM)],
         out_specs=pl.BlockSpec(memory_space=pltpu.VMEM),
         scratch_shapes=[
+            pltpu.VMEM((n,) + chunk, jnp.float32),
             pltpu.VMEM((n // 2,) + chunk, jnp.float32),
             pltpu.VMEM((n // 2,) + chunk, jnp.float32),
             pltpu.VMEM((n // 2,) + chunk, jnp.float32),
@@ -564,7 +576,7 @@
     part_above = lax.slice_in_dim(weighted_all, 0, lax.axis_size("site") * per_dev, axis=0)
     part_below = lax.slice_in_dim(partial_all, 0, lax.axis_size("site") * per_dev, axis=0)
     part_counts = jnp.einsum("bis,bjs->bij", part_above, part_below, precision=lax.Precision.HIGH)
-    own_counts = pair_scatter(part_counts.reshape(site_count, -1, 128), 2).reshape((per_dev, 64, 64))
+    own_counts = pair_scatter(part_counts, site_count, 2)
     d_scaled = own_pull(own_counts)[0]
     use_rates = lax.dynamic_slice_in_dim(slot_rates, own_start, per_dev, 0)
     use_len = lax.dynamic_slice_in_dim(slot_len, own_start, per_dev, 0)

time: 189 us -> 188 us (level)
  local copies, waits for them, and re-layouts: 23.1 us -> 17.4 us
  Pallas kernels: 70.9 us -> 74.3 us
    reshape x2 -> x0, local copies, waits for them, and re-layouts: 5.68 us -> none  [the longest x1 4.72 us: body(): part_counts.reshape(site_count, -1, 128)]
    pallas_call x1, Pallas kernels: 24.6 us -> 28.1 us  [pair_scatter(): pl.pallas_call(pair_scatter_kernel, out_shape=jax.ShapeDtypeStruct((per,)...]
where the time goes in v7:
time: 188 us; the launch traced here: 187 us
  Pallas kernels  74.3 us (40%)
  other arithmetic  43.9 us (23%)
  matrix products  36.8 us (20%)
  local copies, waits for them, and re-layouts  17.4 us (9%)
  blocking collectives  10.3 us (5%)
  between operations  4.56 us (2%)
    pallas_call x1, Pallas kernels, pair_gather(): pl.pallas_call(pair_gather_kernel, out_shape=jax.ShapeDtypeStruct((n * pe...  29.1 us
    pallas_call x1, Pallas kernels, pair_scatter(): pl.pallas_call(pair_scatter_kernel, out_shape=jax.ShapeDtypeStruct((per,)...  28.1 us
    pallas_call x1, Pallas kernels, allreduce_all(): pl.pallas_call(functools.partial(allreduce_kernel, n_site, n_branch), out...  17.1 us
    unnamed x14, other arithmetic  15.6 us
    dot_general x1, matrix products, body(): jnp.einsum('bis,bjs->bij', part_above, part_below, precision=lax.Precisio...  11.7 us
    dot_general x35, matrix products, product(): return jnp.einsum('bij,bjk->bik', left, right, precision=lax.Precision.HIGH)  11.3 us
    all_gather x1, blocking collectives, body(): top_all = lax.all_gather(top_pack, 'branch', axis=0, tiled=False)  10.3 us
    unnamed x144, local copies, waits for them, and re-layouts  6.24 us

profile of v7, /device:TPU:1, one launch (start us, length us, event | category | flops | bytes accessed | tf_op | source)
XLA Modules:
  0.0 187.4 jit_solution(3938295456044136425)
XLA Ops:
  1.4 0.7 pad_add_fusion
  2.1 0.7 pad_maximum_fusion.5
  3.4 0.8 compare_and_fusion
  4.2 1.2 convert_element_type.44
  5.4 1.3 fusion.82
  8.1 0.8 copy.101
  8.9 0.8 fusion.65
  9.7 1.0 fusion.29
  12.1 1.6 gather_fusion
  13.8 2.2 %fusion.27 = f32[128,64,64]{0,2,1:T(8,128)S(1)} fusion(f32[8]{0:T(128)S(1)} %multiply_reduce_fusion.10, f32[64,64]{1,0:T(8,128)S(1)} %fusion.66, f32[8,64]{0,1:T(8,128)S(1)} %fusion.29, f32[64,64]{1,0:T(8,128)} %constant.112, f32[8]{0:T(128)S(1)} %broadcast_add_fusion, f32[64,64]{1,0:T(8,128)} %constant.111, f32[64,64]{1,0:T(8,128)S(1)} %fusion.65, ...), kind=kOutput, calls=%fused_computation.96 | convolution fusion | flops 25396224 | bytes 2165312 | tf_op jit(solution)/shard_map/bc,cij->bij/dot_general | solution.py:550
  22.6 0.8 reshape.308.x_ref
  23.4 29.1 %shard_map.174 = f32[128,64,64]{2,1,0:T(8,128)} custom-call(f32[64,256]{1,0:T(8,128)} %reshape.308.x_ref), custom_call_target="tpu_custom_call" | custom-call | tf_op jit(solution)/shard_map/pallas_call | solution.py:519
  52.5 0.9 convert_select_fusion.4
  53.5 1.2 copy-done.2
  54.7 2.0 %fusion.7 = f32[64,64,256]{2,1,0:T(8,128)S(1)} fusion(f32[128,64,64]{2,1,0:T(8,128)S(1)} %copy-done.2, f32[64,64,256]{2,1,0:T(8,128)S(1)} %convert_select_fusion.4), kind=kOutput, calls=%fused_computation.13 | convolution fusion | flops 402653184 | bytes 10485760 | tf_op jit(solution)/shard_map/bij,bjs->bis/dot_general | solution.py:62
  57.2 1.1 fusion.24
  61.7 10.3 %all-gather.1 = f32[4,65,256]{2,1,0:T(8,128)S(1)} all-gather(f32[1,65,256]{2,1,0:T(8,128)S(1)} %maximum_bitcast_fusion.2), channel_id=2, replica_groups=mesh['site'=32,'branch'=4] {'branch'}, dimensions={0}, use_global_device_ids=true | all-gather | bytes 332800 | tf_op jit(solution)/shard_map/all_gather | solution.py:565
  72.9 1.2 multiply_reduce_fusion.11
  74.8 1.2 fusion.83
  75.9 0.9 fusion.50
  76.8 0.9 multiply_reduce_fusion.9
  78.4 1.1 fusion.44
  79.8 1.1 multiply_reduce_fusion.7
  80.9 0.8 multiply_divide_fusion.4
  81.7 1.2 fusion.93
  85.6 1.0 fusion.12
  87.3 1.2 fusion.96
  88.5 1.9 fusion.11
  90.8 2.7 %fusion.6 = f32[128,64,256]{2,1,0:T(8,128)} fusion(s32[64,256]{1,0:T(8,128)S(1)} %copy-done.37, pred[64,256]{1,0:T(8,128)(4,1)S(1)} %select_compare_fusion), kind=kLoop, calls=%fused_computation.12 | loop fusion | flops 3145727 | bytes 4276224
  93.5 2.4 %multiply_bitcast_fusion.1 = (f32[32,1,64,256]{3,2,0,1:T(8,128)S(1)}, f32[32,1,64,256]{3,2,0,1:T(8,128)S(1)}, f32[128,64,256]{2,1,0:T(8,128)}) fusion(f32[32,64,256]{2,1,0:T(8,128)S(1)} %fusion.11, f32[64,64,256]{2,1,0:T(8,128)S(1)} %copy-done.5, f32[128,64,256]{2,1,0:T(8,128)} %fusion.6, f32[32,256]{1,0:T(8,128)S(1)} %copy-done.42), kind=kLoop, calls=%fused_computation.19 | loop fusion | flops 2097152 | bytes 12615680 | tf_op jit(solution)/shard_map/stack | solution.py:119
  96.5 1.4 fusion.5
  98.0 3.4 %constant_dynamic-update-slice_fusion.1 = f32[128,64,256]{2,1,0:T(8,128)} fusion(f32[64,256]{1,0:T(8,128)S(1)} %multiply_divide_fusion, f32[32,2,64,256]{3,2,1,0:T(8,128)S(1)} %copy.114), kind=kLoop, calls=%fused_computation.166 | loop fusion | flops 1048575 | bytes 8454144
  101.3 1.5 multiply_dynamic-update-slice_fusion
  102.9 1.1 multiply_dynamic-update-slice_fusion.1
  104.0 0.8 multiply_dynamic-update-slice_fusion.2
  104.8 0.7 multiply_dynamic-update-slice_fusion.3
  106.8 1.2 fusion.25
  108.0 0.9 fusion.30
  108.9 0.7 fusion.42
  111.5 11.7 %fusion.87.x_ref = f32[128,64,64]{2,1,0:T(8,128)} fusion(f32[128,64,256]{2,1,0:T(8,128)} %get-tuple-element.43, f32[128,64,256]{2,1,0:T(8,128)} %get-tuple-element.44), kind=kOutput, calls=%fused_computation.231 | convolution fusion | flops 805306368 | bytes 18874368 | tf_op jit(solution)/shard_map/bis,bjs->bij/dot_general | solution.py:578
  123.3 28.1 %shard_map.175 = f32[4,64,64]{2,1,0:T(8,128)} custom-call(f32[128,64,64]{2,1,0:T(8,128)} %fusion.87.x_ref), custom_call_target="tpu_custom_call" | custom-call | tf_op jit(solution)/shard_map/pallas_call | solution.py:390
  151.5 1.2 fusion.88
  152.7 1.1 convolution_add_fusion.10
  160.7 1.2 multiply_reduce_fusion.5
  163.4 17.1 %shard_map.176 = f32[40,128]{1,0:T(8,128)} custom-call(f32[40,128]{1,0:T(8,128)} %pad_bitcast_fusion.x_ref), custom_call_target="tpu_custom_call" | custom-call | tf_op jit(solution)/shard_map/pallas_call | solution.py:193
  180.5 1.3 slice.171
  182.4 1.2 slice.169
  183.6 0.7 slice_bitcast_fusion
  (257 shorter events, 33.2 us)
Async XLA Ops:
  0.6 10.7 %copy-start = (s32[256,256]{1,0:T(8,128)S(1)}, s32[256,256]{1,0:T(8,128)}, u32[]{:S(2)}) copy-start(s32[256,256]{1,0:T(8,128)} %param.17) | copy-start | bytes 786436
  1.4 16.0 %copy-start.63 = (f32[8]{0:T(128)}, f32[8]{0:T(128)S(1)}, u32[]{:S(2)}) copy-start(f32[8]{0:T(128)S(1)} %broadcast_add_fusion) | copy-start | bytes 100
  3.4 15.9 %copy-start.49 = (f32[4]{0:T(128)}, f32[4]{0:T(128)S(1)}, u32[]{:S(2)}) copy-start(f32[4]{0:T(128)S(1)} %get-tuple-element.10) | copy-start | bytes 52
  8.1 11.3 %copy-start.10 = (f32[64,64]{1,0:T(8,128)}, f32[64,64]{1,0:T(8,128)S(1)}, u32[]{:S(2)}) copy-start(f32[64,64]{1,0:T(8,128)S(1)} %fusion.66) | copy-start | bytes 49156
  9.7 6.4 %copy-start.39 = (f32[64,64]{1,0:T(8,128)}, f32[64,64]{1,0:T(8,128)S(1)}, u32[]{:S(2)}) copy-start(f32[64,64]{1,0:T(8,128)S(1)} %fusion.65) | copy-start | bytes 49156
  10.7 5.3 %copy-start.43 = (f32[8,64]{0,1:T(8,128)}, f32[8,64]{0,1:T(8,128)S(1)}, u32[]{:S(2)}) copy-start(f32[8,64]{0,1:T(8,128)S(1)} %fusion.29) | copy-start | bytes 6148
  10.8 6.6 %copy-start.65 = (f32[8]{0:T(128)}, f32[8]{0:T(128)S(1)}, u32[]{:S(2)}) copy-start(f32[8]{0:T(128)S(1)} %multiply_reduce_fusion.10) | copy-start | bytes 100
  12.1 40.4 %copy-start.36 = (s32[64,256]{1,0:T(8,128)}, s32[64,256]{1,0:T(8,128)S(1)}, u32[]{:S(2)}) copy-start(s32[64,256]{1,0:T(8,128)S(1)} %broadcast_select_fusion) | copy-start | bytes 196612
  18.5 3.9 %copy-start.30 = (f32[4,64,64]{2,1,0:T(8,128)}, f32[4,64,64]{2,1,0:T(8,128)S(1)}, u32[]{:S(2)}) copy-start(f32[4,64,64]{2,1,0:T(8,128)S(1)} %fusion.19) | copy-start | bytes 196612
  21.2 32.3 %copy-start.12 = (f32[4,64,64]{2,1,0:T(8,128)}, f32[4,64,64]{2,1,0:T(8,128)S(1)}, u32[]{:S(2)}) copy-start(f32[4,64,64]{2,1,0:T(8,128)S(1)} %fusion.84) | copy-start | bytes 196612
  21.4 32.1 %copy-start.14 = (f32[4,64,64]{2,1,0:T(8,128)}, f32[4,64,64]{2,1,0:T(8,128)S(1)}, u32[]{:S(2)}) copy-start(f32[4,64,64]{2,1,0:T(8,128)S(1)} %fusion.85) | copy-start | bytes 196612
  59.5 12.6 %copy-start.57 = (f32[64]{0:T(128)S(1)}, f32[64]{0:T(128)}, u32[]{:S(2)}) copy-start(f32[64]{0:T(128)} %copy-done.56) | copy-start | bytes 772
  59.5 13.4 %copy-start.68 = (s32[256]{0:T(256)S(1)}, s32[256]{0:T(256)}, u32[]{:S(2)}) copy-start(s32[256]{0:T(256)} %param.19) | copy-start | bytes 3076
  60.5 19.2 %copy-start.8 = (f32[4,64,256]{2,1,0:T(8,128)}, f32[4,64,256]{2,1,0:T(8,128)S(1)}, u32[]{:S(2)}) copy-start(f32[4,64,256]{2,1,0:T(8,128)S(1)} %fusion.43) | copy-start | bytes 786436
  74.7 8.4 %copy-start.7 = (f32[8,64,256]{2,1,0:T(8,128)S(1)}, f32[8,64,256]{2,1,0:T(8,128)}, u32[]{:S(2)}) copy-start(f32[8,64,256]{2,1,0:T(8,128)} %copy-done.6) | copy-start | bytes 1572868
  79.7 3.7 %copy-start.3 = (f32[128,64,64]{2,1,0:T(8,128)S(1)}, f32[128,64,64]{2,1,0:T(8,128)}, u32[]{:S(2)}) copy-start(f32[128,64,64]{2,1,0:T(8,128)} %shard_map.174) | copy-start | bytes 6291460
  101.3 4.8 %copy-start.38 = (f32[1,64,256]{2,1,0:T(8,128)S(1)}, f32[1,64,256]{2,1,0:T(8,128)}, u32[]{:S(2)}) copy-start(f32[1,64,256]{2,1,0:T(8,128)} %get-tuple-element.12) | copy-start | bytes 196612
  101.3 4.8 %copy-start.67 = (f32[256]{0:T(256)S(1)}, f32[256]{0:T(256)}, u32[]{:S(2)}) copy-start(f32[256]{0:T(256)} %get-tuple-element.39) | copy-start | bytes 3076
  101.3 5.5 %copy-start.48 = (f32[16,256]{1,0:T(8,128)S(1)}, f32[16,256]{1,0:T(8,128)}, u32[]{:S(2)}) copy-start(f32[16,256]{1,0:T(8,128)} %copy-done.47) | copy-start | bytes 49156
  102.9 5.1 %copy-start.52 = (f32[8,256]{1,0:T(8,128)S(1)}, f32[8,256]{1,0:T(8,128)}, u32[]{:S(2)}) copy-start(f32[8,256]{1,0:T(8,128)} %copy-done.51) | copy-start | bytes 24580
  102.9 6.0 %copy-start.55 = (f32[4,256]{1,0:T(4,128)S(1)}, f32[4,256]{1,0:T(4,128)}, u32[]{:S(2)}) copy-start(f32[4,256]{1,0:T(4,128)} %copy-done.54) | copy-start | bytes 12292
  104.0 5.6 %copy-start.9 = (f32[4,64,256]{2,1,0:T(8,128)S(1)}, f32[4,64,256]{2,1,0:T(8,128)}, u32[]{:S(2)}) copy-start(f32[4,64,256]{2,1,0:T(8,128)} %copy-done.8) | copy-start | bytes 786436
  104.0 5.6 %copy-start.60 = (f32[2,256]{1,0:T(2,128)S(1)}, f32[2,256]{1,0:T(2,128)}, u32[]{:S(2)}) copy-start(f32[2,256]{1,0:T(2,128)} %copy-done.59) | copy-start | bytes 6148
  104.0 6.3 %copy-start.21 = (f32[2,64,256]{2,1,0:T(8,128)S(1)}, f32[2,64,256]{2,1,0:T(8,128)}, u32[]{:S(2)}) copy-start(f32[2,64,256]{2,1,0:T(8,128)} %copy-done.20) | copy-start | bytes 393220
  104.0 6.3 %copy-start.62 = (f32[256]{0:T(256)S(1)}, f32[256]{0:T(256)}, u32[]{:S(2)}) copy-start(f32[256]{0:T(256)} %copy-done.61) | copy-start | bytes 3076
  123.2 28.2 %copy-start.17 = (f32[4,64,64]{2,1,0:T(8,128)S(1)}, f32[4,64,64]{2,1,0:T(8,128)}, u32[]{:S(2)}) copy-start(f32[4,64,64]{2,1,0:T(8,128)} %copy-done.16) | copy-start | bytes 196612
  123.2 30.6 %copy-start.15 = (f32[4,64,64]{2,1,0:T(8,128)S(1)}, f32[4,64,64]{2,1,0:T(8,128)}, u32[]{:S(2)}) copy-start(f32[4,64,64]{2,1,0:T(8,128)} %copy-done.14) | copy-start | bytes 196612
  123.2 31.2 %copy-start.13 = (f32[4,64,64]{2,1,0:T(8,128)S(1)}, f32[4,64,64]{2,1,0:T(8,128)}, u32[]{:S(2)}) copy-start(f32[4,64,64]{2,1,0:T(8,128)} %copy-done.12) | copy-start | bytes 196612
  123.2 31.8 %copy-start.19 = (f32[4,64,64]{2,1,0:T(8,128)S(1)}, f32[4,64,64]{2,1,0:T(8,128)}, u32[]{:S(2)}) copy-start(f32[4,64,64]{2,1,0:T(8,128)} %copy-done.18) | copy-start | bytes 196612
  123.2 32.4 %copy-start.23 = (f32[4,64,64]{2,1,0:T(8,128)S(1)}, f32[4,64,64]{2,1,0:T(8,128)}, u32[]{:S(2)}) copy-start(f32[4,64,64]{2,1,0:T(8,128)} %copy-done.22) | copy-start | bytes 196612
  123.3 32.6 %copy-start.50 = (f32[4]{0:T(128)S(1)}, f32[4]{0:T(128)}, u32[]{:S(2)}) copy-start(f32[4]{0:T(128)} %copy-done.49) | copy-start | bytes 52
  123.3 33.0 %copy-start.35 = (f32[4,64,64]{2,1,0:T(8,128)S(1)}, f32[4,64,64]{2,1,0:T(8,128)}, u32[]{:S(2)}) copy-start(f32[4,64,64]{2,1,0:T(8,128)} %copy-done.34) | copy-start | bytes 196612
  123.3 33.6 %copy-start.33 = (f32[4,64,64]{2,1,0:T(8,128)S(1)}, f32[4,64,64]{2,1,0:T(8,128)}, u32[]{:S(2)}) copy-start(f32[4,64,64]{2,1,0:T(8,128)} %copy-done.32) | copy-start | bytes 196612
  151.5 6.1 %copy-start.31 = (f32[4,64,64]{2,1,0:T(8,128)S(1)}, f32[4,64,64]{2,1,0:T(8,128)}, u32[]{:S(2)}) copy-start(f32[4,64,64]{2,1,0:T(8,128)} %copy-done.30) | copy-start | bytes 196612
  151.5 6.7 %copy-start.29 = (f32[4,64,64]{2,1,0:T(8,128)S(1)}, f32[4,64,64]{2,1,0:T(8,128)}, u32[]{:S(2)}) copy-start(f32[4,64,64]{2,1,0:T(8,128)} %copy-done.28) | copy-start | bytes 196612
  151.5 7.3 %copy-start.27 = (f32[4,64,64]{2,1,0:T(8,128)S(1)}, f32[4,64,64]{2,1,0:T(8,128)}, u32[]{:S(2)}) copy-start(f32[4,64,64]{2,1,0:T(8,128)} %copy-done.26) | copy-start | bytes 196612
  153.9 5.5 %copy-start.25 = (f32[4,64,64]{2,1,0:T(8,128)S(1)}, f32[4,64,64]{2,1,0:T(8,128)}, u32[]{:S(2)}) copy-start(f32[4,64,64]{2,1,0:T(8,128)} %copy-done.24) | copy-start | bytes 196612
  154.4 5.5 %copy-start.11 = (f32[64,64]{1,0:T(8,128)S(1)}, f32[64,64]{1,0:T(8,128)}, u32[]{:S(2)}) copy-start(f32[64,64]{1,0:T(8,128)} %copy-done.10) | copy-start | bytes 49156
  154.5 5.5 %copy-start.69 = (f32[4]{0:T(128)S(1)}, f32[4]{0:T(128)}, u32[]{:S(2)}) copy-start(f32[4]{0:T(128)} %get-tuple-element.9) | copy-start | bytes 52
  154.8 5.9 %copy-start.40 = (f32[64,64]{1,0:T(8,128)S(1)}, f32[64,64]{1,0:T(8,128)}, u32[]{:S(2)}) copy-start(f32[64,64]{1,0:T(8,128)} %copy-done.39) | copy-start | bytes 49156
  154.8 5.9 %copy-start.44 = (f32[8,64]{0,1:T(8,128)S(1)}, f32[8,64]{0,1:T(8,128)}, u32[]{:S(2)}) copy-start(f32[8,64]{0,1:T(8,128)} %copy-done.43) | copy-start | bytes 6148
  154.8 5.9 %copy-start.45 = (f32[64,64]{1,0:T(8,128)S(1)}, f32[64,64]{1,0:T(8,128)}, u32[]{:S(2)}) copy-start(f32[64,64]{1,0:T(8,128)} %constant.112) | copy-start | bytes 49156
  154.8 5.9 %copy-start.46 = (f32[64,64]{1,0:T(8,128)S(1)}, f32[64,64]{1,0:T(8,128)}, u32[]{:S(2)}) copy-start(f32[64,64]{1,0:T(8,128)} %constant.111) | copy-start | bytes 49156
  154.8 5.9 %copy-start.64 = (f32[8]{0:T(128)S(1)}, f32[8]{0:T(128)}, u32[]{:S(2)}) copy-start(f32[8]{0:T(128)} %copy-done.63) | copy-start | bytes 100
  154.8 5.9 %copy-start.66 = (f32[8]{0:T(128)S(1)}, f32[8]{0:T(128)}, u32[]{:S(2)}) copy-start(f32[8]{0:T(128)} %copy-done.65) | copy-start | bytes 100
  154.8 5.9 %copy-start.70 = (f32[8]{0:T(128)S(1)}, f32[8]{0:T(128)}, u32[]{:S(2)}) copy-start(f32[8]{0:T(128)} %multiply_divide_fusion.7) | copy-start | bytes 100
  155.9 6.1 %copy-start.58 = (f32[64]{0:T(128)S(1)}, f32[64]{0:T(128)}, u32[]{:S(2)}) copy-start(f32[64]{0:T(128)} %copy-done.56) | copy-start | bytes 772
  156.3 30.0 %copy-start.1 = (s32[256,256]{1,0:T(8,128)S(1)}, s32[256,256]{1,0:T(8,128)}, u32[]{:S(2)}) copy-start(s32[256,256]{1,0:T(8,128)} %param.17) | copy-start | bytes 786436
  (23 other events, 40.8 us)

commit v8 on v7

--- a/solution.py
+++ b/solution.py
@@ -570,12 +570,12 @@
     above_top = lax.dynamic_slice_in_dim(above_all, subtree, 1, 0)
     a_list = down_pass(probs, levels, messages, above_top)
     weighted = weigh(a_list, messages, site_weight, total_sites)
-    padding = jnp.zeros((1, 64, site_span), jnp.float32)
-    weighted_all = jnp.concatenate(weighted + [padding], axis=0)
-    partial_all = jnp.concatenate(levels + [padding], axis=0)
-    part_above = lax.slice_in_dim(weighted_all, 0, lax.axis_size("site") * per_dev, axis=0)
-    part_below = lax.slice_in_dim(partial_all, 0, lax.axis_size("site") * per_dev, axis=0)
-    part_counts = jnp.einsum("bis,bjs->bij", part_above, part_below, precision=lax.Precision.HIGH)
+    level_counts = [
+        jnp.einsum("bis,bjs->bij", vector, partial_value, precision=lax.Precision.HIGH)
+        for vector, partial_value in zip(weighted, levels)
+    ]
+    spare = site_count * per_dev - sum(c.shape[0] for c in level_counts)
+    part_counts = jnp.concatenate(level_counts + [jnp.zeros((spare, 64, 64), jnp.float32)], axis=0)
     own_counts = pair_scatter(part_counts, site_count, 2)
     d_scaled = own_pull(own_counts)[0]
     use_rates = lax.dynamic_slice_in_dim(slot_rates, own_start, per_dev, 0)

time: 188 us -> 172 us (0.915)
  other arithmetic: 43.9 us -> 28.8 us
    unnamed x14 -> x1, other arithmetic: 15.6 us -> 0.01 us
    dot_general x1 -> x7, matrix products: 11.7 us -> 10.8 us  [body(): jnp.einsum('bis,bjs->bij', vector, partial_value, precision=lax.Precision...]
    unnamed x144 -> x136, local copies, waits for them, and re-layouts: 6.24 us -> 6.14 us
where the time goes in v8:
time: 172 us; the launch traced here: 171 us
  Pallas kernels  74.1 us (43%)
  matrix products  35.9 us (21%)
  other arithmetic  28.8 us (17%)
  local copies, waits for them, and re-layouts  17.2 us (10%)
  blocking collectives  10.3 us (6%)
  between operations  4.61 us (3%)
    pallas_call x1, Pallas kernels, pair_gather(): pl.pallas_call(pair_gather_kernel, out_shape=jax.ShapeDtypeStruct((n * pe...  29.1 us
    pallas_call x1, Pallas kernels, pair_scatter(): pl.pallas_call(pair_scatter_kernel, out_shape=jax.ShapeDtypeStruct((per,)...  28 us
    pallas_call x1, Pallas kernels, allreduce_all(): pl.pallas_call(functools.partial(allreduce_kernel, n_site, n_branch), out...  17 us
    dot_general x35, matrix products, product(): return jnp.einsum('bij,bjk->bik', left, right, precision=lax.Precision.HIGH)  11.3 us
    dot_general x7, matrix products, body(): jnp.einsum('bis,bjs->bij', vector, partial_value, precision=lax.Precision...  10.8 us
    all_gather x1, blocking collectives, body(): top_all = lax.all_gather(top_pack, 'branch', axis=0, tiled=False)  10.3 us
    unnamed x136, local copies, waits for them, and re-layouts  6.14 us
    dot_general x6, matrix products, carried(): jnp.einsum('bji,bjs->bis', probs, vectors, precision=lax.Precision.HIGH)  5.72 us

profile of v8, /device:TPU:1, one launch (start us, length us, event | category | flops | bytes accessed | tf_op | source)
XLA Modules:
  0.0 171.0 jit_solution(10135117097451084062)
XLA Ops:
  1.4 0.7 pad_add_fusion
  2.1 0.7 pad_maximum_fusion.5
  3.5 0.8 compare_and_fusion
  4.2 1.2 convert_element_type.44
  5.5 1.3 fusion.102
  8.1 0.8 copy.101
  9.0 0.8 fusion.82
  9.7 1.0 fusion.43
  12.1 1.6 gather_fusion
  13.9 2.2 %fusion.41 = f32[128,64,64]{0,2,1:T(8,128)S(1)} fusion(f32[8]{0:T(128)S(1)} %multiply_reduce_fusion.10, f32[64,64]{1,0:T(8,128)S(1)} %fusion.84, f32[8,64]{0,1:T(8,128)S(1)} %fusion.43, f32[64,64]{1,0:T(8,128)} %constant.112, f32[8]{0:T(128)S(1)} %broadcast_add_fusion, f32[64,64]{1,0:T(8,128)} %constant.111, f32[64,64]{1,0:T(8,128)S(1)} %fusion.82, ...), kind=kOutput, calls=%fused_computation.109 | convolution fusion | flops 25396224 | bytes 2165312 | tf_op jit(solution)/shard_map/bc,cij->bij/dot_general | solution.py:550
  16.7 0.7 copy.147
  22.6 0.8 reshape.313.x_ref
  23.3 29.1 %shard_map.174 = f32[128,64,64]{2,1,0:T(8,128)} custom-call(f32[64,256]{1,0:T(8,128)} %reshape.313.x_ref), custom_call_target="tpu_custom_call" | custom-call | tf_op jit(solution)/shard_map/pallas_call | solution.py:519
  52.5 0.9 convert_select_fusion.7
  53.4 1.2 copy-done.2
  54.6 2.0 %fusion.7 = f32[64,64,256]{2,1,0:T(8,128)S(1)} fusion(f32[128,64,64]{2,1,0:T(8,128)S(1)} %copy-done.2, f32[64,64,256]{2,1,0:T(8,128)S(1)} %convert_select_fusion.7), kind=kOutput, calls=%fused_computation.13 | convolution fusion | flops 402653184 | bytes 10485760 | tf_op jit(solution)/shard_map/bij,bjs->bis/dot_general | solution.py:62
  57.1 1.1 fusion.35
  61.6 10.3 %all-gather.1 = f32[4,65,256]{2,1,0:T(8,128)S(1)} all-gather(f32[1,65,256]{2,1,0:T(8,128)S(1)} %maximum_bitcast_fusion.3), channel_id=2, replica_groups=mesh['site'=32,'branch'=4] {'branch'}, dimensions={0}, use_global_device_ids=true | all-gather | bytes 332800 | tf_op jit(solution)/shard_map/all_gather | solution.py:565
  72.8 1.2 multiply_reduce_fusion.11
  74.7 1.2 fusion.103
  75.9 0.9 fusion.65
  76.8 0.9 multiply_reduce_fusion.9
  78.4 1.1 fusion.58
  79.7 1.2 multiply_bitcast_fusion.9
  80.9 1.2 multiply_reduce_fusion.7
  82.7 1.2 fusion.112
  86.6 1.0 fusion.21
  88.3 1.2 fusion.115
  89.5 1.9 %fusion.17 = f32[32,64,256]{2,1,0:T(8,128)S(1)} fusion(f32[32,64,256]{2,1,0:T(8,128)S(1)} %fusion.115), kind=kOutput, calls=%fused_computation.29 | output fusion | flops 532543 | bytes 4194304 | tf_op jit(solution)/shard_map/div | solution.py:117
  91.8 0.8 multiply_bitcast_fusion.1
  93.2 1.4 fusion.5
  94.7 1.0 bitcast_multiply_fusion
  95.7 3.5 %fusion.16 = f32[128,64,64]{2,1,0:T(8,128)} fusion(f32[64,64,256]{2,1,0:T(8,128)S(1)} %bitcast_multiply_fusion, s32[64,256]{1,0:T(8,128)S(1)} %copy-done.33, pred[64,256]{1,0:T(8,128)(4,1)S(1)} %select_compare_fusion), kind=kOutput, calls=%fused_computation.28 | convolution fusion | flops 405798912 | bytes 6373376 | tf_op jit(solution)/shard_map/bis,bjs->bij/dot_general | solution.py:574
  99.3 2.2 %fusion.18 = f32[128,64,64]{2,1,0:T(8,128)} fusion(f32[128,64,64]{2,1,0:T(8,128)} %fusion.16, f32[32,64,256]{2,1,0:T(8,128)S(1)} %bitcast.205, f32[32,256]{1,0:T(8,128)S(1)} %multiply_divide_fusion.1, f32[32,256]{1,0:T(8,128)S(1)} %copy-done.44, f32[64,64,256]{2,1,0:T(8,128)S(1)} %copy-done.5), kind=kOutput, calls=%fused_computation.30 | convolution fusion | flops 202899456 | bytes 7405568 | tf_op jit(solution)/shard_map/bis,bjs->bij/dot_general | solution.py:574
  101.5 1.5 convolution_dynamic-update-slice_fusion
  102.9 1.1 convolution_dynamic-update-slice_fusion.1
  104.1 0.9 convolution_dynamic-update-slice_fusion.2
  105.0 0.8 convolution_dynamic-update-slice_fusion.3
  105.8 0.8 fusion.32
  107.2 28.0 %shard_map.175 = f32[4,64,64]{2,1,0:T(8,128)} custom-call(f32[128,64,64]{2,1,0:T(8,128)} %constant_dynamic-update-slice_fusion.x_ref), custom_call_target="tpu_custom_call" | custom-call | tf_op jit(solution)/shard_map/pallas_call | solution.py:390
  135.2 1.2 fusion.107
  136.5 1.1 convolution_add_fusion.10
  144.5 1.2 multiply_reduce_fusion.5
  147.1 17.0 %shard_map.176 = f32[40,128]{1,0:T(8,128)} custom-call(f32[40,128]{1,0:T(8,128)} %pad_bitcast_fusion.x_ref), custom_call_target="tpu_custom_call" | custom-call | tf_op jit(solution)/shard_map/pallas_call | solution.py:193
  164.1 1.3 slice.171
  166.0 1.2 slice.169
  167.2 0.7 slice_bitcast_fusion
  168.5 0.7 slice.152
  (243 shorter events, 29.7 us)
Async XLA Ops:
  0.6 10.8 %copy-start = (s32[256,256]{1,0:T(8,128)S(1)}, s32[256,256]{1,0:T(8,128)}, u32[]{:S(2)}) copy-start(s32[256,256]{1,0:T(8,128)} %param.17) | copy-start | bytes 786436
  1.4 16.1 %copy-start.57 = (f32[8]{0:T(128)}, f32[8]{0:T(128)S(1)}, u32[]{:S(2)}) copy-start(f32[8]{0:T(128)S(1)} %broadcast_add_fusion) | copy-start | bytes 100
  3.5 15.9 %copy-start.41 = (f32[4]{0:T(128)}, f32[4]{0:T(128)S(1)}, u32[]{:S(2)}) copy-start(f32[4]{0:T(128)S(1)} %get-tuple-element.10) | copy-start | bytes 52
  7.4 3.5 %copy-start.50 = (f32[64]{0:T(128)}, f32[64]{0:T(128)S(1)}, u32[]{:S(2)}) copy-start(f32[64]{0:T(128)S(1)} %get-tuple-element.16) | copy-start | bytes 772
  8.1 11.3 %copy-start.8 = (f32[64,64]{1,0:T(8,128)}, f32[64,64]{1,0:T(8,128)S(1)}, u32[]{:S(2)}) copy-start(f32[64,64]{1,0:T(8,128)S(1)} %fusion.84) | copy-start | bytes 49156
  9.7 6.4 %copy-start.34 = (f32[64,64]{1,0:T(8,128)}, f32[64,64]{1,0:T(8,128)S(1)}, u32[]{:S(2)}) copy-start(f32[64,64]{1,0:T(8,128)S(1)} %fusion.82) | copy-start | bytes 49156
  10.7 5.3 %copy-start.36 = (f32[8,64]{0,1:T(8,128)}, f32[8,64]{0,1:T(8,128)S(1)}, u32[]{:S(2)}) copy-start(f32[8,64]{0,1:T(8,128)S(1)} %fusion.43) | copy-start | bytes 6148
  10.9 6.6 %copy-start.59 = (f32[8]{0:T(128)}, f32[8]{0:T(128)S(1)}, u32[]{:S(2)}) copy-start(f32[8]{0:T(128)S(1)} %multiply_reduce_fusion.10) | copy-start | bytes 100
  12.1 40.3 %copy-start.32 = (s32[64,256]{1,0:T(8,128)}, s32[64,256]{1,0:T(8,128)S(1)}, u32[]{:S(2)}) copy-start(s32[64,256]{1,0:T(8,128)S(1)} %broadcast_select_fusion) | copy-start | bytes 196612
  18.3 2.9 %copy-start.24 = (f32[4,64,64]{2,1,0:T(8,128)}, f32[4,64,64]{2,1,0:T(8,128)S(1)}, u32[]{:S(2)}) copy-start(f32[4,64,64]{2,1,0:T(8,128)S(1)} %fusion.29) | copy-start | bytes 196612
  18.5 3.9 %copy-start.26 = (f32[4,64,64]{2,1,0:T(8,128)}, f32[4,64,64]{2,1,0:T(8,128)S(1)}, u32[]{:S(2)}) copy-start(f32[4,64,64]{2,1,0:T(8,128)S(1)} %fusion.28) | copy-start | bytes 196612
  18.8 3.6 %copy-start.28 = (f32[4,64,64]{2,1,0:T(8,128)}, f32[4,64,64]{2,1,0:T(8,128)S(1)}, u32[]{:S(2)}) copy-start(f32[4,64,64]{2,1,0:T(8,128)S(1)} %fusion.27) | copy-start | bytes 196612
  19.1 3.3 %copy-start.30 = (f32[4,64,64]{2,1,0:T(8,128)}, f32[4,64,64]{2,1,0:T(8,128)S(1)}, u32[]{:S(2)}) copy-start(f32[4,64,64]{2,1,0:T(8,128)S(1)} %fusion.26) | copy-start | bytes 196612
  59.4 12.5 %copy-start.51 = (f32[64]{0:T(128)S(1)}, f32[64]{0:T(128)}, u32[]{:S(2)}) copy-start(f32[64]{0:T(128)} %copy-done.50) | copy-start | bytes 772
  59.5 13.4 %copy-start.63 = (s32[256]{0:T(256)S(1)}, s32[256]{0:T(256)}, u32[]{:S(2)}) copy-start(s32[256]{0:T(256)} %param.19) | copy-start | bytes 3076
  59.6 13.3 %copy-start.48 = (f32[8,256]{1,0:T(8,128)}, f32[8,256]{1,0:T(8,128)S(1)}, u32[]{:S(2)}) copy-start(f32[8,256]{1,0:T(8,128)S(1)} %fusion.98) | copy-start | bytes 24580
  74.7 9.4 %copy-start.7 = (f32[8,64,256]{2,1,0:T(8,128)S(1)}, f32[8,64,256]{2,1,0:T(8,128)}, u32[]{:S(2)}) copy-start(f32[8,64,256]{2,1,0:T(8,128)} %copy-done.6) | copy-start | bytes 1572868
  79.6 4.8 %copy-start.47 = (f32[256]{0:T(256)S(1)}, f32[256]{0:T(256)}, u32[]{:S(2)}) copy-start(f32[256]{0:T(256)} %convert_element_type.44) | copy-start | bytes 3076
  79.7 4.8 %copy-start.3 = (f32[128,64,64]{2,1,0:T(8,128)S(1)}, f32[128,64,64]{2,1,0:T(8,128)}, u32[]{:S(2)}) copy-start(f32[128,64,64]{2,1,0:T(8,128)} %shard_map.174) | copy-start | bytes 6291460
  95.7 3.5 %copy-start.44 = (f32[32,256]{1,0:T(8,128)S(1)}, f32[32,256]{1,0:T(8,128)}, u32[]{:S(2)}) copy-start(f32[32,256]{1,0:T(8,128)} %copy-done.43) | copy-start | bytes 98308
  101.4 2.6 %copy-start.54 = (f32[4,256]{1,0:T(4,128)S(1)}, f32[4,256]{1,0:T(4,128)}, u32[]{:S(2)}) copy-start(f32[4,256]{1,0:T(4,128)} %copy-done.53) | copy-start | bytes 12292
  101.4 3.5 %copy-start.15 = (f32[4,64,256]{2,1,0:T(8,128)S(1)}, f32[4,64,256]{2,1,0:T(8,128)}, u32[]{:S(2)}) copy-start(f32[4,64,256]{2,1,0:T(8,128)} %copy-done.14) | copy-start | bytes 786436
  101.4 3.5 %copy-start.56 = (f32[2,256]{1,0:T(2,128)S(1)}, f32[2,256]{1,0:T(2,128)}, u32[]{:S(2)}) copy-start(f32[2,256]{1,0:T(2,128)} %copy-done.55) | copy-start | bytes 6148
  101.4 4.4 %copy-start.17 = (f32[2,64,256]{2,1,0:T(8,128)S(1)}, f32[2,64,256]{2,1,0:T(8,128)}, u32[]{:S(2)}) copy-start(f32[2,64,256]{2,1,0:T(8,128)} %copy-done.16) | copy-start | bytes 393220
  101.4 4.4 %copy-start.40 = (f32[1,64,256]{2,1,0:T(8,128)S(1)}, f32[1,64,256]{2,1,0:T(8,128)}, u32[]{:S(2)}) copy-start(f32[1,64,256]{2,1,0:T(8,128)} %get-tuple-element.12) | copy-start | bytes 196612
  101.4 4.4 %copy-start.62 = (f32[256]{0:T(256)S(1)}, f32[256]{0:T(256)}, u32[]{:S(2)}) copy-start(f32[256]{0:T(256)} %copy-done.61) | copy-start | bytes 3076
  101.5 4.4 %copy-start.65 = (f32[256]{0:T(256)S(1)}, f32[256]{0:T(256)}, u32[]{:S(2)}) copy-start(f32[256]{0:T(256)} %get-tuple-element.38) | copy-start | bytes 3076
  102.9 32.3 %copy-start.11 = (f32[4,64,64]{2,1,0:T(8,128)S(1)}, f32[4,64,64]{2,1,0:T(8,128)}, u32[]{:S(2)}) copy-start(f32[4,64,64]{2,1,0:T(8,128)} %copy-done.10) | copy-start | bytes 196612
  105.0 33.9 %copy-start.13 = (f32[4,64,64]{2,1,0:T(8,128)S(1)}, f32[4,64,64]{2,1,0:T(8,128)}, u32[]{:S(2)}) copy-start(f32[4,64,64]{2,1,0:T(8,128)} %copy-done.12) | copy-start | bytes 196612
  105.8 33.6 %copy-start.19 = (f32[4,64,64]{2,1,0:T(8,128)S(1)}, f32[4,64,64]{2,1,0:T(8,128)}, u32[]{:S(2)}) copy-start(f32[4,64,64]{2,1,0:T(8,128)} %copy-done.18) | copy-start | bytes 196612
  107.2 32.4 %copy-start.42 = (f32[4]{0:T(128)S(1)}, f32[4]{0:T(128)}, u32[]{:S(2)}) copy-start(f32[4]{0:T(128)} %copy-done.41) | copy-start | bytes 52
  107.2 32.8 %copy-start.31 = (f32[4,64,64]{2,1,0:T(8,128)S(1)}, f32[4,64,64]{2,1,0:T(8,128)}, u32[]{:S(2)}) copy-start(f32[4,64,64]{2,1,0:T(8,128)} %copy-done.30) | copy-start | bytes 196612
  107.2 33.4 %copy-start.29 = (f32[4,64,64]{2,1,0:T(8,128)S(1)}, f32[4,64,64]{2,1,0:T(8,128)}, u32[]{:S(2)}) copy-start(f32[4,64,64]{2,1,0:T(8,128)} %copy-done.28) | copy-start | bytes 196612
  135.2 6.0 %copy-start.27 = (f32[4,64,64]{2,1,0:T(8,128)S(1)}, f32[4,64,64]{2,1,0:T(8,128)}, u32[]{:S(2)}) copy-start(f32[4,64,64]{2,1,0:T(8,128)} %copy-done.26) | copy-start | bytes 196612
  135.2 6.6 %copy-start.25 = (f32[4,64,64]{2,1,0:T(8,128)S(1)}, f32[4,64,64]{2,1,0:T(8,128)}, u32[]{:S(2)}) copy-start(f32[4,64,64]{2,1,0:T(8,128)} %copy-done.24) | copy-start | bytes 196612
  135.2 7.3 %copy-start.23 = (f32[4,64,64]{2,1,0:T(8,128)S(1)}, f32[4,64,64]{2,1,0:T(8,128)}, u32[]{:S(2)}) copy-start(f32[4,64,64]{2,1,0:T(8,128)} %copy-done.22) | copy-start | bytes 196612
  137.6 5.5 %copy-start.21 = (f32[4,64,64]{2,1,0:T(8,128)S(1)}, f32[4,64,64]{2,1,0:T(8,128)}, u32[]{:S(2)}) copy-start(f32[4,64,64]{2,1,0:T(8,128)} %copy-done.20) | copy-start | bytes 196612
  138.2 5.5 %copy-start.9 = (f32[64,64]{1,0:T(8,128)S(1)}, f32[64,64]{1,0:T(8,128)}, u32[]{:S(2)}) copy-start(f32[64,64]{1,0:T(8,128)} %copy-done.8) | copy-start | bytes 49156
  138.2 5.5 %copy-start.64 = (f32[4]{0:T(128)S(1)}, f32[4]{0:T(128)}, u32[]{:S(2)}) copy-start(f32[4]{0:T(128)} %get-tuple-element.9) | copy-start | bytes 52
  138.5 5.9 %copy-start.35 = (f32[64,64]{1,0:T(8,128)S(1)}, f32[64,64]{1,0:T(8,128)}, u32[]{:S(2)}) copy-start(f32[64,64]{1,0:T(8,128)} %copy-done.34) | copy-start | bytes 49156
  138.5 5.9 %copy-start.37 = (f32[8,64]{0,1:T(8,128)S(1)}, f32[8,64]{0,1:T(8,128)}, u32[]{:S(2)}) copy-start(f32[8,64]{0,1:T(8,128)} %copy-done.36) | copy-start | bytes 6148
  138.5 5.9 %copy-start.38 = (f32[64,64]{1,0:T(8,128)S(1)}, f32[64,64]{1,0:T(8,128)}, u32[]{:S(2)}) copy-start(f32[64,64]{1,0:T(8,128)} %constant.112) | copy-start | bytes 49156
  138.5 5.9 %copy-start.39 = (f32[64,64]{1,0:T(8,128)S(1)}, f32[64,64]{1,0:T(8,128)}, u32[]{:S(2)}) copy-start(f32[64,64]{1,0:T(8,128)} %constant.111) | copy-start | bytes 49156
  138.5 5.9 %copy-start.58 = (f32[8]{0:T(128)S(1)}, f32[8]{0:T(128)}, u32[]{:S(2)}) copy-start(f32[8]{0:T(128)} %copy-done.57) | copy-start | bytes 100
  138.6 5.9 %copy-start.60 = (f32[8]{0:T(128)S(1)}, f32[8]{0:T(128)}, u32[]{:S(2)}) copy-start(f32[8]{0:T(128)} %copy-done.59) | copy-start | bytes 100
  138.6 5.9 %copy-start.66 = (f32[8]{0:T(128)S(1)}, f32[8]{0:T(128)}, u32[]{:S(2)}) copy-start(f32[8]{0:T(128)} %multiply_divide_fusion.7) | copy-start | bytes 100
  139.6 6.1 %copy-start.52 = (f32[64]{0:T(128)S(1)}, f32[64]{0:T(128)}, u32[]{:S(2)}) copy-start(f32[64]{0:T(128)} %copy-done.50) | copy-start | bytes 772
  140.0 29.9 %copy-start.1 = (s32[256,256]{1,0:T(8,128)S(1)}, s32[256,256]{1,0:T(8,128)}, u32[]{:S(2)}) copy-start(s32[256,256]{1,0:T(8,128)} %param.17) | copy-start | bytes 786436
  (19 other events, 22.6 us)

commit v9 on v8

--- a/solution.py
+++ b/solution.py
@@ -116,9 +116,8 @@
         down_part = carried(probs[offset : offset + amount], current)
         down_part = down_part / jnp.sum(down_part, axis=1, keepdims=True)
         message = messages[height - 1]
-        current = jnp.stack([down_part * message[1::2], down_part * message[0::2]], axis=1).reshape(
-            message.shape
-        )
+        pairs = message.reshape((amount, 2) + message.shape[1:])
+        current = (down_part[:, None] * pairs[:, ::-1]).reshape(message.shape)
         a_list.append(current)
     return a_list[::-1]
 

time: 172 us -> 170 us (0.988)
  other arithmetic: 28.8 us -> 24.5 us
  local copies, waits for them, and re-layouts: 17.2 us -> 20.4 us
    another operation x11 -> x0, other arithmetic: 3.97 us -> none  [down_pass(): jnp.stack([down_part * message[1::2], down_part * message[0::2]], axis=1)]
    unnamed x136 -> x148, local copies, waits for them, and re-layouts: 6.14 us -> 9.51 us
    mul x0 -> x5, other arithmetic: none -> 2.36 us  [down_pass(): current = (down_part[:, None] * pairs[:, ::-1]).reshape(message.shape)]
    reduce_sum x2, other arithmetic: 0.12 us -> 2.22 us  [root_terms(): site_ll = jnp.log(jnp.sum(joint, axis=0)) + jnp.sum(top_logs, axis=0)]
    div x5 -> x6, other arithmetic: 3.82 us -> 3.83 us  [down_pass(): down_part = down_part / jnp.sum(down_part, axis=1, keepdims=True)]
where the time goes in v9:
time: 170 us; the launch traced here: 169 us
  Pallas kernels  74.3 us (44%)
  matrix products  35 us (21%)
  other arithmetic  24.5 us (14%)
  local copies, waits for them, and re-layouts  20.4 us (12%)
  blocking collectives  10.3 us (6%)
  between operations  4.59 us (3%)
    pallas_call x1, Pallas kernels, pair_gather(): pl.pallas_call(pair_gather_kernel, out_shape=jax.ShapeDtypeStruct((n * pe...  29.1 us
    pallas_call x1, Pallas kernels, pair_scatter(): pl.pallas_call(pair_scatter_kernel, out_shape=jax.ShapeDtypeStruct((per,)...  28.2 us
    pallas_call x1, Pallas kernels, allreduce_all(): pl.pallas_call(functools.partial(allreduce_kernel, n_site, n_branch), out...  17.1 us
    dot_general x35, matrix products, product(): return jnp.einsum('bij,bjk->bik', left, right, precision=lax.Precision.HIGH)  11.3 us
    dot_general x7, matrix products, body(): jnp.einsum('bis,bjs->bij', vector, partial_value, precision=lax.Precision...  10.8 us
    all_gather x1, blocking collectives, body(): top_all = lax.all_gather(top_pack, 'branch', axis=0, tiled=False)  10.3 us
    unnamed x148, local copies, waits for them, and re-layouts  9.51 us
    dot_general x6, matrix products, carried(): jnp.einsum('bji,bjs->bis', probs, vectors, precision=lax.Precision.HIGH)  5.47 us

profile of v9, /device:TPU:1, one launch (start us, length us, event | category | flops | bytes accessed | tf_op | source)
XLA Modules:
  0.0 169.2 jit_solution(12333322549871836496)
XLA Ops:
  0.6 1.3 fusion.97
  2.6 0.8 copy.91
  3.5 0.8 fusion.79
  4.9 1.0 fusion.39
  6.1 0.7 pad_add_fusion
  6.8 2.2 %fusion.37 = f32[128,64,64]{0,2,1:T(8,128)S(1)} fusion(f32[8]{0:T(128)S(1)} %multiply_reduce_fusion.10, f32[64,64]{1,0:T(8,128)S(1)} %fusion.81, f32[8,64]{0,1:T(8,128)S(1)} %fusion.39, f32[64,64]{1,0:T(8,128)} %constant.112, f32[8]{0:T(128)S(1)} %broadcast_add_fusion, f32[64,64]{1,0:T(8,128)} %constant.111, f32[64,64]{1,0:T(8,128)S(1)} %fusion.79, ...), kind=kOutput, calls=%fused_computation.98 | convolution fusion | flops 25396224 | bytes 2165312 | tf_op jit(solution)/shard_map/bc,cij->bij/dot_general | solution.py:549
  9.1 2.0 %constant_dynamic-slice_fusion.1 = f32[4,64,64]{0,2,1:T(8,128)} fusion(f32[128,64,64]{0,2,1:T(8,128)S(1)} %fusion.37, s32[]{:T(128)S(6)} %select_n.31), kind=kLoop, calls=%fused_computation.201 | loop fusion | bytes 131076 | tf_op jit(solution)/shard_map/dynamic_slice | solution.py:553
  11.1 2.3 %copy.132 = f32[4,64,64]{2,1,0:T(8,128)S(1)} copy(f32[4,64,64]{0,2,1:T(8,128)} %constant_dynamic-slice_fusion.1) | data formatting | bytes 131072
  19.9 0.8 reshape.339.x_ref
  20.6 29.1 %shard_map.174 = f32[128,64,64]{2,1,0:T(8,128)} custom-call(f32[64,256]{1,0:T(8,128)} %reshape.339.x_ref), custom_call_target="tpu_custom_call" | custom-call | tf_op jit(solution)/shard_map/pallas_call | solution.py:518
  51.4 0.9 convert_select_fusion.7
  52.3 1.1 copy-done.1
  53.5 2.0 %fusion.2 = f32[64,64,256]{2,1,0:T(8,128)S(1)} fusion(f32[128,64,64]{2,1,0:T(8,128)S(1)} %copy-done.1, f32[64,64,256]{2,1,0:T(8,128)S(1)} %convert_select_fusion.7), kind=kOutput, calls=%fused_computation.8 | convolution fusion | flops 402653184 | bytes 10485760 | tf_op jit(solution)/shard_map/bij,bjs->bis/dot_general | solution.py:62
  56.0 1.1 fusion.27
  60.6 10.3 %all-gather.1 = f32[4,65,256]{2,1,0:T(8,128)S(1)} all-gather(f32[1,65,256]{2,1,0:T(8,128)S(1)} %maximum_bitcast_fusion), channel_id=2, replica_groups=mesh['site'=32,'branch'=4] {'branch'}, dimensions={0}, use_global_device_ids=true | all-gather | bytes 332800 | tf_op jit(solution)/shard_map/all_gather | solution.py:564
  71.0 0.7 copy-done.19
  71.7 0.8 multiply_multiply_fusion.3
  72.5 1.1 fusion.61
  73.6 1.4 fusion.59
  75.0 0.8 slice_reduce_fusion
  75.8 1.3 multiply_reduce_fusion.11
  77.1 1.0 fusion.98
  78.1 1.0 multiply_reduce_fusion.9
  79.2 1.1 fusion.107
  80.4 1.0 reverse_multiply_fusion.4
  81.4 1.2 fusion.108
  84.7 1.0 fusion.31
  86.6 1.1 fusion.111
  87.7 1.9 %fusion.26 = f32[32,64,256]{2,1,0:T(8,128)S(1)} fusion(f32[32,64,256]{2,1,0:T(8,128)S(1)} %fusion.111), kind=kOutput, calls=%fused_computation.67 | output fusion | flops 532543 | bytes 4194304 | tf_op jit(solution)/shard_map/div | solution.py:117
  89.9 0.9 reverse_multiply_fusion
  90.8 1.4 fusion
  92.3 0.9 bitcast_multiply_fusion
  93.2 3.5 %fusion.11 = f32[128,64,64]{2,1,0:T(8,128)} fusion(f32[64,64,256]{2,1,0:T(8,128)S(1)} %bitcast_multiply_fusion, s32[64,256]{1,0:T(8,128)S(1)} %copy-done.36, pred[64,256]{1,0:T(8,128)(4,1)S(1)} %select_compare_fusion), kind=kOutput, calls=%fused_computation.21 | convolution fusion | flops 405798912 | bytes 6373376 | tf_op jit(solution)/shard_map/bis,bjs->bij/dot_general | solution.py:573
  96.7 2.2 %fusion.12 = f32[128,64,64]{2,1,0:T(8,128)} fusion(f32[128,64,64]{2,1,0:T(8,128)} %fusion.11, f32[32,64,256]{2,1,0:T(8,128)S(1)} %bitcast.174, f32[32,256]{1,0:T(8,128)S(1)} %multiply_divide_fusion.1, f32[32,256]{1,0:T(8,128)S(1)} %copy-done.49, f32[64,64,256]{2,1,0:T(8,128)S(1)} %copy-done.4), kind=kOutput, calls=%fused_computation.22 | convolution fusion | flops 202899456 | bytes 7405568 | tf_op jit(solution)/shard_map/bis,bjs->bij/dot_general | solution.py:573
  99.2 1.5 convolution_dynamic-update-slice_fusion
  100.8 1.1 convolution_dynamic-update-slice_fusion.1
  102.0 0.9 convolution_dynamic-update-slice_fusion.2
  102.9 0.8 convolution_dynamic-update-slice_fusion.3
  103.7 0.8 fusion.22
  105.1 28.2 %shard_map.175 = f32[4,64,64]{2,1,0:T(8,128)} custom-call(f32[128,64,64]{2,1,0:T(8,128)} %constant_dynamic-update-slice_fusion.x_ref), custom_call_target="tpu_custom_call" | custom-call | tf_op jit(solution)/shard_map/pallas_call | solution.py:389
  133.3 1.3 fusion.102
  134.6 1.2 convolution_add_fusion.10
  145.3 17.1 %shard_map.176 = f32[40,128]{1,0:T(8,128)} custom-call(f32[40,128]{1,0:T(8,128)} %pad_bitcast_fusion.x_ref), custom_call_target="tpu_custom_call" | custom-call | tf_op jit(solution)/shard_map/pallas_call | solution.py:192
  162.3 0.7 slice.140
  163.1 0.7 reshape.357
  163.7 0.7 slice_bitcast_fusion
  165.0 1.3 slice.159
  166.9 1.2 slice.157
  (245 shorter events, 26.5 us)
Async XLA Ops:
  0.6 49.2 %copy-start = (s32[256,256]{1,0:T(8,128)S(1)}, s32[256,256]{1,0:T(8,128)}, u32[]{:S(2)}) copy-start(s32[256,256]{1,0:T(8,128)} %param.17) | copy-start | bytes 786436
  2.6 6.4 %copy-start.54 = (f32[64]{0:T(128)}, f32[64]{0:T(128)S(1)}, u32[]{:S(2)}) copy-start(f32[64]{0:T(128)S(1)} %get-tuple-element.16) | copy-start | bytes 772
  4.9 4.2 %copy-start.61 = (f32[8]{0:T(128)}, f32[8]{0:T(128)S(1)}, u32[]{:S(2)}) copy-start(f32[8]{0:T(128)S(1)} %broadcast_add_fusion) | copy-start | bytes 100
  5.9 3.1 %copy-start.41 = (f32[8,64]{0,1:T(8,128)}, f32[8,64]{0,1:T(8,128)S(1)}, u32[]{:S(2)}) copy-start(f32[8,64]{0,1:T(8,128)S(1)} %fusion.39) | copy-start | bytes 6148
  6.0 3.1 %copy-start.63 = (f32[8]{0:T(128)}, f32[8]{0:T(128)S(1)}, u32[]{:S(2)}) copy-start(f32[8]{0:T(128)S(1)} %multiply_reduce_fusion.10) | copy-start | bytes 100
  6.0 10.0 %copy-start.7 = (f32[64,64]{1,0:T(8,128)}, f32[64,64]{1,0:T(8,128)S(1)}, u32[]{:S(2)}) copy-start(f32[64,64]{1,0:T(8,128)S(1)} %fusion.81) | copy-start | bytes 49156
  6.8 6.6 %copy-start.72 = (f32[127]{0:T(128)S(1)}, f32[127]{0:T(128)}, u32[]{:S(2)}) copy-start(f32[127]{0:T(128)} %param.24) | copy-start | bytes 1528
  14.0 5.7 %copy-start.46 = (f32[4]{0:T(128)}, f32[4]{0:T(128)S(1)}, u32[]{:S(2)}) copy-start(f32[4]{0:T(128)S(1)} %get-tuple-element.10) | copy-start | bytes 52
  14.9 34.9 %copy-start.71 = (s32[256]{0:T(256)S(1)}, s32[256]{0:T(256)}, u32[]{:S(2)}) copy-start(s32[256]{0:T(256)} %param.20) | copy-start | bytes 3076
  15.2 4.6 %copy-start.28 = (f32[4,64,64]{2,1,0:T(8,128)}, f32[4,64,64]{2,1,0:T(8,128)S(1)}, u32[]{:S(2)}) copy-start(f32[4,64,64]{2,1,0:T(8,128)S(1)} %fusion.18) | copy-start | bytes 196612
  15.4 4.3 %copy-start.30 = (f32[4,64,64]{2,1,0:T(8,128)}, f32[4,64,64]{2,1,0:T(8,128)S(1)}, u32[]{:S(2)}) copy-start(f32[4,64,64]{2,1,0:T(8,128)S(1)} %fusion.17) | copy-start | bytes 196612
  15.4 35.2 %copy-start.34 = (s32[256,256]{1,0:T(8,128)S(1)}, s32[256,256]{1,0:T(8,128)}, u32[]{:S(2)}) copy-start(s32[256,256]{1,0:T(8,128)} %param.18) | copy-start | bytes 786436
  15.7 4.0 %copy-start.32 = (f32[4,64,64]{2,1,0:T(8,128)}, f32[4,64,64]{2,1,0:T(8,128)S(1)}, u32[]{:S(2)}) copy-start(f32[4,64,64]{2,1,0:T(8,128)S(1)} %fusion.16) | copy-start | bytes 196612
  17.0 35.4 %copy-start.15 = (f32[4,64,64]{2,1,0:T(8,128)}, f32[4,64,64]{2,1,0:T(8,128)S(1)}, u32[]{:S(2)}) copy-start(f32[4,64,64]{2,1,0:T(8,128)S(1)} %convolution_add_fusion.11) | copy-start | bytes 196612
  50.6 4.9 %copy-start.35 = (s32[64,256]{1,0:T(8,128)}, s32[64,256]{1,0:T(8,128)S(1)}, u32[]{:S(2)}) copy-start(s32[64,256]{1,0:T(8,128)S(1)} %broadcast_select_fusion) | copy-start | bytes 196612
  55.9 3.6 %copy-start.48 = (f32[32,256]{1,0:T(8,128)}, f32[32,256]{1,0:T(8,128)S(1)}, u32[]{:S(2)}) copy-start(f32[32,256]{1,0:T(8,128)S(1)} %fusion.95) | copy-start | bytes 98308
  58.2 13.5 %copy-start.55 = (f32[64]{0:T(128)S(1)}, f32[64]{0:T(128)}, u32[]{:S(2)}) copy-start(f32[64]{0:T(128)} %copy-done.54) | copy-start | bytes 772
  58.3 14.2 %copy-start.52 = (f32[8,256]{1,0:T(8,128)}, f32[8,256]{1,0:T(8,128)S(1)}, u32[]{:S(2)}) copy-start(f32[8,256]{1,0:T(8,128)S(1)} %fusion.93) | copy-start | bytes 24580
  72.5 10.3 %copy-start.6 = (f32[8,64,256]{2,1,0:T(8,128)S(1)}, f32[8,64,256]{2,1,0:T(8,128)}, u32[]{:S(2)}) copy-start(f32[8,64,256]{2,1,0:T(8,128)} %copy-done.5) | copy-start | bytes 1572868
  72.5 10.4 %copy-start.2 = (f32[128,64,64]{2,1,0:T(8,128)S(1)}, f32[128,64,64]{2,1,0:T(8,128)}, u32[]{:S(2)}) copy-start(f32[128,64,64]{2,1,0:T(8,128)} %shard_map.174) | copy-start | bytes 6291460
  93.2 3.5 %copy-start.49 = (f32[32,256]{1,0:T(8,128)S(1)}, f32[32,256]{1,0:T(8,128)}, u32[]{:S(2)}) copy-start(f32[32,256]{1,0:T(8,128)} %copy-done.48) | copy-start | bytes 98308
  99.1 2.7 %copy-start.18 = (f32[4,64,256]{2,1,0:T(8,128)S(1)}, f32[4,64,256]{2,1,0:T(8,128)}, u32[]{:S(2)}) copy-start(f32[4,64,256]{2,1,0:T(8,128)} %copy-done.17) | copy-start | bytes 786436
  99.2 2.8 %copy-start.58 = (f32[4,256]{1,0:T(4,128)S(1)}, f32[4,256]{1,0:T(4,128)}, u32[]{:S(2)}) copy-start(f32[4,256]{1,0:T(4,128)} %copy-done.57) | copy-start | bytes 12292
  99.2 3.7 %copy-start.60 = (f32[2,256]{1,0:T(2,128)S(1)}, f32[2,256]{1,0:T(2,128)}, u32[]{:S(2)}) copy-start(f32[2,256]{1,0:T(2,128)} %copy-done.59) | copy-start | bytes 6148
  100.6 3.1 %copy-start.40 = (f32[2,64,256]{2,1,0:T(8,128)S(1)}, f32[2,64,256]{2,1,0:T(8,128)}, u32[]{:S(2)}) copy-start(f32[2,64,256]{2,1,0:T(8,128)} %copy-done.39) | copy-start | bytes 393220
  100.6 3.1 %copy-start.66 = (f32[256]{0:T(256)S(1)}, f32[256]{0:T(256)}, u32[]{:S(2)}) copy-start(f32[256]{0:T(256)} %copy-done.65) | copy-start | bytes 3076
  100.8 32.5 %copy-start.14 = (f32[4,64,64]{2,1,0:T(8,128)S(1)}, f32[4,64,64]{2,1,0:T(8,128)}, u32[]{:S(2)}) copy-start(f32[4,64,64]{2,1,0:T(8,128)} %copy-done.13) | copy-start | bytes 196612
  101.9 33.9 %copy-start.12 = (f32[4,64,64]{2,1,0:T(8,128)S(1)}, f32[4,64,64]{2,1,0:T(8,128)}, u32[]{:S(2)}) copy-start(f32[4,64,64]{2,1,0:T(8,128)} %copy-done.11) | copy-start | bytes 196612
  101.9 34.4 %copy-start.10 = (f32[4,64,64]{2,1,0:T(8,128)S(1)}, f32[4,64,64]{2,1,0:T(8,128)}, u32[]{:S(2)}) copy-start(f32[4,64,64]{2,1,0:T(8,128)} %copy-done.9) | copy-start | bytes 196612
  102.9 34.1 %copy-start.16 = (f32[4,64,64]{2,1,0:T(8,128)S(1)}, f32[4,64,64]{2,1,0:T(8,128)}, u32[]{:S(2)}) copy-start(f32[4,64,64]{2,1,0:T(8,128)} %copy-done.15) | copy-start | bytes 196612
  103.7 33.8 %copy-start.47 = (f32[4]{0:T(128)S(1)}, f32[4]{0:T(128)}, u32[]{:S(2)}) copy-start(f32[4]{0:T(128)} %copy-done.46) | copy-start | bytes 52
  133.3 6.8 %copy-start.21 = (f32[4,64,64]{2,1,0:T(8,128)S(1)}, f32[4,64,64]{2,1,0:T(8,128)}, u32[]{:S(2)}) copy-start(f32[4,64,64]{2,1,0:T(8,128)} %copy-done.20) | copy-start | bytes 196612
  133.3 7.1 %copy-start.33 = (f32[4,64,64]{2,1,0:T(8,128)S(1)}, f32[4,64,64]{2,1,0:T(8,128)}, u32[]{:S(2)}) copy-start(f32[4,64,64]{2,1,0:T(8,128)} %copy-done.32) | copy-start | bytes 196612
  133.3 7.3 %copy-start.31 = (f32[4,64,64]{2,1,0:T(8,128)S(1)}, f32[4,64,64]{2,1,0:T(8,128)}, u32[]{:S(2)}) copy-start(f32[4,64,64]{2,1,0:T(8,128)} %copy-done.30) | copy-start | bytes 196612
  133.3 7.6 %copy-start.29 = (f32[4,64,64]{2,1,0:T(8,128)S(1)}, f32[4,64,64]{2,1,0:T(8,128)}, u32[]{:S(2)}) copy-start(f32[4,64,64]{2,1,0:T(8,128)} %copy-done.28) | copy-start | bytes 196612
  133.3 7.8 %copy-start.27 = (f32[4,64,64]{2,1,0:T(8,128)S(1)}, f32[4,64,64]{2,1,0:T(8,128)}, u32[]{:S(2)}) copy-start(f32[4,64,64]{2,1,0:T(8,128)} %copy-done.26) | copy-start | bytes 196612
  134.6 6.8 %copy-start.25 = (f32[4,64,64]{2,1,0:T(8,128)S(1)}, f32[4,64,64]{2,1,0:T(8,128)}, u32[]{:S(2)}) copy-start(f32[4,64,64]{2,1,0:T(8,128)} %copy-done.24) | copy-start | bytes 196612
  135.8 5.8 %copy-start.23 = (f32[4,64,64]{2,1,0:T(8,128)S(1)}, f32[4,64,64]{2,1,0:T(8,128)}, u32[]{:S(2)}) copy-start(f32[4,64,64]{2,1,0:T(8,128)} %copy-done.22) | copy-start | bytes 196612
  136.4 5.5 %copy-start.8 = (f32[64,64]{1,0:T(8,128)S(1)}, f32[64,64]{1,0:T(8,128)}, u32[]{:S(2)}) copy-start(f32[64,64]{1,0:T(8,128)} %copy-done.7) | copy-start | bytes 49156
  136.4 5.5 %copy-start.70 = (f32[4]{0:T(128)S(1)}, f32[4]{0:T(128)}, u32[]{:S(2)}) copy-start(f32[4]{0:T(128)} %get-tuple-element.9) | copy-start | bytes 52
  136.7 5.6 %copy-start.64 = (f32[8]{0:T(128)S(1)}, f32[8]{0:T(128)}, u32[]{:S(2)}) copy-start(f32[8]{0:T(128)} %copy-done.63) | copy-start | bytes 100
  136.7 5.6 %copy-start.69 = (s32[128]{0:T(128)S(1)}, s32[128]{0:T(128)}, u32[]{:S(2)}) copy-start(s32[128]{0:T(128)} %copy-done.68) | copy-start | bytes 1540
  136.7 5.7 %copy-start.38 = (f32[64,64]{1,0:T(8,128)S(1)}, f32[64,64]{1,0:T(8,128)}, u32[]{:S(2)}) copy-start(f32[64,64]{1,0:T(8,128)} %copy-done.37) | copy-start | bytes 49156
  136.7 5.7 %copy-start.42 = (f32[8,64]{0,1:T(8,128)S(1)}, f32[8,64]{0,1:T(8,128)}, u32[]{:S(2)}) copy-start(f32[8,64]{0,1:T(8,128)} %copy-done.41) | copy-start | bytes 6148
  136.7 5.7 %copy-start.43 = (f32[64,64]{1,0:T(8,128)S(1)}, f32[64,64]{1,0:T(8,128)}, u32[]{:S(2)}) copy-start(f32[64,64]{1,0:T(8,128)} %constant.111) | copy-start | bytes 49156
  136.7 5.7 %copy-start.44 = (f32[64,64]{1,0:T(8,128)S(1)}, f32[64,64]{1,0:T(8,128)}, u32[]{:S(2)}) copy-start(f32[64,64]{1,0:T(8,128)} %constant.112) | copy-start | bytes 49156
  136.7 5.7 %copy-start.62 = (f32[8]{0:T(128)S(1)}, f32[8]{0:T(128)}, u32[]{:S(2)}) copy-start(f32[8]{0:T(128)} %copy-done.61) | copy-start | bytes 100
  137.9 5.1 %copy-start.56 = (f32[64]{0:T(128)S(1)}, f32[64]{0:T(128)}, u32[]{:S(2)}) copy-start(f32[64]{0:T(128)} %copy-done.54) | copy-start | bytes 772
  (25 other events, 32.8 us)

commit v10 on v9

--- a/solution.py
+++ b/solution.py
@@ -82,7 +82,8 @@
         offset = 2 * LEAF_DEV - 2 * amount
         message = forward(probs[offset : offset + amount], current)
         messages.append(message)
-        raw_parent = message[0::2] * message[1::2]
+        halves = message.reshape((amount // 2, 2) + message.shape[1:])
+        raw_parent = halves[:, 0] * halves[:, 1]
         scaling = jnp.sum(raw_parent, axis=1)
         current = raw_parent / scaling[:, None, :]
         logscale = logscale + jnp.sum(jnp.log(scaling), axis=0)

time: 170 us -> 171 us (level)
  no operation moved by 1% of the time
where the time goes in v10:
time: 171 us; the launch traced here: 170 us
  Pallas kernels  74.3 us (43%)
  matrix products  35.1 us (21%)
  other arithmetic  24.5 us (14%)
  local copies, waits for them, and re-layouts  21.1 us (12%)
  blocking collectives  10.3 us (6%)
  between operations  4.59 us (3%)
    pallas_call x1, Pallas kernels, pair_gather(): pl.pallas_call(pair_gather_kernel, out_shape=jax.ShapeDtypeStruct((n * pe...  29.1 us
    pallas_call x1, Pallas kernels, pair_scatter(): pl.pallas_call(pair_scatter_kernel, out_shape=jax.ShapeDtypeStruct((per,)...  28.2 us
    pallas_call x1, Pallas kernels, allreduce_all(): pl.pallas_call(functools.partial(allreduce_kernel, n_site, n_branch), out...  17 us
    dot_general x35, matrix products, product(): return jnp.einsum('bij,bjk->bik', left, right, precision=lax.Precision.HIGH)  11.3 us
    dot_general x7, matrix products, body(): jnp.einsum('bis,bjs->bij', vector, partial_value, precision=lax.Precision...  10.8 us
    all_gather x1, blocking collectives, body(): top_all = lax.all_gather(top_pack, 'branch', axis=0, tiled=False)  10.3 us
    unnamed x148, local copies, waits for them, and re-layouts  10.1 us
    dot_general x6, matrix products, carried(): jnp.einsum('bji,bjs->bis', probs, vectors, precision=lax.Precision.HIGH)  5.47 us

profile of v10, /device:TPU:1, one launch (start us, length us, event | category | flops | bytes accessed | tf_op | source)
XLA Modules:
  0.0 169.9 jit_solution(8327510745233871445)
XLA Ops:
  0.6 1.3 fusion.112
  2.6 0.8 copy.111
  3.5 0.8 fusion.84
  4.9 1.0 fusion.43
  6.1 0.7 pad_add_fusion
  6.8 2.2 %fusion.41 = f32[128,64,64]{0,2,1:T(8,128)S(1)} fusion(f32[8]{0:T(128)S(1)} %multiply_reduce_fusion.10, f32[64,64]{1,0:T(8,128)S(1)} %fusion.86, f32[8,64]{0,1:T(8,128)S(1)} %fusion.43, f32[64,64]{1,0:T(8,128)} %constant.112, f32[8]{0:T(128)S(1)} %broadcast_add_fusion, f32[64,64]{1,0:T(8,128)} %constant.111, f32[64,64]{1,0:T(8,128)S(1)} %fusion.84, ...), kind=kOutput, calls=%fused_computation.107 | convolution fusion | flops 25396224 | bytes 2165312 | tf_op jit(solution)/shard_map/bc,cij->bij/dot_general | solution.py:550
  9.1 2.0 %constant_dynamic-slice_fusion.1 = f32[4,64,64]{0,2,1:T(8,128)} fusion(f32[128,64,64]{0,2,1:T(8,128)S(1)} %fusion.41, s32[]{:T(128)S(6)} %select_n.31), kind=kLoop, calls=%fused_computation.211 | loop fusion | bytes 131076 | tf_op jit(solution)/shard_map/dynamic_slice | solution.py:554
  11.1 2.3 %copy.172 = f32[4,64,64]{2,1,0:T(8,128)S(1)} copy(f32[4,64,64]{0,2,1:T(8,128)} %constant_dynamic-slice_fusion.1) | data formatting | bytes 131072
  20.5 0.8 reshape.407.x_ref
  21.3 29.1 %shard_map.174 = f32[128,64,64]{2,1,0:T(8,128)} custom-call(f32[64,256]{1,0:T(8,128)} %reshape.407.x_ref), custom_call_target="tpu_custom_call" | custom-call | tf_op jit(solution)/shard_map/pallas_call | solution.py:519
  52.0 0.9 convert_select_fusion.7
  53.0 1.2 copy-done.1
  54.1 2.0 %fusion.2 = f32[64,64,256]{2,1,0:T(8,128)S(1)} fusion(f32[128,64,64]{2,1,0:T(8,128)S(1)} %copy-done.1, f32[64,64,256]{2,1,0:T(8,128)S(1)} %convert_select_fusion.7), kind=kOutput, calls=%fused_computation.8 | convolution fusion | flops 402653184 | bytes 10485760 | tf_op jit(solution)/shard_map/bij,bjs->bis/dot_general | solution.py:62
  56.6 1.1 fusion.29
  61.3 10.3 %all-gather.1 = f32[4,65,256]{2,1,0:T(8,128)S(1)} all-gather(f32[1,65,256]{2,1,0:T(8,128)S(1)} %maximum_bitcast_fusion), channel_id=2, replica_groups=mesh['site'=32,'branch'=4] {'branch'}, dimensions={0}, use_global_device_ids=true | all-gather | bytes 332800 | tf_op jit(solution)/shard_map/all_gather | solution.py:565
  71.6 0.7 copy-done.19
  72.4 0.8 multiply_multiply_fusion.3
  73.2 1.1 fusion.66
  74.2 1.4 fusion.64
  75.7 0.8 slice_reduce_fusion
  76.5 1.3 multiply_reduce_fusion.11
  77.8 1.0 fusion.113
  78.8 1.0 multiply_reduce_fusion.9
  79.8 1.1 fusion.122
  81.0 1.0 reverse_multiply_fusion.4
  82.0 1.2 fusion.123
  85.4 1.0 fusion.34
  87.3 1.1 fusion.126
  88.4 1.9 %fusion.28 = f32[32,64,256]{2,1,0:T(8,128)S(1)} fusion(f32[32,64,256]{2,1,0:T(8,128)S(1)} %fusion.126), kind=kOutput, calls=%fused_computation.74 | output fusion | flops 532543 | bytes 4194304 | tf_op jit(solution)/shard_map/div | solution.py:118
  90.6 0.9 reverse_multiply_fusion
  91.5 1.4 fusion
  93.0 0.9 bitcast_multiply_fusion
  93.9 3.5 %fusion.12 = f32[128,64,64]{2,1,0:T(8,128)} fusion(f32[64,64,256]{2,1,0:T(8,128)S(1)} %bitcast_multiply_fusion, s32[64,256]{1,0:T(8,128)S(1)} %copy-done.36, pred[64,256]{1,0:T(8,128)(4,1)S(1)} %select_compare_fusion), kind=kOutput, calls=%fused_computation.24 | convolution fusion | flops 405798912 | bytes 6373376 | tf_op jit(solution)/shard_map/bis,bjs->bij/dot_general | solution.py:574
  97.4 2.2 %fusion.13 = f32[128,64,64]{2,1,0:T(8,128)} fusion(f32[128,64,64]{2,1,0:T(8,128)} %fusion.12, f32[32,64,256]{2,1,0:T(8,128)S(1)} %bitcast.321, f32[32,256]{1,0:T(8,128)S(1)} %multiply_divide_fusion.1, f32[32,256]{1,0:T(8,128)S(1)} %copy-done.49, f32[32,2,64,256]{3,2,1,0:T(8,128)S(1)} %bitcast.315), kind=kOutput, calls=%fused_computation.25 | convolution fusion | flops 202899456 | bytes 7405568 | tf_op jit(solution)/shard_map/bis,bjs->bij/dot_general | solution.py:574
  99.8 1.5 convolution_dynamic-update-slice_fusion
  101.4 1.1 convolution_dynamic-update-slice_fusion.1
  102.6 0.9 convolution_dynamic-update-slice_fusion.2
  103.5 0.8 convolution_dynamic-update-slice_fusion.3
  104.4 0.8 fusion.23
  105.8 28.2 %shard_map.175 = f32[4,64,64]{2,1,0:T(8,128)} custom-call(f32[128,64,64]{2,1,0:T(8,128)} %constant_dynamic-update-slice_fusion.x_ref), custom_call_target="tpu_custom_call" | custom-call | tf_op jit(solution)/shard_map/pallas_call | solution.py:390
  134.0 1.3 fusion.117
  135.3 1.2 convolution_add_fusion.10
  145.9 17.0 %shard_map.176 = f32[40,128]{1,0:T(8,128)} custom-call(f32[40,128]{1,0:T(8,128)} %pad_bitcast_fusion.x_ref), custom_call_target="tpu_custom_call" | custom-call | tf_op jit(solution)/shard_map/pallas_call | solution.py:193
  163.0 0.7 slice.138
  163.7 0.7 reshape.425
  164.4 0.7 slice_bitcast_fusion.10
  165.7 1.3 slice.167
  167.6 1.2 slice.165
  (245 shorter events, 27.1 us)
Async XLA Ops:
  0.6 49.9 %copy-start = (s32[256,256]{1,0:T(8,128)S(1)}, s32[256,256]{1,0:T(8,128)}, u32[]{:S(2)}) copy-start(s32[256,256]{1,0:T(8,128)} %param.17) | copy-start | bytes 786436
  2.6 6.4 %copy-start.54 = (f32[64]{0:T(128)}, f32[64]{0:T(128)S(1)}, u32[]{:S(2)}) copy-start(f32[64]{0:T(128)S(1)} %get-tuple-element.16) | copy-start | bytes 772
  4.2 4.8 %copy-start.37 = (f32[64,64]{1,0:T(8,128)}, f32[64,64]{1,0:T(8,128)S(1)}, u32[]{:S(2)}) copy-start(f32[64,64]{1,0:T(8,128)S(1)} %fusion.84) | copy-start | bytes 49156
  4.9 4.2 %copy-start.61 = (f32[8]{0:T(128)}, f32[8]{0:T(128)S(1)}, u32[]{:S(2)}) copy-start(f32[8]{0:T(128)S(1)} %broadcast_add_fusion) | copy-start | bytes 100
  5.9 3.2 %copy-start.41 = (f32[8,64]{0,1:T(8,128)}, f32[8,64]{0,1:T(8,128)S(1)}, u32[]{:S(2)}) copy-start(f32[8,64]{0,1:T(8,128)S(1)} %fusion.43) | copy-start | bytes 6148
  6.0 3.1 %copy-start.63 = (f32[8]{0:T(128)}, f32[8]{0:T(128)S(1)}, u32[]{:S(2)}) copy-start(f32[8]{0:T(128)S(1)} %multiply_reduce_fusion.10) | copy-start | bytes 100
  6.0 10.0 %copy-start.7 = (f32[64,64]{1,0:T(8,128)}, f32[64,64]{1,0:T(8,128)S(1)}, u32[]{:S(2)}) copy-start(f32[64,64]{1,0:T(8,128)S(1)} %fusion.86) | copy-start | bytes 49156
  6.8 6.6 %copy-start.72 = (f32[127]{0:T(128)S(1)}, f32[127]{0:T(128)}, u32[]{:S(2)}) copy-start(f32[127]{0:T(128)} %param.24) | copy-start | bytes 1528
  14.0 6.3 %copy-start.46 = (f32[4]{0:T(128)}, f32[4]{0:T(128)S(1)}, u32[]{:S(2)}) copy-start(f32[4]{0:T(128)S(1)} %get-tuple-element.10) | copy-start | bytes 52
  14.9 5.5 %copy-start.26 = (f32[4,64,64]{2,1,0:T(8,128)}, f32[4,64,64]{2,1,0:T(8,128)S(1)}, u32[]{:S(2)}) copy-start(f32[4,64,64]{2,1,0:T(8,128)S(1)} %fusion.20) | copy-start | bytes 196612
  14.9 35.5 %copy-start.71 = (s32[256]{0:T(256)S(1)}, s32[256]{0:T(256)}, u32[]{:S(2)}) copy-start(s32[256]{0:T(256)} %param.20) | copy-start | bytes 3076
  15.2 5.2 %copy-start.28 = (f32[4,64,64]{2,1,0:T(8,128)}, f32[4,64,64]{2,1,0:T(8,128)S(1)}, u32[]{:S(2)}) copy-start(f32[4,64,64]{2,1,0:T(8,128)S(1)} %fusion.19) | copy-start | bytes 196612
  15.4 5.0 %copy-start.30 = (f32[4,64,64]{2,1,0:T(8,128)}, f32[4,64,64]{2,1,0:T(8,128)S(1)}, u32[]{:S(2)}) copy-start(f32[4,64,64]{2,1,0:T(8,128)S(1)} %fusion.18) | copy-start | bytes 196612
  15.5 35.8 %copy-start.34 = (s32[256,256]{1,0:T(8,128)S(1)}, s32[256,256]{1,0:T(8,128)}, u32[]{:S(2)}) copy-start(s32[256,256]{1,0:T(8,128)} %param.18) | copy-start | bytes 786436
  15.7 4.7 %copy-start.32 = (f32[4,64,64]{2,1,0:T(8,128)}, f32[4,64,64]{2,1,0:T(8,128)S(1)}, u32[]{:S(2)}) copy-start(f32[4,64,64]{2,1,0:T(8,128)S(1)} %fusion.17) | copy-start | bytes 196612
  51.3 4.9 %copy-start.35 = (s32[64,256]{1,0:T(8,128)}, s32[64,256]{1,0:T(8,128)S(1)}, u32[]{:S(2)}) copy-start(s32[64,256]{1,0:T(8,128)S(1)} %broadcast_select_fusion) | copy-start | bytes 196612
  56.6 3.6 %copy-start.48 = (f32[32,256]{1,0:T(8,128)}, f32[32,256]{1,0:T(8,128)S(1)}, u32[]{:S(2)}) copy-start(f32[32,256]{1,0:T(8,128)S(1)} %fusion.109) | copy-start | bytes 98308
  58.9 13.5 %copy-start.55 = (f32[64]{0:T(128)S(1)}, f32[64]{0:T(128)}, u32[]{:S(2)}) copy-start(f32[64]{0:T(128)} %copy-done.54) | copy-start | bytes 772
  59.0 14.2 %copy-start.52 = (f32[8,256]{1,0:T(8,128)}, f32[8,256]{1,0:T(8,128)S(1)}, u32[]{:S(2)}) copy-start(f32[8,256]{1,0:T(8,128)S(1)} %fusion.103) | copy-start | bytes 24580
  73.2 10.3 %copy-start.6 = (f32[8,64,256]{2,1,0:T(8,128)S(1)}, f32[8,64,256]{2,1,0:T(8,128)}, u32[]{:S(2)}) copy-start(f32[8,64,256]{2,1,0:T(8,128)} %copy-done.5) | copy-start | bytes 1572868
  73.2 10.4 %copy-start.2 = (f32[128,64,64]{2,1,0:T(8,128)S(1)}, f32[128,64,64]{2,1,0:T(8,128)}, u32[]{:S(2)}) copy-start(f32[128,64,64]{2,1,0:T(8,128)} %shard_map.174) | copy-start | bytes 6291460
  93.9 3.5 %copy-start.49 = (f32[32,256]{1,0:T(8,128)S(1)}, f32[32,256]{1,0:T(8,128)}, u32[]{:S(2)}) copy-start(f32[32,256]{1,0:T(8,128)} %copy-done.48) | copy-start | bytes 98308
  99.8 2.8 %copy-start.58 = (f32[4,256]{1,0:T(4,128)S(1)}, f32[4,256]{1,0:T(4,128)}, u32[]{:S(2)}) copy-start(f32[4,256]{1,0:T(4,128)} %copy-done.57) | copy-start | bytes 12292
  99.8 3.7 %copy-start.60 = (f32[2,256]{1,0:T(2,128)S(1)}, f32[2,256]{1,0:T(2,128)}, u32[]{:S(2)}) copy-start(f32[2,256]{1,0:T(2,128)} %copy-done.59) | copy-start | bytes 6148
  101.3 3.1 %copy-start.40 = (f32[2,64,256]{2,1,0:T(8,128)S(1)}, f32[2,64,256]{2,1,0:T(8,128)}, u32[]{:S(2)}) copy-start(f32[2,64,256]{2,1,0:T(8,128)} %copy-done.39) | copy-start | bytes 393220
  101.3 3.1 %copy-start.66 = (f32[256]{0:T(256)S(1)}, f32[256]{0:T(256)}, u32[]{:S(2)}) copy-start(f32[256]{0:T(256)} %copy-done.65) | copy-start | bytes 3076
  101.4 32.5 %copy-start.14 = (f32[4,64,64]{2,1,0:T(8,128)S(1)}, f32[4,64,64]{2,1,0:T(8,128)}, u32[]{:S(2)}) copy-start(f32[4,64,64]{2,1,0:T(8,128)} %copy-done.13) | copy-start | bytes 196612
  102.5 33.9 %copy-start.12 = (f32[4,64,64]{2,1,0:T(8,128)S(1)}, f32[4,64,64]{2,1,0:T(8,128)}, u32[]{:S(2)}) copy-start(f32[4,64,64]{2,1,0:T(8,128)} %copy-done.11) | copy-start | bytes 196612
  102.6 34.4 %copy-start.10 = (f32[4,64,64]{2,1,0:T(8,128)S(1)}, f32[4,64,64]{2,1,0:T(8,128)}, u32[]{:S(2)}) copy-start(f32[4,64,64]{2,1,0:T(8,128)} %copy-done.9) | copy-start | bytes 196612
  103.5 34.2 %copy-start.16 = (f32[4,64,64]{2,1,0:T(8,128)S(1)}, f32[4,64,64]{2,1,0:T(8,128)}, u32[]{:S(2)}) copy-start(f32[4,64,64]{2,1,0:T(8,128)} %copy-done.15) | copy-start | bytes 196612
  104.4 33.8 %copy-start.47 = (f32[4]{0:T(128)S(1)}, f32[4]{0:T(128)}, u32[]{:S(2)}) copy-start(f32[4]{0:T(128)} %copy-done.46) | copy-start | bytes 52
  133.9 6.8 %copy-start.21 = (f32[4,64,64]{2,1,0:T(8,128)S(1)}, f32[4,64,64]{2,1,0:T(8,128)}, u32[]{:S(2)}) copy-start(f32[4,64,64]{2,1,0:T(8,128)} %copy-done.20) | copy-start | bytes 196612
  134.0 7.1 %copy-start.33 = (f32[4,64,64]{2,1,0:T(8,128)S(1)}, f32[4,64,64]{2,1,0:T(8,128)}, u32[]{:S(2)}) copy-start(f32[4,64,64]{2,1,0:T(8,128)} %copy-done.32) | copy-start | bytes 196612
  134.0 7.3 %copy-start.31 = (f32[4,64,64]{2,1,0:T(8,128)S(1)}, f32[4,64,64]{2,1,0:T(8,128)}, u32[]{:S(2)}) copy-start(f32[4,64,64]{2,1,0:T(8,128)} %copy-done.30) | copy-start | bytes 196612
  134.0 7.6 %copy-start.29 = (f32[4,64,64]{2,1,0:T(8,128)S(1)}, f32[4,64,64]{2,1,0:T(8,128)}, u32[]{:S(2)}) copy-start(f32[4,64,64]{2,1,0:T(8,128)} %copy-done.28) | copy-start | bytes 196612
  134.0 7.8 %copy-start.27 = (f32[4,64,64]{2,1,0:T(8,128)S(1)}, f32[4,64,64]{2,1,0:T(8,128)}, u32[]{:S(2)}) copy-start(f32[4,64,64]{2,1,0:T(8,128)} %copy-done.26) | copy-start | bytes 196612
  135.3 6.8 %copy-start.25 = (f32[4,64,64]{2,1,0:T(8,128)S(1)}, f32[4,64,64]{2,1,0:T(8,128)}, u32[]{:S(2)}) copy-start(f32[4,64,64]{2,1,0:T(8,128)} %copy-done.24) | copy-start | bytes 196612
  136.5 5.8 %copy-start.23 = (f32[4,64,64]{2,1,0:T(8,128)S(1)}, f32[4,64,64]{2,1,0:T(8,128)}, u32[]{:S(2)}) copy-start(f32[4,64,64]{2,1,0:T(8,128)} %copy-done.22) | copy-start | bytes 196612
  137.0 5.5 %copy-start.8 = (f32[64,64]{1,0:T(8,128)S(1)}, f32[64,64]{1,0:T(8,128)}, u32[]{:S(2)}) copy-start(f32[64,64]{1,0:T(8,128)} %copy-done.7) | copy-start | bytes 49156
  137.0 5.5 %copy-start.70 = (f32[4]{0:T(128)S(1)}, f32[4]{0:T(128)}, u32[]{:S(2)}) copy-start(f32[4]{0:T(128)} %get-tuple-element.9) | copy-start | bytes 52
  137.3 5.6 %copy-start.64 = (f32[8]{0:T(128)S(1)}, f32[8]{0:T(128)}, u32[]{:S(2)}) copy-start(f32[8]{0:T(128)} %copy-done.63) | copy-start | bytes 100
  137.3 5.6 %copy-start.69 = (s32[128]{0:T(128)S(1)}, s32[128]{0:T(128)}, u32[]{:S(2)}) copy-start(s32[128]{0:T(128)} %copy-done.68) | copy-start | bytes 1540
  137.4 5.7 %copy-start.38 = (f32[64,64]{1,0:T(8,128)S(1)}, f32[64,64]{1,0:T(8,128)}, u32[]{:S(2)}) copy-start(f32[64,64]{1,0:T(8,128)} %copy-done.37) | copy-start | bytes 49156
  137.4 5.7 %copy-start.42 = (f32[8,64]{0,1:T(8,128)S(1)}, f32[8,64]{0,1:T(8,128)}, u32[]{:S(2)}) copy-start(f32[8,64]{0,1:T(8,128)} %copy-done.41) | copy-start | bytes 6148
  137.4 5.7 %copy-start.43 = (f32[64,64]{1,0:T(8,128)S(1)}, f32[64,64]{1,0:T(8,128)}, u32[]{:S(2)}) copy-start(f32[64,64]{1,0:T(8,128)} %constant.111) | copy-start | bytes 49156
  137.4 5.7 %copy-start.44 = (f32[64,64]{1,0:T(8,128)S(1)}, f32[64,64]{1,0:T(8,128)}, u32[]{:S(2)}) copy-start(f32[64,64]{1,0:T(8,128)} %constant.112) | copy-start | bytes 49156
  137.4 5.7 %copy-start.62 = (f32[8]{0:T(128)S(1)}, f32[8]{0:T(128)}, u32[]{:S(2)}) copy-start(f32[8]{0:T(128)} %copy-done.61) | copy-start | bytes 100
  138.6 5.1 %copy-start.56 = (f32[64]{0:T(128)S(1)}, f32[64]{0:T(128)}, u32[]{:S(2)}) copy-start(f32[64]{0:T(128)} %copy-done.54) | copy-start | bytes 772
  (25 other events, 31.6 us)
